TPU v7x, 32 devices: a whole 2x2x4 slice. The times are simulated.
32 devices in a mesh: dp: 8 (over z, x), tensor: 4 (over y, core).
Axes of the slice: x: 2, y: 2, z: 4, core: 2. Of those that a mesh axis runs over, the one named last changes fastest.
Arguments:
- tokens: bfloat16 [32768, 1024], P('dp', 'tensor'), may hold values from -6 to 6
- lengths: int32 [16], P('dp'), may hold values from 512 to 2048, as said below
- grad_out: bfloat16 [32768, 1024], P('dp', 'tensor'), may hold values from -6 to 6
- norm_gain: bfloat16 [1024], P('dp'), may hold values from 0.099609375 to 1.8984375
- w_gate: bfloat16 [1024, 2048], P('dp', 'tensor'), may hold values from -0.1875 to 0.1875
- w_value: bfloat16 [1024, 2048], P('dp', 'tensor'), may hold values from -0.1875 to 0.1875
- w_bc: bfloat16 [1024, 256], P('dp'), may hold values from -0.1875 to 0.1875
- w_dt: bfloat16 [1024, 32], P('dp', 'tensor'), may hold values from -0.1875 to 0.1875
- conv_x: float32 [5, 2048], P(None, 'tensor'), may hold values from -3 to 3
- conv_bc: float32 [5, 256], replicated, may hold values from -3 to 3
- dt_bias: float32 [32], P('tensor'), may hold values from -7 to -2.5
- a_log: float32 [32], P('tensor'), may hold values from 0 to 2.77
- skip_d: float32 [32], P('tensor'), may hold values from 0.35 to 2.75
- gate_gain: float32 [2048], P('tensor'), may hold values from 0.1 to 1.9
- w_out: bfloat16 [1024, 2048], P('dp', 'tensor'), may hold values from -0.125 to 0.125
Outputs:
- out: bfloat16 [32768, 1024], P('dp', 'tensor')
- grad_tokens: float32 [32768, 1024], P('dp', 'tensor')
- grad_norm_gain: float32 [1024], P(('dp', 'tensor'))
- grad_w_gate: float32 [1024, 2048], P('dp', 'tensor')
- grad_w_value: float32 [1024, 2048], P('dp', 'tensor')
- grad_w_bc: float32 [1024, 256], P(('dp', 'tensor'))
- grad_w_dt: float32 [1024, 32], P('dp', 'tensor')
- grad_conv_x: float32 [5, 2048], P(None, 'tensor')
- grad_conv_bc: float32 [5, 256], replicated
- grad_dt_bias: float32 [32], P('tensor')
- grad_a_log: float32 [32], P('tensor')
- grad_skip_d: float32 [32], P('tensor')
- grad_gate_gain: float32 [2048], P('tensor')
- grad_w_out: float32 [1024, 2048], P('dp', 'tensor')
Inputs may be any that keep to these rules, and one draw needn't show every extreme that they name: Sequence i occupies the first lengths[i] of its 2048 slots; the rest is padding. Sequence 0 is full.
All inputs are finite; a program needn't handle non-finite values.
Results may differ from a plain program's by a relative error of at most 0.0085.
Values may be sent and summed in bfloat16 or wider, within the bound.
No kernel may reach another device: no remote copies, remote signals or barrier semaphores. Data moves between devices by JAX's collectives and lax.ppermute only.
A program may use at most 192 MiB of HBM per device.

v0:
```python
import functools

import jax
import jax.numpy as jnp
from jax import lax
from jax.experimental import pallas as pl
from jax.experimental.pallas import tpu as pltpu
from jax.sharding import PartitionSpec as P


SEQ_LEN = 2048
Q = 256
HALF = 128
F32 = jnp.float32
BF16 = jnp.bfloat16
epsilon = 1e-05
NEG = -1e30


def nn(a, b):
    return lax.dot_general(a, b, (((1,), (0,)), ((), ())), preferred_element_type=F32)


def nt(a, b):
    return lax.dot_general(a, b, (((1,), (1,)), ((), ())), preferred_element_type=F32)


def split3(a):
    high = a.astype(BF16)
    rest = a - high.astype(F32)
    mid = rest.astype(BF16)
    low = (rest - mid.astype(F32)).astype(BF16)
    return high, mid, low


def times_ones(a, ones):
    rows = a.shape[0]
    got = nn(jnp.concatenate(split3(a), 0), ones)
    return got[:rows] + got[rows : 2 * rows] + got[2 * rows :]


def twice(a):
    return jnp.concatenate([a, a], 1)


def fold(a):
    return a[:, :HALF] + a[:, HALF:]


def triangle(keep):
    row = lax.broadcasted_iota(jnp.int32, (Q, Q), 0)
    col = lax.broadcasted_iota(jnp.int32, (Q, Q), 1)
    return jnp.where(keep(row, col), 1.0, 0.0).astype(BF16)


def conv(raw, tail, taps):
    ext = jnp.concatenate([tail, raw], 1)
    total = twice(taps[4]) + twice(taps[3]) * raw
    for k in range(1, 4):
        total = total + twice(taps[3 - k]) * pltpu.roll(ext, k, 1)[:, HALF:]
    return total


def conv_back(grad, head, taps):
    ext = jnp.concatenate([grad, head], 1)
    shifted = [grad] + [pltpu.roll(ext, 3 * HALF - k, 1)[:, :Q] for k in range(1, 4)]
    total = twice(taps[3]) * grad
    for k in range(1, 4):
        total = total + twice(taps[3 - k]) * shifted[k]
    return total, shifted


def decay_blocks(run_row, run_col, upper):
    early, late = run_row[:, :HALF], run_row[:, HALF:]
    col_early = jnp.broadcast_to(run_col[:HALF], (HALF, HALF))
    col_late = jnp.broadcast_to(run_col[HALF:], (HALF, HALF))
    first = jnp.exp(jnp.where(upper, early - col_early, NEG))
    cross = jnp.exp(late - col_early)
    second = jnp.exp(jnp.where(upper, late - col_late, NEG))
    return first, cross, second


def stack_blocks(first, cross, second):
    zero = jnp.zeros((HALF, HALF), first.dtype)
    return jnp.concatenate(
        [jnp.concatenate([first, cross], 1), jnp.concatenate([zero, second], 1)], 0
    )


def intersection(b_rows, c_rows):
    b_time = jnp.transpose(b_rows)
    b_high = b_time.astype(BF16)
    b_low = (b_time - b_high.astype(F32)).astype(BF16)
    c_high = c_rows.astype(BF16)
    c_low = (c_rows - c_high.astype(F32)).astype(BF16)
    return nn(
        jnp.concatenate([b_high, b_low, b_high], 1), jnp.concatenate([c_high, c_high, c_low], 0)
    )


def rms_scale(xs, width):
    total = xs[0] * xs[0]
    for x in xs[1:]:
        total = total + x * x
    return lax.rsqrt(jnp.sum(total, -1, keepdims=True) / width + epsilon)


def gain_row(wt_ref, base, heads):
    return wt_ref[base : base + 16, :].astype(F32)[heads : heads + 1]


def softplus(a):
    return jnp.maximum(a, 0.0) + jnp.log1p(jnp.exp(-jnp.abs(a)))


def upper_half():
    row = lax.broadcasted_iota(jnp.int32, (HALF, HALF), 0)
    return row <= lax.broadcasted_iota(jnp.int32, (HALF, HALF), 1)


def valid_row(block, length):
    pos = block * Q + lax.broadcasted_iota(jnp.int32, (1, Q), 1)
    return jnp.where(pos < length, 1.0, 0.0)


def forward_kernel(len_ref, *refs, seq, inner, heads, width, aliased):
    x_refs, (wt_ref, chan_ref, bcc_ref, headc_ref) = refs[:4], refs[4:8]
    refs = refs[8 + aliased :]
    (norm_ref, gate_ref, val_ref, z_ref, y_ref, m_ref, bc_ref, bcz_ref) = refs[:8]
    (step_ref, run_ref, state_ref, stat_ref, proj, vtail, btail, state) = refs[8:]
    block = pl.program_id(0)
    length = len_ref[seq]
    per = inner // heads
    part = width // 4
    states = bc_ref.shape[0] // 2

    @pl.when(block == 0)
    def _():
        vtail[...] = jnp.zeros_like(vtail)
        btail[...] = jnp.zeros_like(btail)
        state[...] = jnp.zeros_like(state)

    @pl.when(block * Q >= length)
    def _():
        norm_ref[...] = jnp.zeros_like(norm_ref)
        stat_ref[...] = jnp.zeros_like(stat_ref)

    @pl.when(block * Q < length)
    def _():
        base = 2 * inner + 2 * states
        gain = gain_row(wt_ref, base, heads)
        xs = [ref[...].astype(F32) for ref in x_refs]
        inv = rms_scale(xs, width)
        for k in range(4):
            cols = slice(k * part, (k + 1) * part)
            norm_ref[:, cols] = (xs[k] * inv * gain[:, cols]).astype(BF16)
        proj[...] = nt(wt_ref[: base + 16, :], norm_ref[...])

        raw = proj[2 * inner : base, :]
        bc_ref[...] = raw
        bcz = conv(raw, btail[...], [bcc_ref[j] for j in range(5)])
        btail[...] = raw[:, HALF:]
        bcz_ref[...] = bcz
        shared = bcz * jax.nn.sigmoid(bcz)
        b_rows, c_rows = shared[:states], shared[states:]
        cb = intersection(b_rows, c_rows)
        cb_blocks = (cb[:HALF, :HALF], cb[:HALF, HALF:], cb[HALF:, HALF:])
        b_low, c_low = b_rows.astype(BF16), c_rows.astype(BF16)

        step_raw = proj[base : base + heads, :] + twice(headc_ref[0])
        step_ref[...] = step_raw
        steps = softplus(step_raw)
        running = times_ones(steps * twice(headc_ref[1]), triangle(lambda s, t: s <= t))
        run_ref[...] = running
        run_cols = jnp.transpose(running)
        ends = running[:, Q - 1 :]
        grow = jnp.exp(running)
        to_end = jnp.exp(ends - running)
        whole = jnp.exp(ends)
        upper = upper_half()

        state_ref[...] = state[...]
        squares = jnp.zeros((1, Q), F32)
        for h in range(heads):
            rows = slice(h * per, (h + 1) * per)
            raw_v = proj[inner + h * per : inner + (h + 1) * per, :]
            gate = proj[rows, :]
            val_ref[rows, :] = raw_v
            gate_ref[rows, :] = gate
            z = conv(raw_v, vtail[rows, :], [chan_ref[j, rows, :] for j in range(5)])
            vtail[rows, :] = raw_v[:, HALF:]
            z_ref[rows, :] = z
            v = z * jax.nn.sigmoid(z)
            w = v * steps[h : h + 1]
            decays = decay_blocks(running[h : h + 1], run_cols[:, h : h + 1], upper)
            grid = stack_blocks(*[(d * g).astype(BF16) for d, g in zip(decays, cb_blocks)])
            old = state[rows, :]
            y = nn(w.astype(BF16), grid) + nn(old.astype(BF16), c_low) * grow[h : h + 1]
            y_ref[rows, :] = y
            fresh = nt((w * to_end[h : h + 1]).astype(BF16), b_low)
            state[rows, :] = old * whole[h : h + 1] + fresh
            u = y + twice(chan_ref[6, rows, :]) * v
            m = u * gate * jax.nn.sigmoid(gate)
            m_ref[rows, :] = m
            squares = squares + jnp.sum(m * m, 0, keepdims=True)
        stat_ref[...] = squares


def middle_kernel(
    len_ref, c0, c1, c2, c3, wo_ref, chan_ref, m_ref, sq_ref,
    nout_ref, b0, b1, b2, b3, gno_ref, stat_ref, gain_acc, nout, *, inner, inner_all, width,
):
    seq, block = pl.program_id(0), pl.program_id(1)
    length = len_ref[seq]
    part = width // 4

    @pl.when((seq == 0) & (block == 0))
    def _():
        gain_acc[...] = jnp.zeros_like(gain_acc)

    @pl.when(block * Q >= length)
    def _():
        nout_ref[...] = jnp.zeros_like(nout_ref)
        stat_ref[...] = jnp.zeros_like(stat_ref)
        for ref in (b0, b1, b2, b3):
            ref[...] = jnp.zeros_like(ref)

    @pl.when(block * Q < length)
    def _():
        valid = valid_row(block, length)
        scale = lax.rsqrt(sq_ref[...] / inner_all + epsilon) * valid
        cot = jnp.concatenate([ref[...] for ref in (c0, c1, c2, c3)], 1)
        gno_ref[...] = nt(wo_ref[...], cot) * valid
        inners = jnp.zeros((1, Q), F32)
        for lo in range(0, inner, 64):
            rows = slice(lo, lo + 64)
            gain = twice(chan_ref[5, rows, :])
            m = m_ref[rows, :]
            gno = gno_ref[rows, :]
            nout[rows, :] = (m * scale * gain).astype(BF16)
            inners = inners + jnp.sum(gno * gain * m, 0, keepdims=True)
            gain_acc[rows, :] += fold(gno * m * scale)
        stat_ref[...] = inners
        nout_time = jnp.transpose(nout[...])
        nout_ref[...] = nout_time
        branch = nn(nout_time, wo_ref[...])
        for k, ref in enumerate((b0, b1, b2, b3)):
            ref[...] = branch[:, k * part : (k + 1) * part].astype(BF16)


def backward_kernel(len_ref, *refs, seq, inner, inner_all, heads, width, blocks):
    x_refs, (wt_ref, chan_ref, bcc_ref, headc_ref) = refs[:4], refs[4:8]
    (gate_ref, val_ref, z_ref, y_ref, gno_ref, bc_ref, bcz_ref) = refs[8:15]
    (step_ref, run_ref, state_ref, sq_ref, stat_ref) = refs[15:20]
    low_ref, g_refs, (chan_acc, bc_acc, head_acc, norm_acc) = refs[20], refs[21:25], refs[25:29]
    low, gstate, vhead, bhead, dcb, wdec, gudec = refs[29:]
    step = pl.program_id(0)
    block = blocks - 1 - step
    length = len_ref[seq]
    per = inner // heads
    part = width // 4
    states = bc_ref.shape[0] // 2
    base = 2 * inner + 2 * states

    @pl.when(step == 0)
    def _():
        chan_acc[...] = jnp.zeros_like(chan_acc)
        bc_acc[...] = jnp.zeros_like(bc_acc)
        head_acc[...] = jnp.zeros_like(head_acc)
        norm_acc[...] = jnp.zeros_like(norm_acc)
        low[base:, :] = jnp.zeros_like(low[base:, :])
        gstate[...] = jnp.zeros_like(gstate)
        vhead[...] = jnp.zeros_like(vhead)
        bhead[...] = jnp.zeros_like(bhead)

    @pl.when(block * Q >= length)
    def _():
        low_ref[...] = jnp.zeros_like(low_ref)
        for ref in g_refs:
            ref[...] = jnp.zeros_like(ref)

    @pl.when(block * Q < length)
    def _():
        inv_gate = lax.rsqrt(sq_ref[...] / inner_all + epsilon)
        pull = inv_gate * inv_gate * inv_gate * stat_ref[...] / inner_all

        bcz = bcz_ref[...]
        sig = jax.nn.sigmoid(bcz)
        shared = bcz * sig
        shared_slope = sig * (1.0 + bcz * (1.0 - sig))
        b_rows, c_rows = shared[:states], shared[states:]
        cb = intersection(b_rows, c_rows)
        cb_blocks = (cb[:HALF, :HALF], cb[:HALF, HALF:], cb[HALF:, HALF:])
        b_low, c_low = b_rows.astype(BF16), c_rows.astype(BF16)

        step_raw = step_ref[...]
        steps = softplus(step_raw)
        running = run_ref[...]
        run_cols = jnp.transpose(running)
        ends = running[:, Q - 1 :]
        grow = jnp.exp(running)
        to_end = jnp.exp(ends - running)
        whole = jnp.exp(ends)
        upper = upper_half()

        direct, both, after, through = [], [], [], []
        for h in range(heads):
            rows = slice(h * per, (h + 1) * per)
            gate, z, y, gno = gate_ref[rows, :], z_ref[rows, :], y_ref[rows, :], gno_ref[rows, :]
            gain = twice(chan_ref[5, rows, :])
            skip = twice(chan_ref[6, rows, :])
            sig_g = jax.nn.sigmoid(gate)
            silu_g = gate * sig_g
            sig_z = jax.nn.sigmoid(z)
            v = z * sig_z
            u = y + skip * v
            m = u * silu_g
            gm = inv_gate * gain * gno - m * pull
            low[rows, :] = (gm * u * (sig_g * (1.0 + gate * (1.0 - sig_g)))).astype(BF16)
            gu = gm * silu_g
            chan_acc[5, rows, :] += fold(gu * v)
            w = v * steps[h : h + 1]
            w_low, gu_low = w.astype(BF16), gu.astype(BF16)
            decays = decay_blocks(running[h : h + 1], run_cols[:, h : h + 1], upper)
            grid = stack_blocks(*[(d * g).astype(BF16) for d, g in zip(decays, cb_blocks)])
            gw_in = nt(gu_low, grid)
            pair = nn(jnp.transpose(w_low), gu_low)
            pieces = (pair[:HALF, :HALF], pair[:HALF, HALF:], pair[HALF:, HALF:])
            for i in range(3):
                if h == 0:
                    dcb[i] = decays[i] * pieces[i]
                else:
                    dcb[i] += decays[i] * pieces[i]
            gs = gstate[rows, :]
            gs_low = gs.astype(BF16)
            gw_out = nn(gs_low, b_low) * to_end[h : h + 1]
            gw = gw_in + gw_out
            direct.append(jnp.sum(gw * v, 0, keepdims=True))
            both.append(
                jnp.sum(gu_low.astype(F32) * y - gw_in * w_low.astype(F32), 0, keepdims=True)
            )
            after.append(jnp.sum(gw_out * w, 0, keepdims=True))
            through.append(
                jnp.sum(gs * state_ref[rows, :], 0, keepdims=True) * whole[h : h + 1]
            )
            gud = (gu * grow[h : h + 1]).astype(BF16)
            gudec[rows, :] = gud
            wdec[rows, :] = (w * to_end[h : h + 1]).astype(BF16)
            gz = (skip * gu + gw * steps[h : h + 1]) * (sig_z * (1.0 + z * (1.0 - sig_z)))
            taps = [chan_ref[j, rows, :] for j in range(4)]
            gv, shifted = conv_back(gz, vhead[rows, :], taps)
            vhead[rows, :] = gz[:, :HALF]
            raw_v = val_ref[rows, :]
            for k in range(4):
                chan_acc[3 - k, rows, :] += fold(shifted[k] * raw_v)
            chan_acc[4, rows, :] += fold(gz)
            low[inner + h * per : inner + (h + 1) * per, :] = gv.astype(BF16)

        direct = jnp.concatenate(direct, 0)
        both = jnp.concatenate(both, 0)
        after = jnp.concatenate(after, 0)
        through = jnp.sum(jnp.concatenate(through, 0), -1, keepdims=True)
        g_decay = (
            times_ones(both, triangle(lambda t, r: t >= r))
            + times_ones(after, triangle(lambda s, r: s < r))
            + through
        )
        head_acc[1] += fold(steps * g_decay)
        g_step = (direct + twice(headc_ref[1]) * g_decay) * jax.nn.sigmoid(step_raw)
        head_acc[0] += fold(g_step)
        low[base : base + 16, :] = jnp.concatenate(
            [g_step, jnp.zeros((16 - heads, Q), F32)], 0
        ).astype(BF16)

        dcb_low = stack_blocks(*[dcb[i].astype(BF16) for i in range(3)])
        gud, wd = gudec[...], wdec[...]
        gs_old = gstate[...]
        g_c = nn(b_low, dcb_low) + nn(jnp.transpose(state_ref[...]).astype(BF16), gud)
        g_b = nt(c_low, dcb_low) + nn(jnp.transpose(gs_old).astype(BF16), wd)
        fresh = nt(gud, c_low)
        for h in range(heads):
            rows = slice(h * per, (h + 1) * per)
            gstate[rows, :] = gs_old[rows] * whole[h : h + 1] + fresh[rows]
        gbcz = jnp.concatenate([g_b, g_c], 0) * shared_slope
        gbc, shifted = conv_back(gbcz, bhead[...], [bcc_ref[j] for j in range(4)])
        bhead[...] = gbcz[:, :HALF]
        raw = bc_ref[...]
        for k in range(4):
            bc_acc[3 - k] += fold(shifted[k] * raw)
        bc_acc[4] += fold(gbcz)
        low[2 * inner : base, :] = gbc.astype(BF16)

        lows = jnp.transpose(low[...])
        low_ref[...] = lows
        g_norm = nn(lows, wt_ref[...])
        gain = gain_row(wt_ref, base, heads)
        xs = [ref[...].astype(F32) for ref in x_refs]
        inv = rms_scale(xs, width)
        prod = None
        for k in range(4):
            cols = slice(k * part, (k + 1) * part)
            here = g_norm[:, cols] * xs[k]
            norm_acc[:, cols] += jnp.sum((here * inv).reshape(Q // 8, 8, part), 0)
            weighted = here * gain[:, cols]
            prod = weighted if prod is None else prod + weighted
        pull_x = inv * inv * inv * (jnp.sum(prod, -1, keepdims=True) / width)
        for k in range(4):
            cols = slice(k * part, (k + 1) * part)
            g_refs[k][...] = (inv * gain[:, cols] * g_norm[:, cols] - xs[k] * pull_x).astype(BF16)


def shape(dims, kind=F32):
    return jax.ShapeDtypeStruct(dims, kind)


def params(count):
    return pltpu.CompilerParams(
        dimension_semantics=("arbitrary",) * count, vmem_limit_bytes=60 << 20
    )


def fixed(array):
    rank = array.ndim
    return pl.BlockSpec(array.shape, lambda *_: (0,) * rank, pipeline_mode=pl.Buffered(1))


def run_forward(seq, seqs, lengths, xs, wt, chan, bcc, headc, before):
    part = xs[0].shape[1]
    width = 4 * part
    inner, heads, states2 = chan.shape[1], headc.shape[1], bcc.shape[1]
    blocks = SEQ_LEN // Q
    rows = seqs * SEQ_LEN
    at = lambda c: seq * blocks + c
    col = lambda n: pl.BlockSpec((n, Q), lambda c, lens: (0, at(c)))
    out_shape = [
        shape((rows, width), BF16),
        *[shape((inner, rows))] * 5,
        *[shape((states2, rows))] * 2,
        *[shape((heads, rows))] * 2,
        shape((seqs * blocks * inner, states2 // 2)),
        shape((1, SEQ_LEN)),
    ]
    out_specs = [
        pl.BlockSpec((Q, width), lambda c, lens: (at(c), 0)),
        *[col(inner)] * 5,
        *[col(states2)] * 2,
        *[col(heads)] * 2,
        pl.BlockSpec((inner, states2 // 2), lambda c, lens: (at(c), 0)),
        pl.BlockSpec((1, Q), lambda c, lens: (0, c)),
    ]
    consts = (wt, chan, bcc, headc)
    return pl.pallas_call(
        functools.partial(
            forward_kernel,
            seq=seq,
            inner=inner,
            heads=heads,
            width=width,
            aliased=len(before),
        ),
        out_shape=out_shape,
        grid_spec=pltpu.PrefetchScalarGridSpec(
            num_scalar_prefetch=1,
            grid=(blocks,),
            in_specs=[
                *[pl.BlockSpec((Q, part), lambda c, lens: (c, 0))] * 4,
                *[fixed(array) for array in consts],
                *[pl.BlockSpec(memory_space=pl.ANY)] * len(before),
            ],
            out_specs=out_specs,
            scratch_shapes=[
                pltpu.VMEM((2 * inner + states2 + 16, Q), F32),
                pltpu.VMEM((inner, HALF), F32),
                pltpu.VMEM((states2, HALF), F32),
                pltpu.VMEM((inner, states2 // 2), F32),
            ],
        ),
        input_output_aliases={9 + i: i for i in range(len(before))},
        compiler_params=params(1),
        name="mixer_forward",
    )(lengths, *xs, *consts, *before)


def run_middle(lengths, cots, wo, chan, m, squares, inner_all):
    rows, part = cots[0].shape
    width = 4 * part
    inner = wo.shape[0]
    blocks = SEQ_LEN // Q
    at = lambda q, c: q * blocks + c
    piece = pl.BlockSpec((Q, part), lambda q, c, lens: (at(q, c), 0))
    col = lambda n: pl.BlockSpec((n, Q), lambda q, c, lens: (0, at(q, c)))
    return pl.pallas_call(
        functools.partial(middle_kernel, inner=inner, inner_all=inner_all, width=width),
        out_shape=[
            shape((rows, inner), BF16),
            *[shape((rows, part), BF16)] * 4,
            shape((inner, rows)),
            shape((1, rows)),
            shape((inner, HALF)),
        ],
        grid_spec=pltpu.PrefetchScalarGridSpec(
            num_scalar_prefetch=1,
            grid=(rows // SEQ_LEN, blocks),
            in_specs=[*[piece] * 4, fixed(wo), fixed(chan), col(inner), col(1)],
            out_specs=[
                pl.BlockSpec((Q, inner), lambda q, c, lens: (at(q, c), 0)),
                *[piece] * 4,
                col(inner),
                col(1),
                pl.BlockSpec((inner, HALF), lambda q, c, lens: (0, 0)),
            ],
            scratch_shapes=[pltpu.VMEM((inner, Q), BF16)],
        ),
        compiler_params=params(2),
        name="mixer_middle",
    )(lengths, *cots, wo, chan, m, squares)


def run_backward(seq, lengths, xs, wt, chan, bcc, headc, saved, squares, stat, inner_all):
    part = xs[0].shape[1]
    width = 4 * part
    inner, heads, states2 = chan.shape[1], headc.shape[1], bcc.shape[1]
    blocks = SEQ_LEN // Q
    back = lambda c: blocks - 1 - c
    at = lambda c: seq * blocks + back(c)
    col = lambda n: pl.BlockSpec((n, Q), lambda c, lens: (0, at(c)))
    piece = pl.BlockSpec((Q, part), lambda c, lens: (back(c), 0))
    consts = (wt, chan, bcc, headc)
    accs = [(6, inner, HALF), (5, states2, HALF), (2, heads, HALF), (8, width)]
    keep = lambda dims: pl.BlockSpec(dims, lambda c, lens: (0,) * len(dims))
    return pl.pallas_call(
        functools.partial(
            backward_kernel,
            seq=seq,
            inner=inner,
            inner_all=inner_all,
            heads=heads,
            width=width,
            blocks=blocks,
        ),
        out_shape=[
            shape((SEQ_LEN, wt.shape[0]), BF16),
            *[shape((SEQ_LEN, part), BF16)] * 4,
            *[shape(dims) for dims in accs],
        ],
        grid_spec=pltpu.PrefetchScalarGridSpec(
            num_scalar_prefetch=1,
            grid=(blocks,),
            in_specs=[
                *[piece] * 4,
                *[fixed(array) for array in consts],
                *[col(inner)] * 5,
                *[col(states2)] * 2,
                *[col(heads)] * 2,
                pl.BlockSpec((inner, states2 // 2), lambda c, lens: (at(c), 0)),
                *[col(1)] * 2,
            ],
            out_specs=[
                pl.BlockSpec((Q, wt.shape[0]), lambda c, lens: (back(c), 0)),
                *[piece] * 4,
                *[keep(dims) for dims in accs],
            ],
            scratch_shapes=[
                pltpu.VMEM((wt.shape[0], Q), BF16),
                pltpu.VMEM((inner, states2 // 2), F32),
                pltpu.VMEM((inner, HALF), F32),
                pltpu.VMEM((states2, HALF), F32),
                pltpu.VMEM((3, HALF, HALF), F32),
                pltpu.VMEM((inner, Q), BF16),
                pltpu.VMEM((inner, Q), BF16),
            ],
        ),
        compiler_params=params(1),
        name="mixer_backward",
    )(lengths, *xs, *consts, *saved, squares, stat)


def exchange(a, axis, bit):
    return lax.ppermute(a, axis, [(i, i ^ bit) for i in range(lax.axis_size(axis))])


def exchange_sum(a, axis):
    bit = 1
    while bit < lax.axis_size(axis):
        a = a + exchange(a, axis, bit)
        bit *= 2
    return a


def gather_pieces(a):
    across = exchange(a, "tensor", 2)
    beside = exchange(a, "tensor", 1)
    return a, beside, across, exchange(across, "tensor", 1)


def reduce_pieces(pieces, kind=BF16):
    own, beside, across, corner = pieces
    got_corner = exchange(corner.astype(kind), "tensor", 1)
    got_beside = exchange(beside.astype(kind), "tensor", 1)
    onward = (across.astype(F32) + got_corner.astype(F32)).astype(kind)
    here = own.astype(F32) + got_beside.astype(F32)
    return here + exchange(onward, "tensor", 2).astype(F32)


def place():
    index = lax.axis_index("dp")
    return index // 2, index % 2


def take(a, index, dim):
    return lax.dynamic_index_in_dim(a, index, dim, keepdims=False)


def round_to(count, tile):
    return count // tile * tile


def weight_columns(a):
    tensor = lax.axis_index("tensor")
    cols = a.shape[0]
    if lax.axis_size("dp") != 8:
        whole = jnp.transpose(lax.all_gather(jnp.transpose(a), "dp", axis=0, tiled=True))
        blocks = whole.reshape(cols, 4, -1)
        return jnp.concatenate([take(blocks, tensor ^ m, 1) for m in range(4)], 1)
    z, x = place()
    cut = round_to(cols * 7 // 10, 16)
    first, second = a[:cut], a[cut:]
    beside = exchange(second, "dp", 1)
    mine = [first] + [exchange(first, "dp", 2 * j) for j in (3, 2, 1)]
    other = [exchange(first, "dp", 1)]
    pair = jnp.stack([second, beside])
    both = jnp.stack([pair] + [exchange(pair, "dp", 2 * j) for j in (3, 2, 1)])
    mine = jnp.stack(mine)
    other = jnp.concatenate([other[0][None], exchange(mine[1:], "dp", 1)], 0)
    out = []
    for m in range(4):
        step = (tensor ^ m) ^ z
        slot = (4 - step) % 4
        top = [take(mine, slot, 0), take(other, slot, 0)]
        low = take(both, slot, 0)
        for side in (0, 1):
            own = x == side
            out.append(
                jnp.concatenate(
                    [jnp.where(own, top[0], top[1]), jnp.where(own, low[0], low[1])], 0
                )
            )
    return jnp.concatenate(out, 1)


def along_z(pick):
    z, _ = place()
    total = pick(z)
    for j in (3, 2, 1):
        total = total + exchange(pick(z ^ j).astype(BF16), "dp", 2 * j).astype(F32)
    return total


def weight_rows(a):
    tensor = lax.axis_index("tensor")
    width, cols = a.shape
    if lax.axis_size("dp") != 8:
        blocks = a.reshape(4, -1, cols)
        ordered = jnp.concatenate([take(blocks, tensor ^ m, 0) for m in range(4)], 0)
        return lax.psum_scatter(ordered, "dp", scatter_dimension=0, tiled=True)
    _, x = place()
    blocks = a.reshape(4, 2, width // 8, cols)
    cut = round_to(cols * 2 // 3, HALF)
    first, second = blocks[..., :cut], blocks[..., cut:]
    got = exchange(take(first, 1 - x, 1).astype(BF16), "dp", 1).astype(F32)
    pairs = along_z(lambda z: take(second, z ^ tensor, 0))
    halves = take(first, x, 1) + got
    early = along_z(lambda z: take(halves, z ^ tensor, 0))
    late = exchange(take(pairs, 1 - x, 0).astype(BF16), "dp", 1).astype(F32)
    return jnp.concatenate([early, take(pairs, x, 0) + late], 1)


def over_rows(left, right):
    return lax.dot_general(
        left, right, (((0,), (0,)), ((), ())), preferred_element_type=F32
    )


def lanes(a):
    return jnp.broadcast_to(a[..., None], a.shape + (HALF,))


def small_constants(conv_x, conv_bc, dt_bias, a_log, skip_d, gate_gain):
    per = conv_x.shape[1] // skip_d.shape[0]
    chan = lanes(jnp.concatenate([conv_x, gate_gain[None], jnp.repeat(skip_d, per)[None]], 0))
    return chan, lanes(conv_bc), lanes(jnp.stack([dt_bias, -jnp.exp(a_log)], 0))


def per_device(
    tokens,
    lengths,
    grad_out,
    norm_gain,
    w_gate,
    w_value,
    w_bc,
    w_dt,
    conv_x,
    conv_bc,
    dt_bias,
    a_log,
    skip_d,
    gate_gain,
    w_out,
):
    tensor_count = lax.axis_size("tensor")
    tensor = lax.axis_index("tensor")
    rows, _ = tokens.shape
    seqs = rows // SEQ_LEN
    inner = w_gate.shape[1]
    inner_all = inner * tensor_count
    heads = w_dt.shape[1]
    states2 = w_bc.shape[1]
    base = 2 * inner + states2

    local = jnp.concatenate(
        [
            w_gate,
            w_value,
            w_bc,
            w_dt,
            norm_gain[:, None],
            jnp.zeros((w_gate.shape[0], 15 - heads), BF16),
        ],
        1,
    )
    xs = [gather_pieces(tokens[q * SEQ_LEN : (q + 1) * SEQ_LEN]) for q in range(seqs)]
    cots = gather_pieces(grad_out)
    wt = jnp.pad(weight_columns(jnp.transpose(local)), ((0, HALF - 16), (0, 0)))
    w_out, wt = lax.optimization_barrier((w_out, wt))
    wo = weight_columns(jnp.transpose(w_out))
    chan, bcc, headc = small_constants(conv_x, conv_bc, dt_bias, a_log, skip_d, gate_gain)

    saved, squares = [], []
    for q in range(seqs):
        *saved, here = run_forward(q, seqs, lengths, xs[q], wt, chan, bcc, headc, saved)
        squares.append(exchange_sum(here, "tensor"))
    squares = jnp.concatenate(squares, 1)
    normed, gate, val, z, y, m, *shared = saved
    nout, *branch, gno, stat, gain_acc = run_middle(lengths, cots, wo, chan, m, squares, inner_all)
    stat = exchange_sum(stat, "tensor")
    g_out = jnp.concatenate([over_rows(cot, nout) for cot in cots], 0)
    branch = reduce_pieces(branch)
    out_rows = (tokens.astype(F32) + branch).astype(BF16)
    grad_out_rows = weight_rows(g_out)

    grad_rows, accs, g_all = [], None, None
    kept = (gate, val, z, y, gno, *shared)
    for q in range(seqs):
        lows, *rest = run_backward(
            q, lengths, xs[q], wt, chan, bcc, headc, kept, squares, stat, inner_all
        )
        gin, here = rest[:4], rest[4:]
        accs = here if accs is None else [a + b for a, b in zip(accs, here)]
        grad_rows.append(reduce_pieces(gin))
        here = over_rows(normed[q * SEQ_LEN : (q + 1) * SEQ_LEN], lows)
        g_all = here if g_all is None else g_all + here
    valid = (jnp.arange(SEQ_LEN)[None] < lengths[:, None]).reshape(rows)[:, None]
    grad_rows = jnp.concatenate(grad_rows, 0) + jnp.where(valid, grad_out.astype(F32), 0.0)

    chan_acc, bc_acc, head_acc, norm_acc = accs
    column = jnp.arange(g_all.shape[1]) == base + heads
    g_all = jnp.where(column[None], jnp.sum(norm_acc, 0)[:, None], g_all)
    grads = weight_rows(g_all)
    rest = grads[:, 2 * inner :].reshape(tensor_count, -1, states2 + HALF)
    rest = reduce_pieces(
        [lax.dynamic_index_in_dim(rest, tensor ^ i, 0, keepdims=False) for i in range(4)], F32
    )
    sizes = [5 * inner, inner, inner, 2 * heads, 5 * states2]
    flat = jnp.concatenate(
        [
            jnp.sum(chan_acc, -1).reshape(-1),
            jnp.sum(gain_acc, -1),
            jnp.sum(head_acc, -1).reshape(-1),
            jnp.sum(bc_acc, -1).reshape(-1),
        ]
    )
    flat = exchange_sum(flat, "dp")
    cuts = [sum(sizes[: i + 1]) for i in range(4)]
    g_conv, g_skip, g_gain, g_head, g_conv_bc = jnp.split(flat, cuts)
    g_conv_bc = exchange_sum(g_conv_bc, "tensor")
    return (
        out_rows,
        grad_rows,
        rest[:, states2 + heads],
        grads[:, :inner],
        grads[:, inner : 2 * inner],
        rest[:, :states2],
        grads[:, base : base + heads],
        g_conv.reshape(5, inner),
        g_conv_bc.reshape(5, states2),
        g_head[:heads],
        g_head[heads:] * -jnp.exp(a_log),
        jnp.sum(g_skip.reshape(heads, -1), -1),
        g_gain,
        grad_out_rows,
    )


def solution(mesh):
    return mapped(mesh)


def mapped(mesh):
    both = ("dp", "tensor")
    return jax.shard_map(
        per_device,
        mesh=mesh,
        in_specs=(
            P("dp", "tensor"),
            P("dp"),
            P("dp", "tensor"),
            P("dp"),
            P("dp", "tensor"),
            P("dp", "tensor"),
            P("dp", None),
            P("dp", "tensor"),
            P(None, "tensor"),
            P(),
            P("tensor"),
            P("tensor"),
            P("tensor"),
            P("tensor"),
            P("dp", "tensor"),
        ),
        out_specs=(
            P("dp", "tensor"),
            P("dp", "tensor"),
            P(both),
            P("dp", "tensor"),
            P("dp", "tensor"),
            P(both, None),
            P("dp", "tensor"),
            P(None, "tensor"),
            P(),
            P("tensor"),
            P("tensor"),
            P("tensor"),
            P("tensor"),
            P("dp", "tensor"),
        ),
        check_vma=False,
    )
```

profile of v0, /device:TPU:0, one launch (start us, length us, event | category | flops | bytes accessed | tf_op | source)
XLA Modules:
  0.0 544.7 jit_solution(9886220235449167826)
XLA Ops:
  3.7 1.4 concatenate.86
  5.2 5.1 collective-permute-start.3
  11.0 1.7 collective-permute-start.8
  12.7 4.2 collective-permute-done.3
  16.9 12.9 %collective-permute-done.4 = bf16[896,128]{1,0:T(8,128)(2,1)S(1)} collective-permute-done((bf16[896,128]{1,0:T(8,128)(2,1)S(1)}, bf16[896,128]{1,0:T(8,128)(2,1)S(1)}, u32[]{:S(2)}, u32[]{:S(2)}) %collective-permute-start.4) | collective-permute-done | bytes 229408 | tf_op jit(solution)/shard_map/ppermute | solution.py:579
  29.9 1.6 collective-permute-start.7
  32.2 2.5 collective-permute-start.9
  34.6 1.9 collective-permute-start.11
  37.2 5.0 collective-permute-done.9
  42.2 1.5 collective-permute-start.1
  43.7 6.7 %collective-permute-done.10 = bf16[2,400,128]{2,1,0:T(8,128)(2,1)S(1)} collective-permute-done((bf16[2,400,128]{2,1,0:T(8,128)(2,1)}, bf16[2,400,128]{2,1,0:T(8,128)(2,1)S(1)}, u32[]{:S(2)}, u32[]{:S(2)}) %collective-permute-start.10) | collective-permute-done | bytes 204832 | tf_op jit(solution)/shard_map/ppermute | solution.py:579
  53.2 1.8 pad.4.refs_4_
  55.8 2.1 collective-permute-start.12
  57.9 1.6 collective-permute-start.17
  59.4 1.7 fusion.41
  61.1 1.6 collective-permute-start.25
  65.9 3.5 collective-permute-done.14
  69.4 1.5 collective-permute-start.15
  71.5 2.4 collective-permute-done.15
  73.9 2.1 collective-permute-start.18
  76.1 4.3 collective-permute-done.18
  81.1 5.2 collective-permute-done.19
  86.8 4.2 collective-permute-done.20
  92.2 21.3 %collective-permute-done.25.refs_2_ = bf16[2048,256]{1,0:T(8,128)(2,1)} collective-permute-done((bf16[2048,256]{1,0:T(8,128)(2,1)S(1)}, bf16[2048,256]{1,0:T(8,128)(2,1)}, u32[]{:S(2)}, u32[]{:S(2)}) %collective-permute-start.25) | collective-permute-done | bytes 1048608 | tf_op jit(solution)/shard_map/ppermute | solution.py:579
  116.4 14.4 %collective-permute-done.22.refs_2_ = bf16[2048,256]{1,0:T(8,128)(2,1)S(1)} collective-permute-done((bf16[2048,256]{1,0:T(8,128)(2,1)S(1)}, bf16[2048,256]{1,0:T(8,128)(2,1)S(1)}, u32[]{:S(2)}, u32[]{:S(2)}) %collective-permute-start.22) | collective-permute-done | bytes 1048608 | tf_op jit(solution)/shard_map/ppermute | solution.py:579
  136.4 1.8 broadcast_in_dim.74.refs_5_.chan_ref
  139.9 31.8 %mixer_forward.2 = (bf16[4096,1024]{1,0:T(8,128)(2,1)}, f32[512,4096]{1,0:T(8,128)}, f32[512,4096]{1,0:T(8,128)}, f32[512,4096]{1,0:T(8,128)}, f32[512,4096]{1,0...) custom-call(s32[2]{0:T(128)} %len_ref.9, ...), custom_call_target="tpu_custom_call" | custom-call | tf_op jit(solution)/shard_map/mixer_forward/pallas_call | solution.py:452
  171.9 23.6 %mixer_forward.3 = (bf16[4096,1024]{1,0:T(8,128)(2,1)}, f32[512,4096]{1,0:T(8,128)}, f32[512,4096]{1,0:T(8,128)}, f32[512,4096]{1,0:T(8,128)}, f32[512,4096]{1,0...) custom-call(s32[2]{0:T(128)} %len_ref.9, ...), custom_call_target="tpu_custom_call", output_to_operand_aliasing={{0}: (9, {}), {1}: (10, {}), {2}: (11, {}), {3}: (12, {}), ... | custom-call | tf_op jit(solution)/shard_map/mixer_forward/pallas_call | solution.py:452
  196.6 1.6 collective-permute-start.28
  200.4 2.3 collective-permute-done.30
  203.3 23.1 %mixer_middle.1 = (bf16[4096,512]{1,0:T(8,128)(2,1)}, bf16[4096,256]{1,0:T(8,128)(2,1)}, bf16[4096,256]{1,0:T(8,128)(2,1)}, bf16[4096,256]{1,0:T(8,128)(2,1)}, b...) custom-call(s32[2]{0:T(128)} %len_ref.9, bf16[4096,256]{1,0:T(8,128)(2,1)} %c0.1, ...), custom_call_target="tpu_custom_call" | custom-call | tf_op jit(solution)/shard_map/mixer_middle/pallas_call | solution.py:492
  226.4 4.3 convolution_bitcast_fusion.3
  230.7 2.9 convolution_bitcast_fusion
  233.6 2.9 convolution_bitcast_fusion.1
  236.5 2.9 convolution_bitcast_fusion.2
  241.4 11.3 %collective-permute-start.62 = (bf16[2,128,256]{2,1,0:T(8,128)(2,1)}, bf16[2,128,256]{2,1,0:T(8,128)(2,1)S(1)}, u32[]{:S(2)}, u32[]{:S(2)}) collective-permute-start(bf16[2,128,256]{2,1,0:T(8,128)(2,1)} %get-tuple-element.164), channel_id=1, source_target_pairs={{0,24},{4,28},{8,16},{12,20},{16,8},{20,12},{24,0},{28,4},{1,25},{... | collective-permute-start | bytes 393224 | tf_op jit(solution)/shard_map/ppermute | solution.py:579
  254.8 2.4 collective-permute-done.35
  257.8 38.3 %mixer_backward.2 = (bf16[2048,1408]{1,0:T(8,128)(2,1)}, bf16[2048,256]{1,0:T(8,128)(2,1)}, bf16[2048,256]{1,0:T(8,128)(2,1)}, bf16[2048,256]{1,0:T(8,128)(2,1)}...) custom-call(s32[2]{0:T(128)} %len_ref.9, ...), custom_call_target="tpu_custom_call" | custom-call | tf_op jit(solution)/shard_map/mixer_backward/pallas_call | solution.py:531
  296.1 29.3 %mixer_backward.3 = (bf16[2048,1408]{1,0:T(8,128)(2,1)}, bf16[2048,256]{1,0:T(8,128)(2,1)}, bf16[2048,256]{1,0:T(8,128)(2,1)}, bf16[2048,256]{1,0:T(8,128)(2,1)}...) custom-call(s32[2]{0:T(128)} %len_ref.9, ...), custom_call_target="tpu_custom_call" | custom-call | tf_op jit(solution)/shard_map/mixer_backward/pallas_call | solution.py:531
  327.6 1.9 add_reduce_fusion
  330.4 10.3 %fusion = f32[1024,1408]{1,0:T(8,128)S(1)} fusion(bf16[2048,1408]{1,0:T(8,128)(2,1)} %get-tuple-element.109, bf16[4096,1024]{1,0:T(8,128)(2,1)} %get-tuple-element.107), kind=kOutput, calls=%fused_computation.2 | convolution fusion | flops 5905580032 | bytes 15728640 | tf_op jit(solution)/shard_map/dot_general | solution.py:679
  340.7 10.5 %add_select_fusion = f32[1024,1408]{1,0:T(8,128)S(1)} fusion(f32[1024,1408]{1,0:T(8,128)S(1)} %fusion, f32[1024]{0:T(1024)S(1)} %add_reduce_fusion.2, pred[1408]{0:T(1024)(128)(4,1)S(1)} %copy-done.29, bf16[2048,1408]{1,0:T(8,128)(2,1)} %get-tuple-element.108, bf16[4096,1024]{1,0:T(8,128)(2,1)} %get-tuple-element.107), kind=kOutput, calls=%fused_computation | convolution fusion | flops 5908463616 | bytes 21501312 | tf_op jit(solution)/shard_map/dot_general | solution.py:679
  353.6 1.7 collective-permute-done.54
  355.4 11.9 %collective-permute-start.55 = (f32[4880]{0:T(1024)S(1)}, f32[4880]{0:T(1024)S(1)}, u32[]{:S(2)}, u32[]{:S(2)}) collective-permute-start(f32[4880]{0:T(1024)S(1)} %add.311), channel_id=1, source_target_pairs={{0,16},{4,20},{8,24},{12,28},{16,0},{20,4},{24,8},{28,12},{1,17},{... | collective-permute-start | bytes 58568 | tf_op jit(solution)/shard_map/ppermute | solution.py:579
  368.2 1.5 collective-permute-start.42
  370.9 2.6 collective-permute-start.43
  374.2 3.4 collective-permute-start.44
  379.4 1.8 collective-permute-start.65
  385.4 1.8 collective-permute-start.49
  387.2 5.0 collective-permute-done.43
  393.5 1.9 collective-permute-start.45
  397.8 16.2 %collective-permute-done.45 = bf16[128,512]{1,0:T(8,128)(2,1)S(1)} collective-permute-done((bf16[128,512]{1,0:T(8,128)(2,1)S(1)}, bf16[128,512]{1,0:T(8,128)(2,1)S(1)}, u32[]{:S(2)}, u32[]{:S(2)}) %collective-permute-start.45) | collective-permute-done | bytes 131104 | tf_op jit(solution)/shard_map/ppermute | solution.py:579
  414.9 3.3 collective-permute-done.61
  423.9 2.0 bitcast_add_fusion
  426.5 1.7 collective-permute-start.51
  428.6 2.3 collective-permute-start.52
  431.2 5.3 collective-permute-done.50
  436.5 12.5 %collective-permute-done.51 = bf16[128,896]{1,0:T(8,128)(2,1)S(1)} collective-permute-done((bf16[128,896]{1,0:T(8,128)(2,1)S(1)}, bf16[128,896]{1,0:T(8,128)(2,1)S(1)}, u32[]{:S(2)}, u32[]{:S(2)}) %collective-permute-start.51) | collective-permute-done | bytes 229408 | tf_op jit(solution)/shard_map/ppermute | solution.py:579
  452.1 2.2 add_convert_fusion.1
  455.5 19.6 %collective-permute-done.38 = bf16[2048,256]{1,0:T(8,128)(2,1)S(1)} collective-permute-done((bf16[2048,256]{1,0:T(8,128)(2,1)S(1)}, bf16[2048,256]{1,0:T(8,128)(2,1)S(1)}, u32[]{:S(2)}, u32[]{:S(2)}) %collective-permute-start.38) | collective-permute-done | bytes 1048608 | tf_op jit(solution)/shard_map/ppermute | solution.py:579
  475.6 22.0 %collective-permute-done.41 = bf16[2048,256]{1,0:T(8,128)(2,1)S(1)} collective-permute-done((bf16[2048,256]{1,0:T(8,128)(2,1)S(1)}, bf16[2048,256]{1,0:T(8,128)(2,1)S(1)}, u32[]{:S(2)}, u32[]{:S(2)}) %collective-permute-start.41) | collective-permute-done | bytes 1048608 | tf_op jit(solution)/shard_map/ppermute | solution.py:579
  498.1 6.2 %maximum_add_fusion = f32[4096,256]{1,0:T(8,128)} fusion(f32[2048,256]{1,0:T(8,128)S(1)} %convert_add_fusion, f32[2048,256]{1,0:T(8,128)S(1)} %convert_add_fusion.1, bf16[4096,256]{1,0:T(8,128)(2,1)} %c0.1, pred[4096]{0:T(1024)(128)(4,1)S(1)} %lt.161), kind=kLoop, calls=%fused_computation.1 | loop fusion | flops 4194304 | bytes 10489856 | tf_op jit(solution)/shard_map/add | solution.py:764
  504.3 37.7 %collective-permute-done.33 = bf16[4096,256]{1,0:T(8,128)(2,1)S(1)} collective-permute-done((bf16[4096,256]{1,0:T(8,128)(2,1)S(1)}, bf16[4096,256]{1,0:T(8,128)(2,1)S(1)}, u32[]{:S(2)}, u32[]{:S(2)}) %collective-permute-start.33) | collective-permute-done | bytes 2097184 | tf_op jit(solution)/shard_map/ppermute | solution.py:579
  542.0 2.5 add_convert_fusion
  (272 shorter events, 64.8 us)
Async XLA Ops:
  5.2 11.7 %collective-permute-start.3 = (bf16[896,128]{1,0:T(8,128)(2,1)S(1)}, bf16[896,128]{1,0:T(8,128)(2,1)S(1)}, u32[]{:S(2)}, u32[]{:S(2)}) collective-permute-start(bf16[896,128]{1,0:T(8,128)(2,1)S(1)} %get-tuple-element.189), channel_id=1, source_target_pairs={{0,24},{4,28},{8,16},{12,20},{16,8},{20,12},{24,0},{28,4},{1,25},{... | collective-permute-start | bytes 688136 | tf_op jit(solution)/shard_map/ppermute | solution.py:579
  10.3 19.5 %collective-permute-start.4 = (bf16[896,128]{1,0:T(8,128)(2,1)S(1)}, bf16[896,128]{1,0:T(8,128)(2,1)S(1)}, u32[]{:S(2)}, u32[]{:S(2)}) collective-permute-start(bf16[896,128]{1,0:T(8,128)(2,1)S(1)} %get-tuple-element.189), channel_id=1, source_target_pairs={{0,16},{4,20},{8,24},{12,28},{16,0},{20,4},{24,8},{28,12},{1,17},{... | collective-permute-start | bytes 688136 | tf_op jit(solution)/shard_map/ppermute | solution.py:579
  10.3 19.5 %collective-permute-start.5 = (bf16[896,128]{1,0:T(8,128)(2,1)S(1)}, bf16[896,128]{1,0:T(8,128)(2,1)S(1)}, u32[]{:S(2)}, u32[]{:S(2)}) collective-permute-start(bf16[896,128]{1,0:T(8,128)(2,1)S(1)} %get-tuple-element.189), channel_id=1, source_target_pairs={{0,8},{4,12},{8,0},{12,4},{16,24},{20,28},{24,16},{28,20},{1,9},{5... | collective-permute-start | bytes 688136 | tf_op jit(solution)/shard_map/ppermute | solution.py:579
  11.0 20.5 %collective-permute-start.8 = (bf16[400,128]{1,0:T(8,128)(2,1)S(1)}, bf16[400,128]{1,0:T(8,128)(2,1)S(1)}, u32[]{:S(2)}, u32[]{:S(2)}) collective-permute-start(bf16[400,128]{1,0:T(8,128)(2,1)S(1)} %get-tuple-element.191), channel_id=1, source_target_pairs={{0,4},{4,0},{8,12},{12,8},{16,20},{20,16},{24,28},{28,24},{1,5},{5... | collective-permute-start | bytes 307208 | tf_op jit(solution)/shard_map/ppermute | solution.py:579
  29.9 21.7 %collective-permute-start.7 = (bf16[3,896,128]{2,1,0:T(8,128)(2,1)S(1)}, bf16[3,896,128]{2,1,0:T(8,128)(2,1)S(1)}, u32[]{:S(2)}, u32[]{:S(2)}) collective-permute-start(bf16[3,896,128]{2,1,0:T(8,128)(2,1)S(1)} %pad_maximum_fusion.3), channel_id=1, source_target_pairs={{0,4},{4,0},{8,12},{12,8},{16,20},{20,16},{24,28},{28,24},{1,5},{5... | collective-permute-start | bytes 2064392 | tf_op jit(solution)/shard_map/ppermute | solution.py:579
  32.2 10.1 %collective-permute-start.9 = (bf16[2,400,128]{2,1,0:T(8,128)(2,1)}, bf16[2,400,128]{2,1,0:T(8,128)(2,1)S(1)}, u32[]{:S(2)}, u32[]{:S(2)}) collective-permute-start(bf16[2,400,128]{2,1,0:T(8,128)(2,1)} %get-tuple-element.201), channel_id=1, source_target_pairs={{0,24},{4,28},{8,16},{12,20},{16,8},{20,12},{24,0},{28,4},{1,25},{... | collective-permute-start | bytes 614408 | tf_op jit(solution)/shard_map/ppermute | solution.py:579
  34.6 15.8 %collective-permute-start.10 = (bf16[2,400,128]{2,1,0:T(8,128)(2,1)}, bf16[2,400,128]{2,1,0:T(8,128)(2,1)S(1)}, u32[]{:S(2)}, u32[]{:S(2)}) collective-permute-start(bf16[2,400,128]{2,1,0:T(8,128)(2,1)} %get-tuple-element.201), channel_id=1, source_target_pairs={{0,16},{4,20},{8,24},{12,28},{16,0},{20,4},{24,8},{28,12},{1,17},{... | collective-permute-start | bytes 614408 | tf_op jit(solution)/shard_map/ppermute | solution.py:579
  34.6 15.8 %collective-permute-start.11 = (bf16[2,400,128]{2,1,0:T(8,128)(2,1)}, bf16[2,400,128]{2,1,0:T(8,128)(2,1)}, u32[]{:S(2)}, u32[]{:S(2)}) collective-permute-start(bf16[2,400,128]{2,1,0:T(8,128)(2,1)} %get-tuple-element.201), channel_id=1, source_target_pairs={{0,8},{4,12},{8,0},{12,4},{16,24},{20,28},{24,16},{28,20},{1,9},{5... | collective-permute-start | bytes 614408 | tf_op jit(solution)/shard_map/ppermute | solution.py:579
  36.5 15.0 %collective-permute-start.6 = (bf16[896,128]{1,0:T(8,128)(2,1)S(1)}, bf16[896,128]{1,0:T(8,128)(2,1)S(1)}, u32[]{:S(2)}, u32[]{:S(2)}) collective-permute-start(bf16[896,128]{1,0:T(8,128)(2,1)S(1)} %get-tuple-element.189), channel_id=1, source_target_pairs={{0,4},{4,0},{8,12},{12,8},{16,20},{20,16},{24,28},{28,24},{1,5},{5... | collective-permute-start | bytes 688136 | tf_op jit(solution)/shard_map/ppermute | solution.py:579
  42.2 48.8 %collective-permute-start.1 = (bf16[4096,256]{1,0:T(8,128)(2,1)}, bf16[4096,256]{1,0:T(8,128)(2,1)}, u32[]{:S(2)}, u32[]{:S(2)}) collective-permute-start(bf16[4096,256]{1,0:T(8,128)(2,1)} %c0.1), channel_id=1, source_target_pairs={{0,2},{1,3},{2,0},{3,1},{4,6},{5,7},{6,4},{7,5},{8,10},{9,11},{10,... | collective-permute-start | bytes 6291464 | tf_op jit(solution)/shard_map/ppermute | solution.py:579
  55.8 6.9 %collective-permute-start.12 = (bf16[352,128]{1,0:T(8,128)(2,1)S(1)}, bf16[352,128]{1,0:T(8,128)(2,1)S(1)}, u32[]{:S(2)}, u32[]{:S(2)}) collective-permute-start(bf16[352,128]{1,0:T(8,128)(2,1)S(1)} %get-tuple-element.205), channel_id=1, source_target_pairs={{0,24},{4,28},{8,16},{12,20},{16,8},{20,12},{24,0},{28,4},{1,25},{... | collective-permute-start | bytes 270344 | tf_op jit(solution)/shard_map/ppermute | solution.py:579
  57.9 6.9 %collective-permute-start.13 = (bf16[352,128]{1,0:T(8,128)(2,1)S(1)}, bf16[352,128]{1,0:T(8,128)(2,1)S(1)}, u32[]{:S(2)}, u32[]{:S(2)}) collective-permute-start(bf16[352,128]{1,0:T(8,128)(2,1)S(1)} %get-tuple-element.205), channel_id=1, source_target_pairs={{0,16},{4,20},{8,24},{12,28},{16,0},{20,4},{24,8},{28,12},{1,17},{... | collective-permute-start | bytes 270344 | tf_op jit(solution)/shard_map/ppermute | solution.py:579
  57.9 4.8 collective-permute-start.17
  61.1 52.4 %collective-permute-start.25 = (bf16[2048,256]{1,0:T(8,128)(2,1)S(1)}, bf16[2048,256]{1,0:T(8,128)(2,1)}, u32[]{:S(2)}, u32[]{:S(2)}) collective-permute-start(bf16[2048,256]{1,0:T(8,128)(2,1)S(1)} %get-tuple-element.151.refs_0_), channel_id=1, source_target_pairs={{0,2},{1,3},{2,0},{3,1},{4,6},{5,7},{6,4},{7,5},{8,10},{9,11},{10,... | collective-permute-start | bytes 3145736 | tf_op jit(solution)/shard_map/ppermute | solution.py:579
  62.7 53.6 %collective-permute-start.24 = (bf16[2048,256]{1,0:T(8,128)(2,1)S(1)}, bf16[2048,256]{1,0:T(8,128)(2,1)}, u32[]{:S(2)}, u32[]{:S(2)}) collective-permute-start(bf16[2048,256]{1,0:T(8,128)(2,1)S(1)} %get-tuple-element.151.refs_0_), channel_id=1, source_target_pairs={{0,1},{1,0},{2,3},{3,2},{4,5},{5,4},{6,7},{7,6},{8,9},{9,8},{10,11... | collective-permute-start | bytes 3145736 | tf_op jit(solution)/shard_map/ppermute | solution.py:579
  62.8 68.1 %collective-permute-start.22 = (bf16[2048,256]{1,0:T(8,128)(2,1)S(1)}, bf16[2048,256]{1,0:T(8,128)(2,1)S(1)}, u32[]{:S(2)}, u32[]{:S(2)}) collective-permute-start(bf16[2048,256]{1,0:T(8,128)(2,1)S(1)} %get-tuple-element.152.refs_0_), channel_id=1, source_target_pairs={{0,2},{1,3},{2,0},{3,1},{4,6},{5,7},{6,4},{7,5},{8,10},{9,11},{10,... | collective-permute-start | bytes 3145736 | tf_op jit(solution)/shard_map/ppermute | solution.py:579
  64.8 4.5 collective-permute-start.14
  69.4 4.5 collective-permute-start.15
  73.9 6.6 %collective-permute-start.18 = (bf16[2,160,128]{2,1,0:T(8,128)(2,1)}, bf16[2,160,128]{2,1,0:T(8,128)(2,1)}, u32[]{:S(2)}, u32[]{:S(2)}) collective-permute-start(bf16[2,160,128]{2,1,0:T(8,128)(2,1)} %get-tuple-element.209), channel_id=1, source_target_pairs={{0,24},{4,28},{8,16},{12,20},{16,8},{20,12},{24,0},{28,4},{1,25},{... | collective-permute-start | bytes 245768 | tf_op jit(solution)/shard_map/ppermute | solution.py:579
  80.4 5.8 %collective-permute-start.19 = (bf16[2,160,128]{2,1,0:T(8,128)(2,1)}, bf16[2,160,128]{2,1,0:T(8,128)(2,1)}, u32[]{:S(2)}, u32[]{:S(2)}) collective-permute-start(bf16[2,160,128]{2,1,0:T(8,128)(2,1)} %get-tuple-element.209), channel_id=1, source_target_pairs={{0,16},{4,20},{8,24},{12,28},{16,0},{20,4},{24,8},{28,12},{1,17},{... | collective-permute-start | bytes 245768 | tf_op jit(solution)/shard_map/ppermute | solution.py:579
  86.2 4.8 collective-permute-start.20
  91.0 112.3 %collective-permute-start = (bf16[4096,256]{1,0:T(8,128)(2,1)}, bf16[4096,256]{1,0:T(8,128)(2,1)}, u32[]{:S(2)}, u32[]{:S(2)}) collective-permute-start(bf16[4096,256]{1,0:T(8,128)(2,1)} %c0.1), channel_id=1, source_target_pairs={{0,1},{1,0},{2,3},{3,2},{4,5},{5,4},{6,7},{7,6},{8,9},{9,8},{10,11... | collective-permute-start | bytes 6291464 | tf_op jit(solution)/shard_map/ppermute | solution.py:579
  91.0 112.3 %collective-permute-start.2 = (bf16[4096,256]{1,0:T(8,128)(2,1)}, bf16[4096,256]{1,0:T(8,128)(2,1)}, u32[]{:S(2)}, u32[]{:S(2)}) collective-permute-start(bf16[4096,256]{1,0:T(8,128)(2,1)} %collective-permute-done.1.c2), channel_id=1, source_target_pairs={{0,1},{1,0},{2,3},{3,2},{4,5},{5,4},{6,7},{7,6},{8,9},{9,8},{10,11... | collective-permute-start | bytes 6291464 | tf_op jit(solution)/shard_map/ppermute | solution.py:579
  113.5 17.3 %collective-permute-start.16 = (bf16[3,352,128]{2,1,0:T(8,128)(2,1)}, bf16[3,352,128]{2,1,0:T(8,128)(2,1)S(1)}, u32[]{:S(2)}, u32[]{:S(2)}) collective-permute-start(bf16[3,352,128]{2,1,0:T(8,128)(2,1)} %pad_maximum_fusion.6), channel_id=1, source_target_pairs={{0,4},{4,0},{8,12},{12,8},{16,20},{20,16},{24,28},{28,24},{1,5},{5... | collective-permute-start | bytes 811016 | tf_op jit(solution)/shard_map/ppermute | solution.py:579
  116.3 55.5 %collective-permute-start.21 = (bf16[2048,256]{1,0:T(8,128)(2,1)S(1)}, bf16[2048,256]{1,0:T(8,128)(2,1)}, u32[]{:S(2)}, u32[]{:S(2)}) collective-permute-start(bf16[2048,256]{1,0:T(8,128)(2,1)S(1)} %get-tuple-element.152.refs_0_), channel_id=1, source_target_pairs={{0,1},{1,0},{2,3},{3,2},{4,5},{5,4},{6,7},{7,6},{8,9},{9,8},{10,11... | collective-permute-start | bytes 3145736 | tf_op jit(solution)/shard_map/ppermute | solution.py:579
  130.8 5.5 %collective-permute-start.26 = (bf16[2048,256]{1,0:T(8,128)(2,1)}, bf16[2048,256]{1,0:T(8,128)(2,1)}, u32[]{:S(2)}, u32[]{:S(2)}) collective-permute-start(bf16[2048,256]{1,0:T(8,128)(2,1)} %collective-permute-done.25.refs_2_), channel_id=1, source_target_pairs={{0,1},{1,0},{2,3},{3,2},{4,5},{5,4},{6,7},{7,6},{8,9},{9,8},{10,11... | collective-permute-start | bytes 3145736 | tf_op jit(solution)/shard_map/ppermute | solution.py:579
  130.9 41.0 %collective-permute-start.23 = (bf16[2048,256]{1,0:T(8,128)(2,1)S(1)}, bf16[2048,256]{1,0:T(8,128)(2,1)}, u32[]{:S(2)}, u32[]{:S(2)}) collective-permute-start(bf16[2048,256]{1,0:T(8,128)(2,1)S(1)} %collective-permute-done.22.refs_2_), channel_id=1, source_target_pairs={{0,1},{1,0},{2,3},{3,2},{4,5},{5,4},{6,7},{7,6},{8,9},{9,8},{10,11... | collective-permute-start | bytes 3145736 | tf_op jit(solution)/shard_map/ppermute | solution.py:579
  171.7 24.9 %collective-permute-start.27 = (f32[1,2048]{1,0:T(1,128)}, f32[1,2048]{1,0:T(1,128)S(1)}, u32[]{:S(2)}, u32[]{:S(2)}) collective-permute-start(f32[1,2048]{1,0:T(1,128)} %get-tuple-element.80), channel_id=1, source_target_pairs={{0,1},{1,0},{2,3},{3,2},{4,5},{5,4},{6,7},{7,6},{8,9},{9,8},{10,11... | collective-permute-start | bytes 24584 | tf_op jit(solution)/shard_map/ppermute | solution.py:579
  195.4 2.8 collective-permute-start.29
  196.6 3.7 collective-permute-start.28
  198.9 3.7 collective-permute-start.30
  240.3 13.1 %collective-permute-start.34 = (f32[1,4096]{1,0:T(1,128)S(1)}, f32[1,4096]{1,0:T(1,128)S(1)}, u32[]{:S(2)}, u32[]{:S(2)}) collective-permute-start(f32[1,4096]{1,0:T(1,128)S(1)} %copy-done.24), channel_id=1, source_target_pairs={{0,1},{1,0},{2,3},{3,2},{4,5},{5,4},{6,7},{7,6},{8,9},{9,8},{10,11... | collective-permute-start | bytes 49160 | tf_op jit(solution)/shard_map/ppermute | solution.py:579
  241.4 132.7 %collective-permute-start.62 = (bf16[2,128,256]{2,1,0:T(8,128)(2,1)}, bf16[2,128,256]{2,1,0:T(8,128)(2,1)S(1)}, u32[]{:S(2)}, u32[]{:S(2)}) collective-permute-start(bf16[2,128,256]{2,1,0:T(8,128)(2,1)} %get-tuple-element.164), channel_id=1, source_target_pairs={{0,24},{4,28},{8,16},{12,20},{16,8},{20,12},{24,0},{28,4},{1,25},{... | collective-permute-start | bytes 393224 | tf_op jit(solution)/shard_map/ppermute | solution.py:579
  252.7 124.8 %collective-permute-start.63 = (bf16[2,128,256]{2,1,0:T(8,128)(2,1)}, bf16[2,128,256]{2,1,0:T(8,128)(2,1)S(1)}, u32[]{:S(2)}, u32[]{:S(2)}) collective-permute-start(bf16[2,128,256]{2,1,0:T(8,128)(2,1)} %get-tuple-element.166), channel_id=1, source_target_pairs={{0,16},{4,20},{8,24},{12,28},{16,0},{20,4},{24,8},{28,12},{1,17},{... | collective-permute-start | bytes 393224 | tf_op jit(solution)/shard_map/ppermute | solution.py:579
  252.7 125.5 %collective-permute-start.64 = (bf16[2,128,256]{2,1,0:T(8,128)(2,1)}, bf16[2,128,256]{2,1,0:T(8,128)(2,1)}, u32[]{:S(2)}, u32[]{:S(2)}) collective-permute-start(bf16[2,128,256]{2,1,0:T(8,128)(2,1)} %get-tuple-element.165), channel_id=1, source_target_pairs={{0,8},{4,12},{8,0},{12,4},{16,24},{20,28},{24,16},{28,20},{1,9},{5... | collective-permute-start | bytes 393224 | tf_op jit(solution)/shard_map/ppermute | solution.py:579
  253.3 3.8 collective-permute-start.35
  329.6 21.9 %collective-permute-start.53 = (f32[4880]{0:T(1024)S(1)}, f32[4880]{0:T(1024)S(1)}, u32[]{:S(2)}, u32[]{:S(2)}) collective-permute-start(f32[4880]{0:T(1024)S(1)} %concatenate.111), channel_id=1, source_target_pairs={{0,4},{4,0},{8,12},{12,8},{16,20},{20,16},{24,28},{28,24},{1,5},{5... | collective-permute-start | bytes 58568 | tf_op jit(solution)/shard_map/ppermute | solution.py:579
  351.5 3.8 collective-permute-start.54
  355.4 14.3 %collective-permute-start.55 = (f32[4880]{0:T(1024)S(1)}, f32[4880]{0:T(1024)S(1)}, u32[]{:S(2)}, u32[]{:S(2)}) collective-permute-start(f32[4880]{0:T(1024)S(1)} %add.311), channel_id=1, source_target_pairs={{0,16},{4,20},{8,24},{12,28},{16,0},{20,4},{24,8},{28,12},{1,17},{... | collective-permute-start | bytes 58568 | tf_op jit(solution)/shard_map/ppermute | solution.py:579
  368.2 17.2 %collective-permute-start.42 = (bf16[2,128,512]{2,1,0:T(8,128)(2,1)}, bf16[2,128,512]{2,1,0:T(8,128)(2,1)}, u32[]{:S(2)}, u32[]{:S(2)}) collective-permute-start(bf16[2,128,512]{2,1,0:T(8,128)(2,1)} %get-tuple-element.148), channel_id=1, source_target_pairs={{0,24},{4,28},{8,16},{12,20},{16,8},{20,12},{24,0},{28,4},{1,25},{... | collective-permute-start | bytes 786440 | tf_op jit(solution)/shard_map/ppermute | solution.py:579
  370.9 21.3 %collective-permute-start.43 = (bf16[2,128,512]{2,1,0:T(8,128)(2,1)}, bf16[2,128,512]{2,1,0:T(8,128)(2,1)}, u32[]{:S(2)}, u32[]{:S(2)}) collective-permute-start(bf16[2,128,512]{2,1,0:T(8,128)(2,1)} %get-tuple-element.150), channel_id=1, source_target_pairs={{0,16},{4,20},{8,24},{12,28},{16,0},{20,4},{24,8},{28,12},{1,17},{... | collective-permute-start | bytes 786440 | tf_op jit(solution)/shard_map/ppermute | solution.py:579
  374.2 18.0 %collective-permute-start.44 = (bf16[2,128,512]{2,1,0:T(8,128)(2,1)}, bf16[2,128,512]{2,1,0:T(8,128)(2,1)}, u32[]{:S(2)}, u32[]{:S(2)}) collective-permute-start(bf16[2,128,512]{2,1,0:T(8,128)(2,1)} %get-tuple-element.149), channel_id=1, source_target_pairs={{0,8},{4,12},{8,0},{12,4},{16,24},{20,28},{24,16},{28,20},{1,9},{5... | collective-permute-start | bytes 786440 | tf_op jit(solution)/shard_map/ppermute | solution.py:579
  377.5 6.2 %collective-permute-start.57 = (f32[1280]{0:T(1024)}, f32[1280]{0:T(1024)}, u32[]{:S(2)}, u32[]{:S(2)}) collective-permute-start(f32[1280]{0:T(1024)} %slice_add_fusion), channel_id=1, source_target_pairs={{0,2},{1,3},{2,0},{3,1},{4,6},{5,7},{6,4},{7,5},{8,10},{9,11},{10,... | collective-permute-start | bytes 15368 | tf_op jit(solution)/shard_map/ppermute | solution.py:579
  379.4 6.0 %collective-permute-start.65 = (bf16[128,256]{1,0:T(8,128)(2,1)S(1)}, bf16[128,256]{1,0:T(8,128)(2,1)S(1)}, u32[]{:S(2)}, u32[]{:S(2)}) collective-permute-start(bf16[128,256]{1,0:T(8,128)(2,1)S(1)} %fusion.35), channel_id=1, source_target_pairs={{0,4},{4,0},{8,12},{12,8},{16,20},{20,16},{24,28},{28,24},{1,5},{5... | collective-permute-start | bytes 196616 | tf_op jit(solution)/shard_map/ppermute | solution.py:579
  383.7 11.6 %collective-permute-start.58 = (bf16[4,128,256]{2,1,0:T(8,128)(2,1)}, bf16[4,128,256]{2,1,0:T(8,128)(2,1)}, u32[]{:S(2)}, u32[]{:S(2)}) collective-permute-start(bf16[4,128,256]{2,1,0:T(8,128)(2,1)} %fusion.12), channel_id=1, source_target_pairs={{0,4},{4,0},{8,12},{12,8},{16,20},{20,16},{24,28},{28,24},{1,5},{5... | collective-permute-start | bytes 786440 | tf_op jit(solution)/shard_map/ppermute | solution.py:579
  385.4 65.8 %collective-permute-start.32 = (bf16[4096,256]{1,0:T(8,128)(2,1)}, bf16[4096,256]{1,0:T(8,128)(2,1)}, u32[]{:S(2)}, u32[]{:S(2)}) collective-permute-start(bf16[4096,256]{1,0:T(8,128)(2,1)} %get-tuple-element.85), channel_id=1, source_target_pairs={{0,1},{1,0},{2,3},{3,2},{4,5},{5,4},{6,7},{7,6},{8,9},{9,8},{10,11... | collective-permute-start | bytes 6291464 | tf_op jit(solution)/shard_map/ppermute | solution.py:579
  385.4 38.5 %collective-permute-start.49 = (bf16[4,128,896]{2,1,0:T(8,128)(2,1)}, bf16[4,128,896]{2,1,0:T(8,128)(2,1)}, u32[]{:S(2)}, u32[]{:S(2)}) collective-permute-start(bf16[4,128,896]{2,1,0:T(8,128)(2,1)} %fusion.4), channel_id=1, source_target_pairs={{0,4},{4,0},{8,12},{12,8},{16,20},{20,16},{24,28},{28,24},{1,5},{5... | collective-permute-start | bytes 2752520 | tf_op jit(solution)/shard_map/ppermute | solution.py:579
  393.5 20.5 %collective-permute-start.45 = (bf16[128,512]{1,0:T(8,128)(2,1)S(1)}, bf16[128,512]{1,0:T(8,128)(2,1)S(1)}, u32[]{:S(2)}, u32[]{:S(2)}) collective-permute-start(bf16[128,512]{1,0:T(8,128)(2,1)S(1)} %fusion.22), channel_id=1, source_target_pairs={{0,4},{4,0},{8,12},{12,8},{16,20},{20,16},{24,28},{28,24},{1,5},{5... | collective-permute-start | bytes 393224 | tf_op jit(solution)/shard_map/ppermute | solution.py:579
  396.4 17.9 %collective-permute-start.59 = (bf16[128,256]{1,0:T(8,128)(2,1)S(1)}, bf16[128,256]{1,0:T(8,128)(2,1)S(1)}, u32[]{:S(2)}, u32[]{:S(2)}) collective-permute-start(bf16[128,256]{1,0:T(8,128)(2,1)S(1)} %get-tuple-element.183), channel_id=1, source_target_pairs={{0,24},{4,28},{8,16},{12,20},{16,8},{20,12},{24,0},{28,4},{1,25},{... | collective-permute-start | bytes 196616 | tf_op jit(solution)/shard_map/ppermute | solution.py:579
  397.8 16.7 %collective-permute-start.60 = (bf16[128,256]{1,0:T(8,128)(2,1)S(1)}, bf16[128,256]{1,0:T(8,128)(2,1)S(1)}, u32[]{:S(2)}, u32[]{:S(2)}) collective-permute-start(bf16[128,256]{1,0:T(8,128)(2,1)S(1)} %get-tuple-element.185), channel_id=1, source_target_pairs={{0,16},{4,20},{8,24},{12,28},{16,0},{20,4},{24,8},{28,12},{1,17},{... | collective-permute-start | bytes 196616 | tf_op jit(solution)/shard_map/ppermute | solution.py:579
  414.0 4.3 collective-permute-start.61
  414.3 12.2 %collective-permute-start.37 = (bf16[2048,256]{1,0:T(8,128)(2,1)}, bf16[2048,256]{1,0:T(8,128)(2,1)S(1)}, u32[]{:S(2)}, u32[]{:S(2)}) collective-permute-start(bf16[2048,256]{1,0:T(8,128)(2,1)} %get-tuple-element.100), channel_id=1, source_target_pairs={{0,1},{1,0},{2,3},{3,2},{4,5},{5,4},{6,7},{7,6},{8,9},{9,8},{10,11... | collective-permute-start | bytes 3145736 | tf_op jit(solution)/shard_map/ppermute | solution.py:579
  414.4 3.9 collective-permute-start.47
  418.4 4.2 collective-permute-start.48
  420.9 83.3 %collective-permute-start.31 = (bf16[4096,256]{1,0:T(8,128)(2,1)}, bf16[4096,256]{1,0:T(8,128)(2,1)S(1)}, u32[]{:S(2)}, u32[]{:S(2)}) collective-permute-start(bf16[4096,256]{1,0:T(8,128)(2,1)} %get-tuple-element.83), channel_id=1, source_target_pairs={{0,1},{1,0},{2,3},{3,2},{4,5},{5,4},{6,7},{7,6},{8,9},{9,8},{10,11... | collective-permute-start | bytes 6291464 | tf_op jit(solution)/shard_map/ppermute | solution.py:579
  422.6 6.0 %collective-permute-start.40 = (bf16[2048,256]{1,0:T(8,128)(2,1)}, bf16[2048,256]{1,0:T(8,128)(2,1)S(1)}, u32[]{:S(2)}, u32[]{:S(2)}) collective-permute-start(bf16[2048,256]{1,0:T(8,128)(2,1)} %get-tuple-element.104), channel_id=1, source_target_pairs={{0,1},{1,0},{2,3},{3,2},{4,5},{5,4},{6,7},{7,6},{8,9},{9,8},{10,11... | collective-permute-start | bytes 3145736 | tf_op jit(solution)/shard_map/ppermute | solution.py:579
  426.0 10.5 %collective-permute-start.50 = (bf16[128,896]{1,0:T(8,128)(2,1)S(1)}, bf16[128,896]{1,0:T(8,128)(2,1)S(1)}, u32[]{:S(2)}, u32[]{:S(2)}) collective-permute-start(bf16[128,896]{1,0:T(8,128)(2,1)S(1)} %get-tuple-element.153), channel_id=1, source_target_pairs={{0,24},{4,28},{8,16},{12,20},{16,8},{20,12},{24,0},{28,4},{1,25},{... | collective-permute-start | bytes 688136 | tf_op jit(solution)/shard_map/ppermute | solution.py:579
  426.5 22.5 %collective-permute-start.51 = (bf16[128,896]{1,0:T(8,128)(2,1)S(1)}, bf16[128,896]{1,0:T(8,128)(2,1)S(1)}, u32[]{:S(2)}, u32[]{:S(2)}) collective-permute-start(bf16[128,896]{1,0:T(8,128)(2,1)S(1)} %get-tuple-element.155), channel_id=1, source_target_pairs={{0,16},{4,20},{8,24},{12,28},{16,0},{20,4},{24,8},{28,12},{1,17},{... | collective-permute-start | bytes 688136 | tf_op jit(solution)/shard_map/ppermute | solution.py:579
  428.6 20.4 %collective-permute-start.52 = (bf16[128,896]{1,0:T(8,128)(2,1)S(1)}, bf16[128,896]{1,0:T(8,128)(2,1)S(1)}, u32[]{:S(2)}, u32[]{:S(2)}) collective-permute-start(bf16[128,896]{1,0:T(8,128)(2,1)S(1)} %get-tuple-element.154), channel_id=1, source_target_pairs={{0,8},{4,12},{8,0},{12,4},{16,24},{20,28},{24,16},{28,20},{1,9},{5... | collective-permute-start | bytes 688136 | tf_op jit(solution)/shard_map/ppermute | solution.py:579
  436.5 17.8 %collective-permute-start.36 = (bf16[2048,256]{1,0:T(8,128)(2,1)S(1)}, bf16[2048,256]{1,0:T(8,128)(2,1)S(1)}, u32[]{:S(2)}, u32[]{:S(2)}) collective-permute-start(bf16[2048,256]{1,0:T(8,128)(2,1)S(1)} %copy-done.36), channel_id=1, source_target_pairs={{0,1},{1,0},{2,3},{3,2},{4,5},{5,4},{6,7},{7,6},{8,9},{9,8},{10,11... | collective-permute-start | bytes 3145736 | tf_op jit(solution)/shard_map/ppermute | solution.py:579
  449.0 26.6 %collective-permute-start.39 = (bf16[2048,256]{1,0:T(8,128)(2,1)S(1)}, bf16[2048,256]{1,0:T(8,128)(2,1)S(1)}, u32[]{:S(2)}, u32[]{:S(2)}) collective-permute-start(bf16[2048,256]{1,0:T(8,128)(2,1)S(1)} %copy-done.35), channel_id=1, source_target_pairs={{0,1},{1,0},{2,3},{3,2},{4,5},{5,4},{6,7},{7,6},{8,9},{9,8},{10,11... | collective-permute-start | bytes 3145736 | tf_op jit(solution)/shard_map/ppermute | solution.py:579
  449.0 26.1 %collective-permute-start.38 = (bf16[2048,256]{1,0:T(8,128)(2,1)S(1)}, bf16[2048,256]{1,0:T(8,128)(2,1)S(1)}, u32[]{:S(2)}, u32[]{:S(2)}) collective-permute-start(bf16[2048,256]{1,0:T(8,128)(2,1)S(1)} %add_convert_fusion.3), channel_id=1, source_target_pairs={{0,2},{1,3},{2,0},{3,1},{4,6},{5,7},{6,4},{7,5},{8,10},{9,11},{10,... | collective-permute-start | bytes 3145736 | tf_op jit(solution)/shard_map/ppermute | solution.py:579
  451.1 46.4 %collective-permute-start.41 = (bf16[2048,256]{1,0:T(8,128)(2,1)S(1)}, bf16[2048,256]{1,0:T(8,128)(2,1)S(1)}, u32[]{:S(2)}, u32[]{:S(2)}) collective-permute-start(bf16[2048,256]{1,0:T(8,128)(2,1)S(1)} %add_convert_fusion.2), channel_id=1, source_target_pairs={{0,2},{1,3},{2,0},{3,1},{4,6},{5,7},{6,4},{7,5},{8,10},{9,11},{10,... | collective-permute-start | bytes 3145736 | tf_op jit(solution)/shard_map/ppermute | solution.py:579
  454.3 87.7 %collective-permute-start.33 = (bf16[4096,256]{1,0:T(8,128)(2,1)S(1)}, bf16[4096,256]{1,0:T(8,128)(2,1)S(1)}, u32[]{:S(2)}, u32[]{:S(2)}) collective-permute-start(bf16[4096,256]{1,0:T(8,128)(2,1)S(1)} %add_convert_fusion.1), channel_id=1, source_target_pairs={{0,2},{1,3},{2,0},{3,1},{4,6},{5,7},{6,4},{7,5},{8,10},{9,11},{10,... | collective-permute-start | bytes 6291464 | tf_op jit(solution)/shard_map/ppermute | solution.py:579
  (39 other events, 817.0 us)
where the time goes:
time: 551 us; the launch traced here: 545 us
  waiting for transfers between devices  215 us (39%)
  Pallas kernels  146 us (26%)
  starting transfers between devices  80.1 us (15%)
  other arithmetic  44 us (8%)
  matrix products  33.7 us (6%)
  local copies, waits for them, and re-layouts  23.5 us (4%)
    ppermute x66, waiting for transfers between devices, exchange(): lax.ppermute(a, axis, [(i, i ^ bit) for i in range(lax.axis_size(axis))])  215 us
    ppermute x66, starting transfers between devices, exchange(): lax.ppermute(a, axis, [(i, i ^ bit) for i in range(lax.axis_size(axis))])  80.1 us
    pallas_call x2, Pallas kernels, run_backward(): pl.pallas_call(functools.partial(backward_kernel, seq=seq, inner=inner, i...  67.6 us
    pallas_call x2, Pallas kernels, run_forward(): pl.pallas_call(functools.partial(forward_kernel, seq=seq, inner=inner, he...  55.4 us
    dot_general x6, matrix products, over_rows(): lax.dot_general(left, right, (((0,), (0,)), ((), ())), preferred_element_...  33.7 us
    pallas_call x1, Pallas kernels, run_middle(): pl.pallas_call(functools.partial(middle_kernel, inner=inner, inner_all=in...  23.1 us
  transfers between devices with their start and end apart: 66, of which 27 were waited for; matrix products, arithmetic and copies ran while one was open for 15% of the time, Pallas kernels for 23%

commit v1 on v0

--- a/solution.py
+++ b/solution.py
@@ -252,8 +252,8 @@
     x_refs, (wt_ref, chan_ref, bcc_ref, headc_ref) = refs[:4], refs[4:8]
     (gate_ref, val_ref, z_ref, y_ref, gno_ref, bc_ref, bcz_ref) = refs[8:15]
     (step_ref, run_ref, state_ref, sq_ref, stat_ref) = refs[15:20]
-    low_ref, g_refs, (chan_acc, bc_acc, head_acc, norm_acc) = refs[20], refs[21:25], refs[25:29]
-    low, gstate, vhead, bhead, dcb, wdec, gudec = refs[29:]
+    low_refs, g_refs, (chan_acc, bc_acc, head_acc, norm_acc) = refs[20:22], refs[22:26], refs[26:30]
+    low, gstate, vhead, bhead, dcb, wdec, gudec = refs[30:]
     step = pl.program_id(0)
     block = blocks - 1 - step
     length = len_ref[seq]
@@ -275,8 +275,7 @@
 
     @pl.when(block * Q >= length)
     def _():
-        low_ref[...] = jnp.zeros_like(low_ref)
-        for ref in g_refs:
+        for ref in (*low_refs, *g_refs):
             ref[...] = jnp.zeros_like(ref)
 
     @pl.when(block * Q < length)
@@ -391,7 +390,9 @@
         low[2 * inner : base, :] = gbc.astype(BF16)
 
         lows = jnp.transpose(low[...])
-        low_ref[...] = lows
+        cut = low_refs[0].shape[1]
+        low_refs[0][...] = lows[:, :cut]
+        low_refs[1][...] = lows[:, cut:]
         g_norm = nn(lows, wt_ref[...])
         gain = gain_row(wt_ref, base, heads)
         xs = [ref[...].astype(F32) for ref in x_refs]
@@ -415,7 +416,7 @@
 
 def params(count):
     return pltpu.CompilerParams(
-        dimension_semantics=("arbitrary",) * count, vmem_limit_bytes=60 << 20
+        dimension_semantics=("arbitrary",) * count, vmem_limit_bytes=44 << 20
     )
 
 
@@ -526,6 +527,8 @@
     col = lambda n: pl.BlockSpec((n, Q), lambda c, lens: (0, at(c)))
     piece = pl.BlockSpec((Q, part), lambda c, lens: (back(c), 0))
     consts = (wt, chan, bcc, headc)
+    cut = inner + inner // 2
+    sets = (cut, wt.shape[0] - cut)
     accs = [(6, inner, HALF), (5, states2, HALF), (2, heads, HALF), (8, width)]
     keep = lambda dims: pl.BlockSpec(dims, lambda c, lens: (0,) * len(dims))
     return pl.pallas_call(
@@ -539,7 +542,7 @@
             blocks=blocks,
         ),
         out_shape=[
-            shape((SEQ_LEN, wt.shape[0]), BF16),
+            *[shape((SEQ_LEN, count), BF16) for count in sets],
             *[shape((SEQ_LEN, part), BF16)] * 4,
             *[shape(dims) for dims in accs],
         ],
@@ -556,7 +559,7 @@
                 *[col(1)] * 2,
             ],
             out_specs=[
-                pl.BlockSpec((Q, wt.shape[0]), lambda c, lens: (back(c), 0)),
+                *[pl.BlockSpec((Q, count), lambda c, lens: (back(c), 0)) for count in sets],
                 *[piece] * 4,
                 *[keep(dims) for dims in accs],
             ],
@@ -615,37 +618,66 @@
     return count // tile * tile
 
 
-def weight_columns(a):
+def side_by_side(pick, extra):
+    _, x = place()
+    out = []
+    for m in range(4):
+        mine, other = pick(m)
+        zero = [jnp.zeros((extra, mine.shape[1]), BF16)] if extra else []
+        for side in (0, 1):
+            out.append(jnp.concatenate([jnp.where(x == side, mine, other)] + zero, 0))
+    return jnp.concatenate(out, 1)
+
+
+def gather_other_way(a):
     tensor = lax.axis_index("tensor")
-    cols = a.shape[0]
+    whole = jnp.transpose(lax.all_gather(jnp.transpose(a), "dp", axis=0, tiled=True))
+    blocks = whole.reshape(a.shape[0], 4, -1)
+    return jnp.concatenate([take(blocks, tensor ^ m, 1) for m in range(4)], 1)
+
+
+def z_stack(a):
+    return jnp.stack([a] + [exchange(a, "dp", 2 * j) for j in (3, 2, 1)])
+
+
+def slot_of(m):
+    z, _ = place()
+    return (4 - ((lax.axis_index("tensor") ^ m) ^ z)) % 4
+
+
+def weight_columns(a, extra, ready):
     if lax.axis_size("dp") != 8:
-        whole = jnp.transpose(lax.all_gather(jnp.transpose(a), "dp", axis=0, tiled=True))
-        blocks = whole.reshape(cols, 4, -1)
-        return jnp.concatenate([take(blocks, tensor ^ m, 1) for m in range(4)], 1)
-    z, x = place()
-    cut = round_to(cols * 7 // 10, 16)
+        return jnp.pad(gather_other_way(a), ((0, extra), (0, 0))), ready
+    cut = round_to(a.shape[0] * 7 // 10, 16)
     first, second = a[:cut], a[cut:]
     beside = exchange(second, "dp", 1)
-    mine = [first] + [exchange(first, "dp", 2 * j) for j in (3, 2, 1)]
-    other = [exchange(first, "dp", 1)]
-    pair = jnp.stack([second, beside])
-    both = jnp.stack([pair] + [exchange(pair, "dp", 2 * j) for j in (3, 2, 1)])
-    mine = jnp.stack(mine)
-    other = jnp.concatenate([other[0][None], exchange(mine[1:], "dp", 1)], 0)
-    out = []
-    for m in range(4):
-        step = (tensor ^ m) ^ z
-        slot = (4 - step) % 4
-        top = [take(mine, slot, 0), take(other, slot, 0)]
+    beside, ready = lax.optimization_barrier((beside, ready))
+    mine = z_stack(first)
+    other = exchange(first, "dp", 1)
+    both = z_stack(jnp.stack([second, beside]))
+    other = jnp.concatenate([other[None], exchange(mine[1:], "dp", 1)], 0)
+
+    def pick(m):
+        slot = slot_of(m)
         low = take(both, slot, 0)
-        for side in (0, 1):
-            own = x == side
-            out.append(
-                jnp.concatenate(
-                    [jnp.where(own, top[0], top[1]), jnp.where(own, low[0], low[1])], 0
-                )
-            )
-    return jnp.concatenate(out, 1)
+        return (
+            jnp.concatenate([take(mine, slot, 0), low[0]], 0),
+            jnp.concatenate([take(other, slot, 0), low[1]], 0),
+        )
+
+    return side_by_side(pick, extra), ready
+
+
+def hidden_columns(a):
+    if lax.axis_size("dp") != 8:
+        return gather_other_way(a)
+    both = z_stack(jnp.stack([a, exchange(a, "dp", 1)]))
+
+    def pick(m):
+        low = take(both, slot_of(m), 0)
+        return low[0], low[1]
+
+    return side_by_side(pick, 0)
 
 
 def along_z(pick):
@@ -656,23 +688,40 @@
     return total
 
 
-def weight_rows(a):
+def reduce_other_way(a):
     tensor = lax.axis_index("tensor")
-    width, cols = a.shape
+    blocks = a.reshape(4, -1, a.shape[1])
+    ordered = jnp.concatenate([take(blocks, tensor ^ m, 0) for m in range(4)], 0)
+    return lax.psum_scatter(ordered, "dp", scatter_dimension=0, tiled=True)
+
+
+def rows_pair_first(a):
     if lax.axis_size("dp") != 8:
-        blocks = a.reshape(4, -1, cols)
-        ordered = jnp.concatenate([take(blocks, tensor ^ m, 0) for m in range(4)], 0)
-        return lax.psum_scatter(ordered, "dp", scatter_dimension=0, tiled=True)
+        return reduce_other_way(a)
+    tensor = lax.axis_index("tensor")
     _, x = place()
-    blocks = a.reshape(4, 2, width // 8, cols)
-    cut = round_to(cols * 2 // 3, HALF)
-    first, second = blocks[..., :cut], blocks[..., cut:]
-    got = exchange(take(first, 1 - x, 1).astype(BF16), "dp", 1).astype(F32)
-    pairs = along_z(lambda z: take(second, z ^ tensor, 0))
-    halves = take(first, x, 1) + got
-    early = along_z(lambda z: take(halves, z ^ tensor, 0))
+    blocks = a.reshape(4, 2, a.shape[0] // 8, a.shape[1])
+    got = exchange(take(blocks, 1 - x, 1).astype(BF16), "dp", 1).astype(F32)
+    halves = take(blocks, x, 1) + got
+    return along_z(lambda z: take(halves, z ^ tensor, 0))
+
+
+def rows_line_first(a):
+    if lax.axis_size("dp") != 8:
+        return reduce_other_way(a)
+    tensor = lax.axis_index("tensor")
+    _, x = place()
+    blocks = a.reshape(4, 2, a.shape[0] // 8, a.shape[1])
+    pairs = along_z(lambda z: take(blocks, z ^ tensor, 0))
     late = exchange(take(pairs, 1 - x, 0).astype(BF16), "dp", 1).astype(F32)
-    return jnp.concatenate([early, take(pairs, x, 0) + late], 1)
+    return take(pairs, x, 0) + late
+
+
+def direct_sum(a, axis, bits):
+    total = a
+    for bit in bits:
+        total = total + exchange(a, axis, bit)
+    return total
 
 
 def over_rows(left, right):
@@ -731,10 +780,12 @@
     )
     xs = [gather_pieces(tokens[q * SEQ_LEN : (q + 1) * SEQ_LEN]) for q in range(seqs)]
     cots = gather_pieces(grad_out)
-    wt = jnp.pad(weight_columns(jnp.transpose(local)), ((0, HALF - 16), (0, 0)))
-    w_out, wt = lax.optimization_barrier((w_out, wt))
-    wo = weight_columns(jnp.transpose(w_out))
-    chan, bcc, headc = small_constants(conv_x, conv_bc, dt_bias, a_log, skip_d, gate_gain)
+    ready = small_constants(conv_x, conv_bc, dt_bias, a_log, skip_d, gate_gain)
+    turned = jnp.transpose(w_out)
+    wt, (turned, *ready) = weight_columns(jnp.transpose(local), HALF - 16, (turned, *ready))
+    turned, wt = lax.optimization_barrier((turned, wt))
+    wo = hidden_columns(turned)
+    chan, bcc, headc = ready
 
     saved, squares = [], []
     for q in range(seqs):
@@ -747,30 +798,37 @@
     g_out = jnp.concatenate([over_rows(cot, nout) for cot in cots], 0)
     branch = reduce_pieces(branch)
     out_rows = (tokens.astype(F32) + branch).astype(BF16)
-    grad_out_rows = weight_rows(g_out)
-
-    grad_rows, accs, g_all = [], None, None
+    grad_out_rows = rows_line_first(g_out)
+
+    grad_rows, accs, sums = [], None, None
     kept = (gate, val, z, y, gno, *shared)
     for q in range(seqs):
-        lows, *rest = run_backward(
+        low_a, low_b, *rest = run_backward(
             q, lengths, xs[q], wt, chan, bcc, headc, kept, squares, stat, inner_all
         )
         gin, here = rest[:4], rest[4:]
         accs = here if accs is None else [a + b for a, b in zip(accs, here)]
         grad_rows.append(reduce_pieces(gin))
-        here = over_rows(normed[q * SEQ_LEN : (q + 1) * SEQ_LEN], lows)
-        g_all = here if g_all is None else g_all + here
+        here = normed[q * SEQ_LEN : (q + 1) * SEQ_LEN]
+        part_b = over_rows(here, low_b)
+        part_a = over_rows(here, low_a)
+        if sums is None:
+            sums = lax.optimization_barrier((part_a, part_b))
+        else:
+            part_b = sums[1] + part_b
+            part_a = sums[0] + part_a
+            sums = (part_a, part_b)
     valid = (jnp.arange(SEQ_LEN)[None] < lengths[:, None]).reshape(rows)[:, None]
     grad_rows = jnp.concatenate(grad_rows, 0) + jnp.where(valid, grad_out.astype(F32), 0.0)
 
     chan_acc, bc_acc, head_acc, norm_acc = accs
-    column = jnp.arange(g_all.shape[1]) == base + heads
-    g_all = jnp.where(column[None], jnp.sum(norm_acc, 0)[:, None], g_all)
-    grads = weight_rows(g_all)
+    cut = sums[0].shape[1]
+    column = jnp.arange(sums[1].shape[1]) == base + heads - cut
+    norm_column = jnp.sum(norm_acc, 0)[:, None]
+    sum_b = jnp.where(column[None], norm_column, sums[1])
+    grads = jnp.concatenate([rows_pair_first(sums[0]), rows_line_first(sum_b)], 1)
     rest = grads[:, 2 * inner :].reshape(tensor_count, -1, states2 + HALF)
-    rest = reduce_pieces(
-        [lax.dynamic_index_in_dim(rest, tensor ^ i, 0, keepdims=False) for i in range(4)], F32
-    )
+    rest = reduce_pieces([take(rest, tensor ^ i, 0) for i in range(4)], F32)
     sizes = [5 * inner, inner, inner, 2 * heads, 5 * states2]
     flat = jnp.concatenate(
         [
@@ -780,10 +838,14 @@
             jnp.sum(bc_acc, -1).reshape(-1),
         ]
     )
-    flat = exchange_sum(flat, "dp")
+    if lax.axis_size("dp") == 8:
+        flat = direct_sum(flat, "dp", (1,))
+        flat = direct_sum(flat, "dp", (2, 4, 6))
+    else:
+        flat = exchange_sum(flat, "dp")
     cuts = [sum(sizes[: i + 1]) for i in range(4)]
     g_conv, g_skip, g_gain, g_head, g_conv_bc = jnp.split(flat, cuts)
-    g_conv_bc = exchange_sum(g_conv_bc, "tensor")
+    g_conv_bc = direct_sum(g_conv_bc, "tensor", (1, 2, 3))
     return (
         out_rows,
         grad_rows,

time: 551 us -> 550 us (level)
  local copies, waits for them, and re-layouts: 23.5 us -> 34.6 us
  Pallas kernels: 146 us -> 139 us
  other arithmetic: 44 us -> 37.6 us
    unnamed x78 -> x144, local copies, waits for them, and re-layouts: 5.51 us -> 18.2 us
    dot_general x6 -> x8, matrix products: 33.7 us -> 37.6 us  [over_rows(): lax.dot_general(left, right, (((0,), (0,)), ((), ())), preferred_element_...]
    ppermute x66 -> x59, starting transfers between devices: 80.1 us -> 76.6 us  [exchange(): lax.ppermute(a, axis, [(i, i ^ bit) for i in range(lax.axis_size(axis))])]
    ppermute x66 -> x59, waiting for transfers between devices: 215 us -> 217 us  [exchange(): lax.ppermute(a, axis, [(i, i ^ bit) for i in range(lax.axis_size(axis))])]
  transfers between devices with their start and end apart: 66 -> 59, of which waited for: 27 -> 24; matrix products, arithmetic and copies ran while one was open for 15% -> 15% of each run, Pallas kernels for 23% -> 9%
where the time goes in v1:
time: 550 us; the launch traced here: 544 us
  waiting for transfers between devices  217 us (39%)
  Pallas kernels  139 us (25%)
  starting transfers between devices  76.6 us (14%)
  other arithmetic  37.6 us (7%)
  matrix products  37.6 us (7%)
  local copies, waits for them, and re-layouts  34.6 us (6%)
    ppermute x59, waiting for transfers between devices, exchange(): lax.ppermute(a, axis, [(i, i ^ bit) for i in range(lax.axis_size(axis))])  217 us
    ppermute x59, starting transfers between devices, exchange(): lax.ppermute(a, axis, [(i, i ^ bit) for i in range(lax.axis_size(axis))])  76.6 us
    pallas_call x2, Pallas kernels, run_backward(): pl.pallas_call(functools.partial(backward_kernel, seq=seq, inner=inner, i...  66.6 us
    pallas_call x2, Pallas kernels, run_forward(): pl.pallas_call(functools.partial(forward_kernel, seq=seq, inner=inner, he...  51.1 us
    dot_general x8, matrix products, over_rows(): lax.dot_general(left, right, (((0,), (0,)), ((), ())), preferred_element_...  37.6 us
    pallas_call x1, Pallas kernels, run_middle(): pl.pallas_call(functools.partial(middle_kernel, inner=inner, inner_all=in...  21 us
    unnamed x144, local copies, waits for them, and re-layouts  18.2 us
  transfers between devices with their start and end apart: 59, of which 24 were waited for; matrix products, arithmetic and copies ran while one was open for 15% of the time, Pallas kernels for 9%

profile of v1, /device:TPU:0, one launch (start us, length us, event | category | flops | bytes accessed | tf_op | source)
XLA Modules:
  0.0 544.3 jit_solution(4237725153189311086)
XLA Ops:
  3.9 1.4 concatenate.79
  6.1 5.1 collective-permute-start.4
  11.7 1.7 collective-permute-start.10
  16.4 1.6 collective-permute-done.4
  18.1 12.9 %collective-permute-done.5 = bf16[896,128]{1,0:T(8,128)(2,1)} collective-permute-done((bf16[896,128]{1,0:T(8,128)(2,1)}, bf16[896,128]{1,0:T(8,128)(2,1)}, u32[]{:S(2)}, u32[]{:S(2)}) %collective-permute-start.5) | collective-permute-done | bytes 229408 | tf_op jit(solution)/shard_map/ppermute | solution.py:582
  31.0 2.1 pad_maximum_fusion.4
  33.1 1.5 collective-permute-start.11
  38.8 2.5 collective-permute-start.7
  41.3 1.9 collective-permute-start.9
  44.7 4.0 collective-permute-done.7
  48.7 1.5 collective-permute-start.20
  50.2 6.7 %collective-permute-done.8 = bf16[2,400,128]{2,1,0:T(8,128)(2,1)S(1)} collective-permute-done((bf16[2,400,128]{2,1,0:T(8,128)(2,1)S(1)}, bf16[2,400,128]{2,1,0:T(8,128)(2,1)S(1)}, u32[]{:S(2)}, u32[]{:S(2)}) %collective-permute-start.8) | collective-permute-done | bytes 204832 | tf_op jit(solution)/shard_map/ppermute | solution.py:582
  56.9 1.5 collective-permute-start.17
  59.2 1.6 fusion.25
  62.4 1.6 copy-done.1
  64.5 4.8 collective-permute-done.12
  70.1 1.5 collective-permute-start.13
  71.5 3.3 collective-permute-done.20.refs_2_
  74.8 3.7 collective-permute-start.14
  80.6 16.7 %collective-permute-done.17.refs_2_ = bf16[2048,256]{1,0:T(8,128)(2,1)} collective-permute-done((bf16[2048,256]{1,0:T(8,128)(2,1)S(1)}, bf16[2048,256]{1,0:T(8,128)(2,1)}, u32[]{:S(2)}, u32[]{:S(2)}) %collective-permute-start.17) | collective-permute-done | bytes 1048608 | tf_op jit(solution)/shard_map/ppermute | solution.py:582
  97.3 39.9 %collective-permute-done.1.c2 = bf16[4096,256]{1,0:T(8,128)(2,1)} collective-permute-done((bf16[4096,256]{1,0:T(8,128)(2,1)}, bf16[4096,256]{1,0:T(8,128)(2,1)}, u32[]{:S(2)}, u32[]{:S(2)}) %collective-permute-start.1) | collective-permute-done | bytes 2097184 | tf_op jit(solution)/shard_map/ppermute | solution.py:582
  141.8 1.6 pad_maximum_fusion.1
  145.9 29.7 %mixer_forward.2 = (bf16[4096,1024]{1,0:T(8,128)(2,1)}, f32[512,4096]{1,0:T(8,128)}, f32[512,4096]{1,0:T(8,128)}, f32[512,4096]{1,0:T(8,128)}, f32[512,4096]{1,0...) custom-call(s32[2]{0:T(128)S(1)} %copy-done.27, ...), custom_call_target="tpu_custom_call" | custom-call | tf_op jit(solution)/shard_map/mixer_forward/pallas_call | solution.py:453
  175.8 21.4 %mixer_forward.3 = (bf16[4096,1024]{1,0:T(8,128)(2,1)}, f32[512,4096]{1,0:T(8,128)}, f32[512,4096]{1,0:T(8,128)}, f32[512,4096]{1,0:T(8,128)}, f32[512,4096]{1,0...) custom-call(s32[2]{0:T(128)S(1)} %copy-done.27, ...), custom_call_target="tpu_custom_call", output_to_operand_aliasing={{0}: (9, {}), {1}: (10, {}), {2}: (11, {}), {3}: (12, {}), ... | custom-call | tf_op jit(solution)/shard_map/mixer_forward/pallas_call | solution.py:453
  197.8 1.6 collective-permute-start.23
  201.5 1.6 collective-permute-done.25
  203.2 21.0 %mixer_middle.1 = (bf16[4096,512]{1,0:T(8,128)(2,1)}, bf16[4096,256]{1,0:T(8,128)(2,1)S(1)}, bf16[4096,256]{1,0:T(8,128)(2,1)S(1)}, bf16[4096,256]{1,0:T(8,128)(...) custom-call(s32[2]{0:T(128)S(1)} %copy-done.28, ...), custom_call_target="tpu_custom_call" | custom-call | tf_op jit(solution)/shard_map/mixer_middle/pallas_call | solution.py:493
  224.2 6.5 %convolution_bitcast_fusion.3 = f32[256,512]{1,0:T(8,128)S(1)} fusion(bf16[4096,512]{1,0:T(8,128)(2,1)} %get-tuple-element.135, bf16[4096,256]{1,0:T(8,128)(2,1)} %c0.1), kind=kOutput, calls=%fused_computation.28 | convolution fusion | flops 1073741824 | bytes 6815744 | tf_op jit(solution)/shard_map/dot_general | solution.py:728
  230.8 2.9 convolution_bitcast_fusion
  233.7 2.9 convolution_bitcast_fusion.1
  236.6 2.9 convolution_bitcast_fusion.2
  242.2 1.4 collective-permute-done.30
  244.9 38.4 %mixer_backward.2 = (bf16[2048,768]{1,0:T(8,128)(2,1)}, bf16[2048,640]{1,0:T(8,128)(2,1)}, bf16[2048,256]{1,0:T(8,128)(2,1)S(1)}, bf16[2048,256]{1,0:T(8,128)(2,...) custom-call(s32[2]{0:T(128)S(1)} %copy-done.29, ...), custom_call_target="tpu_custom_call" | custom-call | tf_op jit(solution)/shard_map/mixer_backward/pallas_call | solution.py:534
  285.3 28.2 %mixer_backward.3 = (bf16[2048,768]{1,0:T(8,128)(2,1)}, bf16[2048,640]{1,0:T(8,128)(2,1)}, bf16[2048,256]{1,0:T(8,128)(2,1)S(1)}, bf16[2048,256]{1,0:T(8,128)(2,...) custom-call(s32[2]{0:T(128)S(1)} %copy-done.29, ...), custom_call_target="tpu_custom_call" | custom-call | tf_op jit(solution)/shard_map/mixer_backward/pallas_call | solution.py:534
  317.0 2.4 add_reduce_fusion
  319.5 6.2 %fusion.4 = f32[1024,640]{1,0:T(8,128)S(1)} fusion(bf16[2048,640]{1,0:T(8,128)(2,1)} %get-tuple-element.123, bf16[4096,1024]{1,0:T(8,128)(2,1)} %get-tuple-element.121), kind=kOutput, calls=%fused_computation.7 | convolution fusion | flops 2684354560 | bytes 9437184 | tf_op jit(solution)/shard_map/dot_general | solution.py:728
  325.8 5.5 %fusion.6 = f32[1024,768]{1,0:T(8,128)S(1)} fusion(bf16[2048,768]{1,0:T(8,128)(2,1)S(1)} %copy-done.61, bf16[4096,1024]{1,0:T(8,128)(2,1)} %get-tuple-element.121), kind=kOutput, calls=%fused_computation.9 | convolution fusion | flops 3221225472 | bytes 10485760 | tf_op jit(solution)/shard_map/dot_general | solution.py:728
  331.3 5.7 %add_select_fusion = f32[1024,640]{1,0:T(8,128)S(1)} fusion(f32[1024,640]{1,0:T(8,128)S(1)} %fusion.4, f32[1024]{0:T(1024)S(1)} %add_reduce_fusion.2, pred[640]{0:T(1024)(128)(4,1)S(1)} %copy-done.63, bf16[2048,640]{1,0:T(8,128)(2,1)S(1)} %copy-done.62, bf16[4096,1024]{1,0:T(8,128)(2,1)} %get-tuple-element.121), kind=kOutput, calls=%fused_computation.11 | convolution fusion | flops 2685665280 | bytes 12063360 | tf_op jit(solution)/shard_map/dot_general | solution.py:728
  337.1 21.9 %collective-permute-start.37 = (bf16[2,128,640]{2,1,0:T(8,128)(2,1)S(1)}, bf16[2,128,640]{2,1,0:T(8,128)(2,1)S(1)}, u32[]{:S(2)}, u32[]{:S(2)}) collective-permute-start(bf16[2,128,640]{2,1,0:T(8,128)(2,1)S(1)} %get-tuple-element.164), channel_id=1, source_target_pairs={{0,24},{4,28},{8,16},{12,20},{16,8},{20,12},{24,0},{28,4},{1,25},{... | collective-permute-start | bytes 983048 | tf_op jit(solution)/shard_map/ppermute | solution.py:582
  359.1 5.2 fusion.8
  365.0 2.4 collective-permute-start.50
  368.7 2.4 fusion.11
  371.1 2.3 collective-permute-done.49
  373.5 2.5 collective-permute-start.39
  375.9 5.8 %collective-permute-done.50 = f32[4880]{0:T(1024)S(1)} collective-permute-done((f32[4880]{0:T(1024)S(1)}, f32[4880]{0:T(1024)S(1)}, u32[]{:S(2)}, u32[]{:S(2)}) %collective-permute-start.50) | collective-permute-done | bytes 19552 | tf_op jit(solution)/shard_map/ppermute | solution.py:582
  386.8 2.8 collective-permute-start.55
  391.1 1.6 collective-permute-start.57
  392.6 1.8 collective-permute-start.44
  395.7 2.6 collective-permute-done.55
  398.2 14.6 %collective-permute-done.56 = bf16[2,128,512]{2,1,0:T(8,128)(2,1)} collective-permute-done((bf16[2,128,512]{2,1,0:T(8,128)(2,1)S(1)}, bf16[2,128,512]{2,1,0:T(8,128)(2,1)}, u32[]{:S(2)}, u32[]{:S(2)}) %collective-permute-start.56) | collective-permute-done | bytes 262176 | tf_op jit(solution)/shard_map/ppermute | solution.py:582
  412.8 1.7 collective-permute-start.40
  416.3 2.7 collective-permute-done.40
  424.6 1.8 bitcast_add_fusion
  426.5 2.7 collective-permute-start.45
  429.2 1.8 collective-permute-start.47
  431.8 4.5 collective-permute-done.45
  437.6 7.8 %collective-permute-done.46 = bf16[128,768]{1,0:T(8,128)(2,1)S(1)} collective-permute-done((bf16[128,768]{1,0:T(8,128)(2,1)S(1)}, bf16[128,768]{1,0:T(8,128)(2,1)S(1)}, u32[]{:S(2)}, u32[]{:S(2)}) %collective-permute-start.46) | collective-permute-done | bytes 196640 | tf_op jit(solution)/shard_map/ppermute | solution.py:582
  446.9 1.7 add_convert_fusion.3
  451.1 2.2 add_convert_fusion.1
  454.5 20.1 %collective-permute-done.33 = bf16[2048,256]{1,0:T(8,128)(2,1)S(1)} collective-permute-done((bf16[2048,256]{1,0:T(8,128)(2,1)S(1)}, bf16[2048,256]{1,0:T(8,128)(2,1)S(1)}, u32[]{:S(2)}, u32[]{:S(2)}) %collective-permute-start.33) | collective-permute-done | bytes 1048608 | tf_op jit(solution)/shard_map/ppermute | solution.py:582
  475.2 22.0 %collective-permute-done.36 = bf16[2048,256]{1,0:T(8,128)(2,1)S(1)} collective-permute-done((bf16[2048,256]{1,0:T(8,128)(2,1)S(1)}, bf16[2048,256]{1,0:T(8,128)(2,1)S(1)}, u32[]{:S(2)}, u32[]{:S(2)}) %collective-permute-start.36) | collective-permute-done | bytes 1048608 | tf_op jit(solution)/shard_map/ppermute | solution.py:582
  497.7 6.2 %maximum_add_fusion = f32[4096,256]{1,0:T(8,128)} fusion(f32[2048,256]{1,0:T(8,128)S(1)} %convert_add_fusion, f32[2048,256]{1,0:T(8,128)S(1)} %convert_add_fusion.1, bf16[4096,256]{1,0:T(8,128)(2,1)} %c0.1, pred[4096]{0:T(1024)(128)(4,1)S(1)} %copy-done.52), kind=kLoop, calls=%fused_computation | loop fusion | flops 4194304 | bytes 10489856 | tf_op jit(solution)/shard_map/add | solution.py:822
  503.9 37.7 %collective-permute-done.28 = bf16[4096,256]{1,0:T(8,128)(2,1)S(1)} collective-permute-done((bf16[4096,256]{1,0:T(8,128)(2,1)S(1)}, bf16[4096,256]{1,0:T(8,128)(2,1)S(1)}, u32[]{:S(2)}, u32[]{:S(2)}) %collective-permute-start.28) | collective-permute-done | bytes 2097184 | tf_op jit(solution)/shard_map/ppermute | solution.py:582
  541.6 2.5 add_convert_fusion
  (303 shorter events, 63.6 us)
Async XLA Ops:
  6.1 12.0 %collective-permute-start.4 = (bf16[896,128]{1,0:T(8,128)(2,1)}, bf16[896,128]{1,0:T(8,128)(2,1)}, u32[]{:S(2)}, u32[]{:S(2)}) collective-permute-start(bf16[896,128]{1,0:T(8,128)(2,1)} %get-tuple-element.202), channel_id=1, source_target_pairs={{0,24},{4,28},{8,16},{12,20},{16,8},{20,12},{24,0},{28,4},{1,25},{... | collective-permute-start | bytes 688136 | tf_op jit(solution)/shard_map/ppermute | solution.py:582
  11.2 19.8 %collective-permute-start.5 = (bf16[896,128]{1,0:T(8,128)(2,1)}, bf16[896,128]{1,0:T(8,128)(2,1)}, u32[]{:S(2)}, u32[]{:S(2)}) collective-permute-start(bf16[896,128]{1,0:T(8,128)(2,1)} %get-tuple-element.202), channel_id=1, source_target_pairs={{0,16},{4,20},{8,24},{12,28},{16,0},{20,4},{24,8},{28,12},{1,17},{... | collective-permute-start | bytes 688136 | tf_op jit(solution)/shard_map/ppermute | solution.py:582
  11.2 19.8 %collective-permute-start.6 = (bf16[896,128]{1,0:T(8,128)(2,1)}, bf16[896,128]{1,0:T(8,128)(2,1)}, u32[]{:S(2)}, u32[]{:S(2)}) collective-permute-start(bf16[896,128]{1,0:T(8,128)(2,1)} %get-tuple-element.202), channel_id=1, source_target_pairs={{0,8},{4,12},{8,0},{12,4},{16,24},{20,28},{24,16},{28,20},{1,9},{5... | collective-permute-start | bytes 688136 | tf_op jit(solution)/shard_map/ppermute | solution.py:582
  11.7 46.9 %collective-permute-start.10 = (bf16[896,128]{1,0:T(8,128)(2,1)}, bf16[896,128]{1,0:T(8,128)(2,1)}, u32[]{:S(2)}, u32[]{:S(2)}) collective-permute-start(bf16[896,128]{1,0:T(8,128)(2,1)} %get-tuple-element.202), channel_id=1, source_target_pairs={{0,4},{4,0},{8,12},{12,8},{16,20},{20,16},{24,28},{28,24},{1,5},{5... | collective-permute-start | bytes 688136 | tf_op jit(solution)/shard_map/ppermute | solution.py:582
  14.1 21.3 %collective-permute-start.3 = (bf16[400,128]{1,0:T(8,128)(2,1)}, bf16[400,128]{1,0:T(8,128)(2,1)S(1)}, u32[]{:S(2)}, u32[]{:S(2)}) collective-permute-start(bf16[400,128]{1,0:T(8,128)(2,1)} %get-tuple-element.204), channel_id=1, source_target_pairs={{0,4},{4,0},{8,12},{12,8},{16,20},{20,16},{24,28},{28,24},{1,5},{5... | collective-permute-start | bytes 307208 | tf_op jit(solution)/shard_map/ppermute | solution.py:582
  33.1 26.1 %collective-permute-start.11 = (bf16[3,896,128]{2,1,0:T(8,128)(2,1)}, bf16[3,896,128]{2,1,0:T(8,128)(2,1)}, u32[]{:S(2)}, u32[]{:S(2)}) collective-permute-start(bf16[3,896,128]{2,1,0:T(8,128)(2,1)} %pad_maximum_fusion.4), channel_id=1, source_target_pairs={{0,4},{4,0},{8,12},{12,8},{16,20},{20,16},{24,28},{28,24},{1,5},{5... | collective-permute-start | bytes 2064392 | tf_op jit(solution)/shard_map/ppermute | solution.py:582
  36.7 166.5 %copy-start = (f32[7,512,128]{2,1,0:T(8,128)}, f32[7,512,128]{2,1,0:T(8,128)S(1)}, u32[]{:S(2)}) copy-start(f32[7,512,128]{2,1,0:T(8,128)S(1)} %broadcast_in_dim.69.refs_5_.chan_ref) | copy-start | bytes 5505028
  37.8 138.0 %copy-start.25 = (f32[2,8,128]{2,1,0:T(8,128)}, f32[2,8,128]{2,1,0:T(8,128)S(1)}, u32[]{:S(2)}) copy-start(f32[2,8,128]{2,1,0:T(8,128)S(1)} %broadcast_in_dim.71.refs_7_) | copy-start | bytes 24580
  38.8 9.9 %collective-permute-start.7 = (bf16[2,400,128]{2,1,0:T(8,128)(2,1)S(1)}, bf16[2,400,128]{2,1,0:T(8,128)(2,1)S(1)}, u32[]{:S(2)}, u32[]{:S(2)}) collective-permute-start(bf16[2,400,128]{2,1,0:T(8,128)(2,1)S(1)} %get-tuple-element.208), channel_id=1, source_target_pairs={{0,24},{4,28},{8,16},{12,20},{16,8},{20,12},{24,0},{28,4},{1,25},{... | collective-permute-start | bytes 614408 | tf_op jit(solution)/shard_map/ppermute | solution.py:582
  41.3 15.6 %collective-permute-start.8 = (bf16[2,400,128]{2,1,0:T(8,128)(2,1)S(1)}, bf16[2,400,128]{2,1,0:T(8,128)(2,1)S(1)}, u32[]{:S(2)}, u32[]{:S(2)}) collective-permute-start(bf16[2,400,128]{2,1,0:T(8,128)(2,1)S(1)} %get-tuple-element.208), channel_id=1, source_target_pairs={{0,16},{4,20},{8,24},{12,28},{16,0},{20,4},{24,8},{28,12},{1,17},{... | collective-permute-start | bytes 614408 | tf_op jit(solution)/shard_map/ppermute | solution.py:582
  41.3 15.6 %collective-permute-start.9 = (bf16[2,400,128]{2,1,0:T(8,128)(2,1)S(1)}, bf16[2,400,128]{2,1,0:T(8,128)(2,1)S(1)}, u32[]{:S(2)}, u32[]{:S(2)}) collective-permute-start(bf16[2,400,128]{2,1,0:T(8,128)(2,1)S(1)} %get-tuple-element.208), channel_id=1, source_target_pairs={{0,8},{4,12},{8,0},{12,4},{16,24},{20,28},{24,16},{28,20},{1,9},{5... | collective-permute-start | bytes 614408 | tf_op jit(solution)/shard_map/ppermute | solution.py:582
  48.7 26.1 %collective-permute-start.20 = (bf16[2048,256]{1,0:T(8,128)(2,1)S(1)}, bf16[2048,256]{1,0:T(8,128)(2,1)}, u32[]{:S(2)}, u32[]{:S(2)}) collective-permute-start(bf16[2048,256]{1,0:T(8,128)(2,1)S(1)} %copy-done.3), channel_id=1, source_target_pairs={{0,2},{1,3},{2,0},{3,1},{4,6},{5,7},{6,4},{7,5},{8,10},{9,11},{10,... | collective-permute-start | bytes 3145736 | tf_op jit(solution)/shard_map/ppermute | solution.py:582
  56.9 21.7 %collective-permute-start.19 = (bf16[2048,256]{1,0:T(8,128)(2,1)S(1)}, bf16[2048,256]{1,0:T(8,128)(2,1)S(1)}, u32[]{:S(2)}, u32[]{:S(2)}) collective-permute-start(bf16[2048,256]{1,0:T(8,128)(2,1)S(1)} %copy-done.3), channel_id=1, source_target_pairs={{0,1},{1,0},{2,3},{3,2},{4,5},{5,4},{6,7},{7,6},{8,9},{9,8},{10,11... | collective-permute-start | bytes 3145736 | tf_op jit(solution)/shard_map/ppermute | solution.py:582
  56.9 40.4 %collective-permute-start.17 = (bf16[2048,256]{1,0:T(8,128)(2,1)S(1)}, bf16[2048,256]{1,0:T(8,128)(2,1)}, u32[]{:S(2)}, u32[]{:S(2)}) collective-permute-start(bf16[2048,256]{1,0:T(8,128)(2,1)S(1)} %get-tuple-element.171.refs_0_), channel_id=1, source_target_pairs={{0,2},{1,3},{2,0},{3,1},{4,6},{5,7},{6,4},{7,5},{8,10},{9,11},{10,... | collective-permute-start | bytes 3145736 | tf_op jit(solution)/shard_map/ppermute | solution.py:582
  58.6 78.6 %collective-permute-start.1 = (bf16[4096,256]{1,0:T(8,128)(2,1)}, bf16[4096,256]{1,0:T(8,128)(2,1)}, u32[]{:S(2)}, u32[]{:S(2)}) collective-permute-start(bf16[4096,256]{1,0:T(8,128)(2,1)} %c0.1), channel_id=1, source_target_pairs={{0,2},{1,3},{2,0},{3,1},{4,6},{5,7},{6,4},{7,5},{8,10},{9,11},{10,... | collective-permute-start | bytes 6291464 | tf_op jit(solution)/shard_map/ppermute | solution.py:582
  61.6 77.6 %copy-start.27 = (s32[2]{0:T(128)S(1)}, s32[2]{0:T(128)}, u32[]{:S(2)}) copy-start(s32[2]{0:T(128)} %len_ref.9) | copy-start | bytes 28
  64.0 5.3 collective-permute-start.12
  70.1 67.1 %collective-permute-start.13 = (bf16[2,512,128]{2,1,0:T(8,128)(2,1)S(1)}, bf16[2,512,128]{2,1,0:T(8,128)(2,1)S(1)}, u32[]{:S(2)}, u32[]{:S(2)}) collective-permute-start(bf16[2,512,128]{2,1,0:T(8,128)(2,1)S(1)} %get-tuple-element.206), channel_id=1, source_target_pairs={{0,24},{4,28},{8,16},{12,20},{16,8},{20,12},{24,0},{28,4},{1,25},{... | collective-permute-start | bytes 786440 | tf_op jit(solution)/shard_map/ppermute | solution.py:582
  74.8 62.9 %collective-permute-start.14 = (bf16[2,512,128]{2,1,0:T(8,128)(2,1)S(1)}, bf16[2,512,128]{2,1,0:T(8,128)(2,1)S(1)}, u32[]{:S(2)}, u32[]{:S(2)}) collective-permute-start(bf16[2,512,128]{2,1,0:T(8,128)(2,1)S(1)} %get-tuple-element.206), channel_id=1, source_target_pairs={{0,16},{4,20},{8,24},{12,28},{16,0},{20,4},{24,8},{28,12},{1,17},{... | collective-permute-start | bytes 786440 | tf_op jit(solution)/shard_map/ppermute | solution.py:582
  79.6 58.3 %collective-permute-start.15 = (bf16[2,512,128]{2,1,0:T(8,128)(2,1)S(1)}, bf16[2,512,128]{2,1,0:T(8,128)(2,1)S(1)}, u32[]{:S(2)}, u32[]{:S(2)}) collective-permute-start(bf16[2,512,128]{2,1,0:T(8,128)(2,1)S(1)} %get-tuple-element.206), channel_id=1, source_target_pairs={{0,8},{4,12},{8,0},{12,4},{16,24},{20,28},{24,16},{28,20},{1,9},{5... | collective-permute-start | bytes 786440 | tf_op jit(solution)/shard_map/ppermute | solution.py:582
  97.3 105.8 %collective-permute-start = (bf16[4096,256]{1,0:T(8,128)(2,1)}, bf16[4096,256]{1,0:T(8,128)(2,1)}, u32[]{:S(2)}, u32[]{:S(2)}) collective-permute-start(bf16[4096,256]{1,0:T(8,128)(2,1)} %c0.1), channel_id=1, source_target_pairs={{0,1},{1,0},{2,3},{3,2},{4,5},{5,4},{6,7},{7,6},{8,9},{9,8},{10,11... | collective-permute-start | bytes 6291464 | tf_op jit(solution)/shard_map/ppermute | solution.py:582
  137.2 65.9 %collective-permute-start.2 = (bf16[4096,256]{1,0:T(8,128)(2,1)}, bf16[4096,256]{1,0:T(8,128)(2,1)}, u32[]{:S(2)}, u32[]{:S(2)}) collective-permute-start(bf16[4096,256]{1,0:T(8,128)(2,1)} %collective-permute-done.1.c2), channel_id=1, source_target_pairs={{0,1},{1,0},{2,3},{3,2},{4,5},{5,4},{6,7},{7,6},{8,9},{9,8},{10,11... | collective-permute-start | bytes 6291464 | tf_op jit(solution)/shard_map/ppermute | solution.py:582
  137.2 38.6 %collective-permute-start.16 = (bf16[2048,256]{1,0:T(8,128)(2,1)S(1)}, bf16[2048,256]{1,0:T(8,128)(2,1)}, u32[]{:S(2)}, u32[]{:S(2)}) collective-permute-start(bf16[2048,256]{1,0:T(8,128)(2,1)S(1)} %get-tuple-element.171.refs_0_), channel_id=1, source_target_pairs={{0,1},{1,0},{2,3},{3,2},{4,5},{5,4},{6,7},{7,6},{8,9},{9,8},{10,11... | collective-permute-start | bytes 3145736 | tf_op jit(solution)/shard_map/ppermute | solution.py:582
  137.7 7.0 %collective-permute-start.21 = (bf16[2048,256]{1,0:T(8,128)(2,1)}, bf16[2048,256]{1,0:T(8,128)(2,1)}, u32[]{:S(2)}, u32[]{:S(2)}) collective-permute-start(bf16[2048,256]{1,0:T(8,128)(2,1)} %collective-permute-done.20.refs_2_), channel_id=1, source_target_pairs={{0,1},{1,0},{2,3},{3,2},{4,5},{5,4},{6,7},{7,6},{8,9},{9,8},{10,11... | collective-permute-start | bytes 3145736 | tf_op jit(solution)/shard_map/ppermute | solution.py:582
  139.1 36.7 %collective-permute-start.18 = (bf16[2048,256]{1,0:T(8,128)(2,1)}, bf16[2048,256]{1,0:T(8,128)(2,1)}, u32[]{:S(2)}, u32[]{:S(2)}) collective-permute-start(bf16[2048,256]{1,0:T(8,128)(2,1)} %collective-permute-done.17.refs_2_), channel_id=1, source_target_pairs={{0,1},{1,0},{2,3},{3,2},{4,5},{5,4},{6,7},{7,6},{8,9},{9,8},{10,11... | collective-permute-start | bytes 3145736 | tf_op jit(solution)/shard_map/ppermute | solution.py:582
  175.7 22.1 %collective-permute-start.22 = (f32[1,2048]{1,0:T(1,128)S(1)}, f32[1,2048]{1,0:T(1,128)S(1)}, u32[]{:S(2)}, u32[]{:S(2)}) collective-permute-start(f32[1,2048]{1,0:T(1,128)S(1)} %get-tuple-element.94), channel_id=1, source_target_pairs={{0,1},{1,0},{2,3},{3,2},{4,5},{5,4},{6,7},{7,6},{8,9},{9,8},{10,11... | collective-permute-start | bytes 24584 | tf_op jit(solution)/shard_map/ppermute | solution.py:582
  197.2 2.1 collective-permute-start.24
  197.8 3.7 collective-permute-start.23
  199.4 3.7 collective-permute-start.25
  230.7 9.0 %collective-permute-start.29 = (f32[1,4096]{1,0:T(1,128)S(1)}, f32[1,4096]{1,0:T(1,128)S(1)}, u32[]{:S(2)}, u32[]{:S(2)}) collective-permute-start(f32[1,4096]{1,0:T(1,128)S(1)} %get-tuple-element.110), channel_id=1, source_target_pairs={{0,1},{1,0},{2,3},{3,2},{4,5},{5,4},{6,7},{7,6},{8,9},{9,8},{10,11... | collective-permute-start | bytes 49160 | tf_op jit(solution)/shard_map/ppermute | solution.py:582
  239.8 3.8 collective-permute-start.30
  319.5 44.8 %collective-permute-start.48 = (f32[4880]{0:T(1024)S(1)}, f32[4880]{0:T(1024)S(1)}, u32[]{:S(2)}, u32[]{:S(2)}) collective-permute-start(f32[4880]{0:T(1024)S(1)} %concatenate.103), channel_id=1, source_target_pairs={{0,4},{4,0},{8,12},{12,8},{16,20},{20,16},{24,28},{28,24},{1,5},{5... | collective-permute-start | bytes 58568 | tf_op jit(solution)/shard_map/ppermute | solution.py:582
  337.1 53.9 %collective-permute-start.37 = (bf16[2,128,640]{2,1,0:T(8,128)(2,1)S(1)}, bf16[2,128,640]{2,1,0:T(8,128)(2,1)S(1)}, u32[]{:S(2)}, u32[]{:S(2)}) collective-permute-start(bf16[2,128,640]{2,1,0:T(8,128)(2,1)S(1)} %get-tuple-element.164), channel_id=1, source_target_pairs={{0,24},{4,28},{8,16},{12,20},{16,8},{20,12},{24,0},{28,4},{1,25},{... | collective-permute-start | bytes 983048 | tf_op jit(solution)/shard_map/ppermute | solution.py:582
  359.0 33.6 %collective-permute-start.38 = (bf16[2,128,640]{2,1,0:T(8,128)(2,1)S(1)}, bf16[2,128,640]{2,1,0:T(8,128)(2,1)S(1)}, u32[]{:S(2)}, u32[]{:S(2)}) collective-permute-start(bf16[2,128,640]{2,1,0:T(8,128)(2,1)S(1)} %get-tuple-element.166), channel_id=1, source_target_pairs={{0,16},{4,20},{8,24},{12,28},{16,0},{20,4},{24,8},{28,12},{1,17},{... | collective-permute-start | bytes 983048 | tf_op jit(solution)/shard_map/ppermute | solution.py:582
  364.3 9.2 %collective-permute-start.49 = (f32[4880]{0:T(1024)S(1)}, f32[4880]{0:T(1024)S(1)}, u32[]{:S(2)}, u32[]{:S(2)}) collective-permute-start(f32[4880]{0:T(1024)S(1)} %add.306), channel_id=1, source_target_pairs={{0,8},{4,12},{8,0},{12,4},{16,24},{20,28},{24,16},{28,20},{1,9},{5... | collective-permute-start | bytes 58568 | tf_op jit(solution)/shard_map/ppermute | solution.py:582
  365.0 16.8 %collective-permute-start.50 = (f32[4880]{0:T(1024)S(1)}, f32[4880]{0:T(1024)S(1)}, u32[]{:S(2)}, u32[]{:S(2)}) collective-permute-start(f32[4880]{0:T(1024)S(1)} %add.306), channel_id=1, source_target_pairs={{0,16},{4,20},{8,24},{12,28},{16,0},{20,4},{24,8},{28,12},{1,17},{... | collective-permute-start | bytes 58568 | tf_op jit(solution)/shard_map/ppermute | solution.py:582
  367.3 14.4 %collective-permute-start.51 = (f32[4880]{0:T(1024)S(1)}, f32[4880]{0:T(1024)S(1)}, u32[]{:S(2)}, u32[]{:S(2)}) collective-permute-start(f32[4880]{0:T(1024)S(1)} %add.306), channel_id=1, source_target_pairs={{0,24},{4,28},{8,16},{12,20},{16,8},{20,12},{24,0},{28,4},{1,25},{... | collective-permute-start | bytes 58568 | tf_op jit(solution)/shard_map/ppermute | solution.py:582
  373.5 19.2 %collective-permute-start.39 = (bf16[2,128,640]{2,1,0:T(8,128)(2,1)S(1)}, bf16[2,128,640]{2,1,0:T(8,128)(2,1)S(1)}, u32[]{:S(2)}, u32[]{:S(2)}) collective-permute-start(bf16[2,128,640]{2,1,0:T(8,128)(2,1)S(1)} %get-tuple-element.165), channel_id=1, source_target_pairs={{0,8},{4,12},{8,0},{12,4},{16,24},{20,28},{24,16},{28,20},{1,9},{5... | collective-permute-start | bytes 983048 | tf_op jit(solution)/shard_map/ppermute | solution.py:582
  382.4 1.4 collective-permute-start.52
  382.4 4.4 collective-permute-start.53
  383.8 5.8 %collective-permute-start.54 = (f32[1280]{0:T(1024)}, f32[1280]{0:T(1024)}, u32[]{:S(2)}, u32[]{:S(2)}) collective-permute-start(f32[1280]{0:T(1024)} %split.18), channel_id=1, source_target_pairs={{0,3},{1,2},{2,1},{3,0},{4,7},{5,6},{6,5},{7,4},{8,11},{9,10},{10,... | collective-permute-start | bytes 15368 | tf_op jit(solution)/shard_map/ppermute | solution.py:582
  386.8 11.4 %collective-permute-start.55 = (bf16[2,128,512]{2,1,0:T(8,128)(2,1)}, bf16[2,128,512]{2,1,0:T(8,128)(2,1)}, u32[]{:S(2)}, u32[]{:S(2)}) collective-permute-start(bf16[2,128,512]{2,1,0:T(8,128)(2,1)} %get-tuple-element.167), channel_id=1, source_target_pairs={{0,24},{4,28},{8,16},{12,20},{16,8},{20,12},{24,0},{28,4},{1,25},{... | collective-permute-start | bytes 786440 | tf_op jit(solution)/shard_map/ppermute | solution.py:582
  389.6 23.2 %collective-permute-start.56 = (bf16[2,128,512]{2,1,0:T(8,128)(2,1)S(1)}, bf16[2,128,512]{2,1,0:T(8,128)(2,1)}, u32[]{:S(2)}, u32[]{:S(2)}) collective-permute-start(bf16[2,128,512]{2,1,0:T(8,128)(2,1)S(1)} %copy-done.45), channel_id=1, source_target_pairs={{0,16},{4,20},{8,24},{12,28},{16,0},{20,4},{24,8},{28,12},{1,17},{... | collective-permute-start | bytes 786440 | tf_op jit(solution)/shard_map/ppermute | solution.py:582
  391.1 23.5 %collective-permute-start.57 = (bf16[2,128,512]{2,1,0:T(8,128)(2,1)S(1)}, bf16[2,128,512]{2,1,0:T(8,128)(2,1)S(1)}, u32[]{:S(2)}, u32[]{:S(2)}) collective-permute-start(bf16[2,128,512]{2,1,0:T(8,128)(2,1)S(1)} %copy-done.44), channel_id=1, source_target_pairs={{0,8},{4,12},{8,0},{12,4},{16,24},{20,28},{24,16},{28,20},{1,9},{5... | collective-permute-start | bytes 786440 | tf_op jit(solution)/shard_map/ppermute | solution.py:582
  392.6 57.5 %collective-permute-start.27 = (bf16[4096,256]{1,0:T(8,128)(2,1)}, bf16[4096,256]{1,0:T(8,128)(2,1)}, u32[]{:S(2)}, u32[]{:S(2)}) collective-permute-start(bf16[4096,256]{1,0:T(8,128)(2,1)} %get-tuple-element.99), channel_id=1, source_target_pairs={{0,1},{1,0},{2,3},{3,2},{4,5},{5,4},{6,7},{7,6},{8,9},{9,8},{10,11... | collective-permute-start | bytes 6291464 | tf_op jit(solution)/shard_map/ppermute | solution.py:582
  392.6 31.9 %collective-permute-start.44 = (bf16[4,128,768]{2,1,0:T(8,128)(2,1)}, bf16[4,128,768]{2,1,0:T(8,128)(2,1)}, u32[]{:S(2)}, u32[]{:S(2)}) collective-permute-start(bf16[4,128,768]{2,1,0:T(8,128)(2,1)} %fusion.11), channel_id=1, source_target_pairs={{0,4},{4,0},{8,12},{12,8},{16,20},{20,16},{24,28},{28,24},{1,5},{5... | collective-permute-start | bytes 2359304 | tf_op jit(solution)/shard_map/ppermute | solution.py:582
  398.2 48.6 %collective-permute-start.32 = (bf16[2048,256]{1,0:T(8,128)(2,1)}, bf16[2048,256]{1,0:T(8,128)(2,1)}, u32[]{:S(2)}, u32[]{:S(2)}) collective-permute-start(bf16[2048,256]{1,0:T(8,128)(2,1)} %get-tuple-element.114), channel_id=1, source_target_pairs={{0,1},{1,0},{2,3},{3,2},{4,5},{5,4},{6,7},{7,6},{8,9},{9,8},{10,11... | collective-permute-start | bytes 3145736 | tf_op jit(solution)/shard_map/ppermute | solution.py:582
  412.8 6.2 %collective-permute-start.40 = (bf16[128,640]{1,0:T(8,128)(2,1)S(1)}, bf16[128,640]{1,0:T(8,128)(2,1)S(1)}, u32[]{:S(2)}, u32[]{:S(2)}) collective-permute-start(bf16[128,640]{1,0:T(8,128)(2,1)S(1)} %fusion.35), channel_id=1, source_target_pairs={{0,4},{4,0},{8,12},{12,8},{16,20},{20,16},{24,28},{28,24},{1,5},{5... | collective-permute-start | bytes 491528 | tf_op jit(solution)/shard_map/ppermute | solution.py:582
  415.9 5.3 collective-permute-start.58
  419.8 2.9 collective-permute-start.42
  422.0 7.2 %collective-permute-start.41 = (f32[32,384]{1,0:T(8,128)}, f32[32,384]{1,0:T(8,128)}, u32[]{:S(2)}, u32[]{:S(2)}) collective-permute-start(f32[32,384]{1,0:T(8,128)} %get-tuple-element.209), channel_id=1, source_target_pairs={{0,1},{1,0},{2,3},{3,2},{4,5},{5,4},{6,7},{7,6},{8,9},{9,8},{10,11... | collective-permute-start | bytes 147464 | tf_op jit(solution)/shard_map/ppermute | solution.py:582
  423.7 5.5 %collective-permute-start.43 = (f32[32,384]{1,0:T(8,128)S(1)}, f32[32,384]{1,0:T(8,128)S(1)}, u32[]{:S(2)}, u32[]{:S(2)}) collective-permute-start(f32[32,384]{1,0:T(8,128)S(1)} %bitcast_add_fusion.6), channel_id=1, source_target_pairs={{0,2},{1,3},{2,0},{3,1},{4,6},{5,7},{6,4},{7,5},{8,10},{9,11},{10,... | collective-permute-start | bytes 147464 | tf_op jit(solution)/shard_map/ppermute | solution.py:582
  426.5 9.8 %collective-permute-start.45 = (bf16[128,768]{1,0:T(8,128)(2,1)S(1)}, bf16[128,768]{1,0:T(8,128)(2,1)S(1)}, u32[]{:S(2)}, u32[]{:S(2)}) collective-permute-start(bf16[128,768]{1,0:T(8,128)(2,1)S(1)} %get-tuple-element.172), channel_id=1, source_target_pairs={{0,24},{4,28},{8,16},{12,20},{16,8},{20,12},{24,0},{28,4},{1,25},{... | collective-permute-start | bytes 589832 | tf_op jit(solution)/shard_map/ppermute | solution.py:582
  429.2 16.2 %collective-permute-start.46 = (bf16[128,768]{1,0:T(8,128)(2,1)S(1)}, bf16[128,768]{1,0:T(8,128)(2,1)S(1)}, u32[]{:S(2)}, u32[]{:S(2)}) collective-permute-start(bf16[128,768]{1,0:T(8,128)(2,1)S(1)} %get-tuple-element.174), channel_id=1, source_target_pairs={{0,16},{4,20},{8,24},{12,28},{16,0},{20,4},{24,8},{28,12},{1,17},{... | collective-permute-start | bytes 589832 | tf_op jit(solution)/shard_map/ppermute | solution.py:582
  429.2 16.2 %collective-permute-start.47 = (bf16[128,768]{1,0:T(8,128)(2,1)S(1)}, bf16[128,768]{1,0:T(8,128)(2,1)S(1)}, u32[]{:S(2)}, u32[]{:S(2)}) collective-permute-start(bf16[128,768]{1,0:T(8,128)(2,1)S(1)} %get-tuple-element.173), channel_id=1, source_target_pairs={{0,8},{4,12},{8,0},{12,4},{16,24},{20,28},{24,16},{28,20},{1,9},{5... | collective-permute-start | bytes 589832 | tf_op jit(solution)/shard_map/ppermute | solution.py:582
  436.2 12.3 %collective-permute-start.35 = (bf16[2048,256]{1,0:T(8,128)(2,1)S(1)}, bf16[2048,256]{1,0:T(8,128)(2,1)S(1)}, u32[]{:S(2)}, u32[]{:S(2)}) collective-permute-start(bf16[2048,256]{1,0:T(8,128)(2,1)S(1)} %copy-done.37), channel_id=1, source_target_pairs={{0,1},{1,0},{2,3},{3,2},{4,5},{5,4},{6,7},{7,6},{8,9},{9,8},{10,11... | collective-permute-start | bytes 3145736 | tf_op jit(solution)/shard_map/ppermute | solution.py:582
  445.3 58.6 %collective-permute-start.26 = (bf16[4096,256]{1,0:T(8,128)(2,1)S(1)}, bf16[4096,256]{1,0:T(8,128)(2,1)S(1)}, u32[]{:S(2)}, u32[]{:S(2)}) collective-permute-start(bf16[4096,256]{1,0:T(8,128)(2,1)S(1)} %copy-done.31), channel_id=1, source_target_pairs={{0,1},{1,0},{2,3},{3,2},{4,5},{5,4},{6,7},{7,6},{8,9},{9,8},{10,11... | collective-permute-start | bytes 6291464 | tf_op jit(solution)/shard_map/ppermute | solution.py:582
  445.4 7.9 %collective-permute-start.31 = (bf16[2048,256]{1,0:T(8,128)(2,1)S(1)}, bf16[2048,256]{1,0:T(8,128)(2,1)S(1)}, u32[]{:S(2)}, u32[]{:S(2)}) collective-permute-start(bf16[2048,256]{1,0:T(8,128)(2,1)S(1)} %copy-done.35), channel_id=1, source_target_pairs={{0,1},{1,0},{2,3},{3,2},{4,5},{5,4},{6,7},{7,6},{8,9},{9,8},{10,11... | collective-permute-start | bytes 3145736 | tf_op jit(solution)/shard_map/ppermute | solution.py:582
  446.9 28.3 %collective-permute-start.34 = (bf16[2048,256]{1,0:T(8,128)(2,1)S(1)}, bf16[2048,256]{1,0:T(8,128)(2,1)S(1)}, u32[]{:S(2)}, u32[]{:S(2)}) collective-permute-start(bf16[2048,256]{1,0:T(8,128)(2,1)S(1)} %copy-done.33), channel_id=1, source_target_pairs={{0,1},{1,0},{2,3},{3,2},{4,5},{5,4},{6,7},{7,6},{8,9},{9,8},{10,11... | collective-permute-start | bytes 3145736 | tf_op jit(solution)/shard_map/ppermute | solution.py:582
  448.6 26.1 %collective-permute-start.33 = (bf16[2048,256]{1,0:T(8,128)(2,1)S(1)}, bf16[2048,256]{1,0:T(8,128)(2,1)S(1)}, u32[]{:S(2)}, u32[]{:S(2)}) collective-permute-start(bf16[2048,256]{1,0:T(8,128)(2,1)S(1)} %add_convert_fusion.3), channel_id=1, source_target_pairs={{0,2},{1,3},{2,0},{3,1},{4,6},{5,7},{6,4},{7,5},{8,10},{9,11},{10,... | collective-permute-start | bytes 3145736 | tf_op jit(solution)/shard_map/ppermute | solution.py:582
  450.2 47.0 %collective-permute-start.36 = (bf16[2048,256]{1,0:T(8,128)(2,1)S(1)}, bf16[2048,256]{1,0:T(8,128)(2,1)S(1)}, u32[]{:S(2)}, u32[]{:S(2)}) collective-permute-start(bf16[2048,256]{1,0:T(8,128)(2,1)S(1)} %add_convert_fusion.2), channel_id=1, source_target_pairs={{0,2},{1,3},{2,0},{3,1},{4,6},{5,7},{6,4},{7,5},{8,10},{9,11},{10,... | collective-permute-start | bytes 3145736 | tf_op jit(solution)/shard_map/ppermute | solution.py:582
  453.3 88.3 %collective-permute-start.28 = (bf16[4096,256]{1,0:T(8,128)(2,1)S(1)}, bf16[4096,256]{1,0:T(8,128)(2,1)S(1)}, u32[]{:S(2)}, u32[]{:S(2)}) collective-permute-start(bf16[4096,256]{1,0:T(8,128)(2,1)S(1)} %add_convert_fusion.1), channel_id=1, source_target_pairs={{0,2},{1,3},{2,0},{3,1},{4,6},{5,7},{6,4},{7,5},{8,10},{9,11},{10,... | collective-permute-start | bytes 6291464 | tf_op jit(solution)/shard_map/ppermute | solution.py:582
  497.6 44.0 %copy-start.10 = (bf16[4096,256]{1,0:T(8,128)(2,1)S(1)}, bf16[4096,256]{1,0:T(8,128)(2,1)}, u32[]{:S(2)}) copy-start(bf16[4096,256]{1,0:T(8,128)(2,1)} %copy-done.9) | copy-start | bytes 6291460
  497.6 44.0 %copy-start.39 = (bf16[4096,256]{1,0:T(8,128)(2,1)S(1)}, bf16[4096,256]{1,0:T(8,128)(2,1)}, u32[]{:S(2)}) copy-start(bf16[4096,256]{1,0:T(8,128)(2,1)} %param.15) | copy-start | bytes 6291460
  (61 other events, 631.9 us)

commit v2 on v1

--- a/solution.py
+++ b/solution.py
@@ -93,9 +93,10 @@
     b_low = (b_time - b_high.astype(F32)).astype(BF16)
     c_high = c_rows.astype(BF16)
     c_low = (c_rows - c_high.astype(F32)).astype(BF16)
-    return nn(
+    full = nn(
         jnp.concatenate([b_high, b_low, b_high], 1), jnp.concatenate([c_high, c_high, c_low], 0)
     )
+    return (full[:HALF, :HALF], full[:HALF, HALF:], full[HALF:, HALF:]), b_high
 
 
 def rms_scale(xs, width):
@@ -127,7 +128,7 @@
     x_refs, (wt_ref, chan_ref, bcc_ref, headc_ref) = refs[:4], refs[4:8]
     refs = refs[8 + aliased :]
     (norm_ref, gate_ref, val_ref, z_ref, y_ref, m_ref, bc_ref, bcz_ref) = refs[:8]
-    (step_ref, run_ref, state_ref, stat_ref, proj, vtail, btail, state) = refs[8:]
+    (step_ref, run_ref, state_ref, stat_ref, proj, vtail, btail, state, carried, wdec) = refs[8:]
     block = pl.program_id(0)
     length = len_ref[seq]
     per = inner // heads
@@ -163,9 +164,8 @@
         bcz_ref[...] = bcz
         shared = bcz * jax.nn.sigmoid(bcz)
         b_rows, c_rows = shared[:states], shared[states:]
-        cb = intersection(b_rows, c_rows)
-        cb_blocks = (cb[:HALF, :HALF], cb[:HALF, HALF:], cb[HALF:, HALF:])
-        b_low, c_low = b_rows.astype(BF16), c_rows.astype(BF16)
+        cb_blocks, b_time = intersection(b_rows, c_rows)
+        c_low = c_rows.astype(BF16)
 
         step_raw = proj[base : base + heads, :] + twice(headc_ref[0])
         step_ref[...] = step_raw
@@ -180,6 +180,7 @@
         upper = upper_half()
 
         state_ref[...] = state[...]
+        carried[...] = nn(state[...].astype(BF16), c_low)
         squares = jnp.zeros((1, Q), F32)
         for h in range(heads):
             rows = slice(h * per, (h + 1) * per)
@@ -194,27 +195,28 @@
             w = v * steps[h : h + 1]
             decays = decay_blocks(running[h : h + 1], run_cols[:, h : h + 1], upper)
             grid = stack_blocks(*[(d * g).astype(BF16) for d, g in zip(decays, cb_blocks)])
-            old = state[rows, :]
-            y = nn(w.astype(BF16), grid) + nn(old.astype(BF16), c_low) * grow[h : h + 1]
+            y = nn(w.astype(BF16), grid) + carried[rows, :] * grow[h : h + 1]
             y_ref[rows, :] = y
-            fresh = nt((w * to_end[h : h + 1]).astype(BF16), b_low)
-            state[rows, :] = old * whole[h : h + 1] + fresh
+            wdec[rows, :] = (w * to_end[h : h + 1]).astype(BF16)
             u = y + twice(chan_ref[6, rows, :]) * v
             m = u * gate * jax.nn.sigmoid(gate)
             m_ref[rows, :] = m
             squares = squares + jnp.sum(m * m, 0, keepdims=True)
         stat_ref[...] = squares
-
-
-def middle_kernel(
-    len_ref, c0, c1, c2, c3, wo_ref, chan_ref, m_ref, sq_ref,
-    nout_ref, b0, b1, b2, b3, gno_ref, stat_ref, gain_acc, nout, *, inner, inner_all, width,
-):
-    seq, block = pl.program_id(0), pl.program_id(1)
+        fresh = nn(wdec[...], b_time)
+        for h in range(heads):
+            rows = slice(h * per, (h + 1) * per)
+            state[rows, :] = state[rows, :] * whole[h : h + 1] + fresh[rows]
+
+
+def middle_kernel(len_ref, *refs, seq, inner, inner_all, width, aliased):
+    c0, c1, c2, c3, wo_ref, chan_ref, m_ref, sq_ref = refs[:8]
+    nout_ref, b0, b1, b2, b3, gno_ref, stat_ref, gain_acc, nout = refs[8 + aliased :]
+    block = pl.program_id(0)
     length = len_ref[seq]
     part = width // 4
 
-    @pl.when((seq == 0) & (block == 0))
+    @pl.when(block == 0)
     def _():
         gain_acc[...] = jnp.zeros_like(gain_acc)
 
@@ -253,7 +255,7 @@
     (gate_ref, val_ref, z_ref, y_ref, gno_ref, bc_ref, bcz_ref) = refs[8:15]
     (step_ref, run_ref, state_ref, sq_ref, stat_ref) = refs[15:20]
     low_refs, g_refs, (chan_acc, bc_acc, head_acc, norm_acc) = refs[20:22], refs[22:26], refs[26:30]
-    low, gstate, vhead, bhead, dcb, wdec, gudec = refs[30:]
+    low, gstate, vhead, bhead, dcb, wdec, gudec, sent = refs[30:]
     step = pl.program_id(0)
     block = blocks - 1 - step
     length = len_ref[seq]
@@ -288,8 +290,7 @@
         shared = bcz * sig
         shared_slope = sig * (1.0 + bcz * (1.0 - sig))
         b_rows, c_rows = shared[:states], shared[states:]
-        cb = intersection(b_rows, c_rows)
-        cb_blocks = (cb[:HALF, :HALF], cb[:HALF, HALF:], cb[HALF:, HALF:])
+        cb_blocks, _ = intersection(b_rows, c_rows)
         b_low, c_low = b_rows.astype(BF16), c_rows.astype(BF16)
 
         step_raw = step_ref[...]
@@ -302,6 +303,7 @@
         whole = jnp.exp(ends)
         upper = upper_half()
 
+        sent[...] = nn(gstate[...].astype(BF16), b_low)
         direct, both, after, through = [], [], [], []
         for h in range(heads):
             rows = slice(h * per, (h + 1) * per)
@@ -331,8 +333,7 @@
                 else:
                     dcb[i] += decays[i] * pieces[i]
             gs = gstate[rows, :]
-            gs_low = gs.astype(BF16)
-            gw_out = nn(gs_low, b_low) * to_end[h : h + 1]
+            gw_out = sent[rows, :] * to_end[h : h + 1]
             gw = gw_in + gw_out
             direct.append(jnp.sum(gw * v, 0, keepdims=True))
             both.append(
@@ -376,7 +377,7 @@
         gs_old = gstate[...]
         g_c = nn(b_low, dcb_low) + nn(jnp.transpose(state_ref[...]).astype(BF16), gud)
         g_b = nt(c_low, dcb_low) + nn(jnp.transpose(gs_old).astype(BF16), wd)
-        fresh = nt(gud, c_low)
+        fresh = nn(gud, jnp.transpose(c_low))
         for h in range(heads):
             rows = slice(h * per, (h + 1) * per)
             gstate[rows, :] = gs_old[rows] * whole[h : h + 1] + fresh[rows]
@@ -474,6 +475,8 @@
                 pltpu.VMEM((inner, HALF), F32),
                 pltpu.VMEM((states2, HALF), F32),
                 pltpu.VMEM((inner, states2 // 2), F32),
+                pltpu.VMEM((inner, Q), F32),
+                pltpu.VMEM((inner, Q), BF16),
             ],
         ),
         input_output_aliases={9 + i: i for i in range(len(before))},
@@ -482,39 +485,55 @@
     )(lengths, *xs, *consts, *before)
 
 
-def run_middle(lengths, cots, wo, chan, m, squares, inner_all):
+def run_middle(seq, lengths, cots, wo, chan, m, squares, inner_all, before):
     rows, part = cots[0].shape
     width = 4 * part
     inner = wo.shape[0]
     blocks = SEQ_LEN // Q
-    at = lambda q, c: q * blocks + c
-    piece = pl.BlockSpec((Q, part), lambda q, c, lens: (at(q, c), 0))
-    col = lambda n: pl.BlockSpec((n, Q), lambda q, c, lens: (0, at(q, c)))
+    at = lambda c: seq * blocks + c
+    piece = pl.BlockSpec((Q, part), lambda c, lens: (at(c), 0))
+    col = pl.BlockSpec((inner, Q), lambda c, lens: (0, at(c)))
+    stat = pl.BlockSpec((1, Q), lambda c, lens: (0, c))
     return pl.pallas_call(
-        functools.partial(middle_kernel, inner=inner, inner_all=inner_all, width=width),
+        functools.partial(
+            middle_kernel,
+            seq=seq,
+            inner=inner,
+            inner_all=inner_all,
+            width=width,
+            aliased=len(before),
+        ),
         out_shape=[
             shape((rows, inner), BF16),
             *[shape((rows, part), BF16)] * 4,
             shape((inner, rows)),
-            shape((1, rows)),
+            shape((1, SEQ_LEN)),
             shape((inner, HALF)),
         ],
         grid_spec=pltpu.PrefetchScalarGridSpec(
             num_scalar_prefetch=1,
-            grid=(rows // SEQ_LEN, blocks),
-            in_specs=[*[piece] * 4, fixed(wo), fixed(chan), col(inner), col(1)],
+            grid=(blocks,),
+            in_specs=[
+                *[piece] * 4,
+                fixed(wo),
+                fixed(chan),
+                col,
+                stat,
+                *[pl.BlockSpec(memory_space=pl.ANY)] * len(before),
+            ],
             out_specs=[
-                pl.BlockSpec((Q, inner), lambda q, c, lens: (at(q, c), 0)),
+                pl.BlockSpec((Q, inner), lambda c, lens: (at(c), 0)),
                 *[piece] * 4,
-                col(inner),
-                col(1),
-                pl.BlockSpec((inner, HALF), lambda q, c, lens: (0, 0)),
+                col,
+                stat,
+                pl.BlockSpec((inner, HALF), lambda c, lens: (0, 0)),
             ],
             scratch_shapes=[pltpu.VMEM((inner, Q), BF16)],
         ),
-        compiler_params=params(2),
+        input_output_aliases={9 + i: i for i in range(len(before))},
+        compiler_params=params(1),
         name="mixer_middle",
-    )(lengths, *cots, wo, chan, m, squares)
+    )(lengths, *cots, wo, chan, m, squares, *before)
 
 
 def run_backward(seq, lengths, xs, wt, chan, bcc, headc, saved, squares, stat, inner_all):
@@ -556,7 +575,7 @@
                 *[col(states2)] * 2,
                 *[col(heads)] * 2,
                 pl.BlockSpec((inner, states2 // 2), lambda c, lens: (at(c), 0)),
-                *[col(1)] * 2,
+                *[pl.BlockSpec((1, Q), lambda c, lens: (0, back(c)))] * 2,
             ],
             out_specs=[
                 *[pl.BlockSpec((Q, count), lambda c, lens: (back(c), 0)) for count in sets],
@@ -571,6 +590,7 @@
                 pltpu.VMEM((3, HALF, HALF), F32),
                 pltpu.VMEM((inner, Q), BF16),
                 pltpu.VMEM((inner, Q), BF16),
+                pltpu.VMEM((inner, Q), F32),
             ],
         ),
         compiler_params=params(1),
@@ -601,8 +621,8 @@
     got_corner = exchange(corner.astype(kind), "tensor", 1)
     got_beside = exchange(beside.astype(kind), "tensor", 1)
     onward = (across.astype(F32) + got_corner.astype(F32)).astype(kind)
-    here = own.astype(F32) + got_beside.astype(F32)
-    return here + exchange(onward, "tensor", 2).astype(F32)
+    last = exchange(onward, "tensor", 2).astype(F32)
+    return own.astype(F32) + got_beside.astype(F32) + last
 
 
 def place():
@@ -636,25 +656,48 @@
     return jnp.concatenate([take(blocks, tensor ^ m, 1) for m in range(4)], 1)
 
 
+ROUNDS = ((3, 2, 1), (1, 3, 2))
+
+
+def exchange_z(a, turn):
+    count, tensor_count = lax.axis_size("dp"), lax.axis_size("tensor")
+    pairs = [
+        (d * tensor_count + t, (d ^ (2 * ROUNDS[t % 2][turn])) * tensor_count + t)
+        for d in range(count)
+        for t in range(tensor_count)
+    ]
+    return lax.ppermute(a, ("dp", "tensor"), pairs)
+
+
+def even_core():
+    return lax.axis_index("tensor") % 2 == 0
+
+
+def distance(turn):
+    return jnp.where(even_core(), ROUNDS[0][turn], ROUNDS[1][turn])
+
+
 def z_stack(a):
-    return jnp.stack([a] + [exchange(a, "dp", 2 * j) for j in (3, 2, 1)])
+    return jnp.stack([a] + [exchange_z(a, turn) for turn in range(3)])
 
 
 def slot_of(m):
     z, _ = place()
-    return (4 - ((lax.axis_index("tensor") ^ m) ^ z)) % 4
+    j = (lax.axis_index("tensor") ^ m) ^ z
+    return jnp.where(even_core(), (4 - j) % 4, jnp.where(j >= 2, 5 - j, j))
 
 
 def weight_columns(a, extra, ready):
     if lax.axis_size("dp") != 8:
         return jnp.pad(gather_other_way(a), ((0, extra), (0, 0))), ready
-    cut = round_to(a.shape[0] * 7 // 10, 16)
+    cut = round_to(a.shape[0] * 6 // 10, 16)
     first, second = a[:cut], a[cut:]
     beside = exchange(second, "dp", 1)
     beside, ready = lax.optimization_barrier((beside, ready))
     mine = z_stack(first)
     other = exchange(first, "dp", 1)
-    both = z_stack(jnp.stack([second, beside]))
+    pair = jnp.stack([second, beside])
+    both = z_stack(pair)
     other = jnp.concatenate([other[None], exchange(mine[1:], "dp", 1)], 0)
 
     def pick(m):
@@ -683,8 +726,9 @@
 def along_z(pick):
     z, _ = place()
     total = pick(z)
-    for j in (3, 2, 1):
-        total = total + exchange(pick(z ^ j).astype(BF16), "dp", 2 * j).astype(F32)
+    for turn in range(3):
+        send = pick(z ^ distance(turn)).astype(BF16)
+        total = total + exchange_z(send, turn).astype(F32)
     return total
 
 
@@ -781,20 +825,25 @@
     xs = [gather_pieces(tokens[q * SEQ_LEN : (q + 1) * SEQ_LEN]) for q in range(seqs)]
     cots = gather_pieces(grad_out)
     ready = small_constants(conv_x, conv_bc, dt_bias, a_log, skip_d, gate_gain)
-    turned = jnp.transpose(w_out)
-    wt, (turned, *ready) = weight_columns(jnp.transpose(local), HALF - 16, (turned, *ready))
-    turned, wt = lax.optimization_barrier((turned, wt))
+    wt, (turned, *ready) = weight_columns(
+        jnp.transpose(local), HALF - 16, (jnp.transpose(w_out), *ready)
+    )
     wo = hidden_columns(turned)
     chan, bcc, headc = ready
 
     saved, squares = [], []
     for q in range(seqs):
         *saved, here = run_forward(q, seqs, lengths, xs[q], wt, chan, bcc, headc, saved)
-        squares.append(exchange_sum(here, "tensor"))
-    squares = jnp.concatenate(squares, 1)
+        squares.append(direct_sum(here, "tensor", (1, 2, 3)))
     normed, gate, val, z, y, m, *shared = saved
-    nout, *branch, gno, stat, gain_acc = run_middle(lengths, cots, wo, chan, m, squares, inner_all)
-    stat = exchange_sum(stat, "tensor")
+    middle, stats, gain_acc = [], [], None
+    for q in range(seqs):
+        *middle, stat, here = run_middle(
+            q, lengths, cots, wo, chan, m, squares[q], inner_all, middle
+        )
+        stats.append(direct_sum(stat, "tensor", (1, 2, 3)))
+        gain_acc = here if gain_acc is None else gain_acc + here
+    nout, *branch, gno = middle
     g_out = jnp.concatenate([over_rows(cot, nout) for cot in cots], 0)
     branch = reduce_pieces(branch)
     out_rows = (tokens.astype(F32) + branch).astype(BF16)
@@ -804,7 +853,7 @@
     kept = (gate, val, z, y, gno, *shared)
     for q in range(seqs):
         low_a, low_b, *rest = run_backward(
-            q, lengths, xs[q], wt, chan, bcc, headc, kept, squares, stat, inner_all
+            q, lengths, xs[q], wt, chan, bcc, headc, kept, squares[q], stats[q], inner_all
         )
         gin, here = rest[:4], rest[4:]
         accs = here if accs is None else [a + b for a, b in zip(accs, here)]

time: 550 us -> 554 us (level)
  starting transfers between devices: 76.6 us -> 94.7 us
  other arithmetic: 37.6 us -> 29.1 us
    ppermute x0 -> x18, starting transfers between devices: none -> 61.6 us  [exchange_z(): return lax.ppermute(a, ('dp', 'tensor'), pairs)]
    ppermute x0 -> x18, waiting for transfers between devices: none -> 51.6 us  [exchange_z(): return lax.ppermute(a, ('dp', 'tensor'), pairs)]
    ppermute x59 -> x47, waiting for transfers between devices: 217 us -> 169 us  [exchange(): lax.ppermute(a, axis, [(i, i ^ bit) for i in range(lax.axis_size(axis))])]
    ppermute x59 -> x47, starting transfers between devices: 76.6 us -> 33.1 us  [exchange(): lax.ppermute(a, axis, [(i, i ^ bit) for i in range(lax.axis_size(axis))])]
    pallas_call x1 -> x2, Pallas kernels: 21 us -> 22.6 us  [run_middle(): pl.pallas_call(functools.partial(middle_kernel, seq=seq, inner=inner, inn...]
    unnamed x144 -> x120, local copies, waits for them, and re-layouts: 18.2 us -> 16.9 us
  transfers between devices with their start and end apart: 59 -> 65, of which waited for: 24 -> 22; matrix products, arithmetic and copies ran while one was open for 15% -> 13% of each run, Pallas kernels for 9% -> 11%
where the time goes in v2:
time: 554 us; the launch traced here: 549 us
  waiting for transfers between devices  221 us (40%)
  Pallas kernels  137 us (25%)
  starting transfers between devices  94.7 us (17%)
  matrix products  33 us (6%)
  local copies, waits for them, and re-layouts  32 us (6%)
  other arithmetic  29.1 us (5%)
    ppermute x47, waiting for transfers between devices, exchange(): lax.ppermute(a, axis, [(i, i ^ bit) for i in range(lax.axis_size(axis))])  169 us
    pallas_call x2, Pallas kernels, run_backward(): pl.pallas_call(functools.partial(backward_kernel, seq=seq, inner=inner, i...  65.9 us
    ppermute x18, starting transfers between devices, exchange_z(): return lax.ppermute(a, ('dp', 'tensor'), pairs)  61.6 us
    ppermute x18, waiting for transfers between devices, exchange_z(): return lax.ppermute(a, ('dp', 'tensor'), pairs)  51.6 us
    pallas_call x2, Pallas kernels, run_forward(): pl.pallas_call(functools.partial(forward_kernel, seq=seq, inner=inner, he...  48.6 us
    ppermute x47, starting transfers between devices, exchange(): lax.ppermute(a, axis, [(i, i ^ bit) for i in range(lax.axis_size(axis))])  33.1 us
    dot_general x8, matrix products, over_rows(): lax.dot_general(left, right, (((0,), (0,)), ((), ())), preferred_element_...  33 us
    pallas_call x2, Pallas kernels, run_middle(): pl.pallas_call(functools.partial(middle_kernel, seq=seq, inner=inner, inn...  22.6 us
  transfers between devices with their start and end apart: 65, of which 22 were waited for; matrix products, arithmetic and copies ran while one was open for 13% of the time, Pallas kernels for 11%

profile of v2, /device:TPU:0, one launch (start us, length us, event | category | flops | bytes accessed | tf_op | source)
XLA Modules:
  0.0 548.6 jit_solution(300930396919156174)
XLA Ops:
  3.7 1.4 concatenate.76
  5.2 5.1 collective-permute-start.11
  11.0 1.6 collective-permute-start.17
  15.7 1.7 fusion.41
  24.2 3.8 collective-permute-start.14
  28.7 1.6 collective-permute-start.4
  30.6 3.1 collective-permute-done.4
  33.7 1.6 collective-permute-start.20
  35.5 14.8 %collective-permute-start.6 = (bf16[2,512,128]{2,1,0:T(8,128)(2,1)S(1)}, bf16[2,512,128]{2,1,0:T(8,128)(2,1)S(1)}, u32[]{:S(2)}, u32[]{:S(2)}) collective-permute-start(bf16[2,512,128]{2,1,0:T(8,128)(2,1)S(1)} %get-tuple-element.220), channel_id=1, source_target_pairs={{0,16},{1,25},{2,18},{3,27},{4,20},{5,29},{6,22},{7,31},{8,24},{9,... | collective-permute-start | bytes 786440 | tf_op jit(solution)/shard_map/ppermute | solution.py:669
  50.3 9.9 %collective-permute-done.15 = bf16[2,528,128]{2,1,0:T(8,128)(2,1)S(1)} collective-permute-done((bf16[2,528,128]{2,1,0:T(8,128)(2,1)S(1)}, bf16[2,528,128]{2,1,0:T(8,128)(2,1)S(1)}, u32[]{:S(2)}, u32[]{:S(2)}) %collective-permute-start.15) | collective-permute-done | bytes 270368 | tf_op jit(solution)/shard_map/ppermute | solution.py:669
  60.3 2.4 collective-permute-start.5
  62.9 3.1 collective-permute-done.6
  66.0 9.2 %collective-permute-done.7 = bf16[2,512,128]{2,1,0:T(8,128)(2,1)S(1)} collective-permute-done((bf16[2,512,128]{2,1,0:T(8,128)(2,1)S(1)}, bf16[2,512,128]{2,1,0:T(8,128)(2,1)S(1)}, u32[]{:S(2)}, u32[]{:S(2)}) %collective-permute-start.7) | collective-permute-done | bytes 262176 | tf_op jit(solution)/shard_map/ppermute | solution.py:669
  75.2 1.5 collective-permute-start.1
  76.7 1.5 collective-permute-start.18
  79.4 10.3 %collective-permute-done.18 = bf16[3,768,128]{2,1,0:T(8,128)(2,1)S(1)} collective-permute-done((bf16[3,768,128]{2,1,0:T(8,128)(2,1)S(1)}, bf16[3,768,128]{2,1,0:T(8,128)(2,1)S(1)}, u32[]{:S(2)}, u32[]{:S(2)}) %collective-permute-start.18) | collective-permute-done | bytes 589856 | tf_op jit(solution)/shard_map/ppermute | solution.py:602
  91.6 51.6 %collective-permute-done.9.refs_2_ = bf16[2048,256]{1,0:T(8,128)(2,1)S(1)} collective-permute-done((bf16[2048,256]{1,0:T(8,128)(2,1)S(1)}, bf16[2048,256]{1,0:T(8,128)(2,1)S(1)}, u32[]{:S(2)}, u32[]{:S(2)}) %collective-permute-start.9) | collective-permute-done | bytes 1048608 | tf_op jit(solution)/shard_map/ppermute | solution.py:602
  144.4 28.5 %mixer_forward.2 = (bf16[4096,1024]{1,0:T(8,128)(2,1)}, f32[512,4096]{1,0:T(8,128)}, f32[512,4096]{1,0:T(8,128)}, f32[512,4096]{1,0:T(8,128)}, f32[512,4096]{1,0...) custom-call(s32[2]{0:T(128)S(1)} %copy-done.24, ...), custom_call_target="tpu_custom_call" | custom-call | tf_op jit(solution)/shard_map/mixer_forward/pallas_call | solution.py:454
  173.1 1.5 collective-permute-start.26
  174.9 20.1 %mixer_forward.3 = (bf16[4096,1024]{1,0:T(8,128)(2,1)}, f32[512,4096]{1,0:T(8,128)}, f32[512,4096]{1,0:T(8,128)}, f32[512,4096]{1,0:T(8,128)}, f32[512,4096]{1,0...) custom-call(s32[2]{0:T(128)S(1)} %copy-done.24, ...), custom_call_target="tpu_custom_call", output_to_operand_aliasing={{0}: (9, {}), {1}: (10, {}), {2}: (11, {}), {3}: (12, {}), ... | custom-call | tf_op jit(solution)/shard_map/mixer_forward/pallas_call | solution.py:454
  195.5 1.5 collective-permute-start.23
  197.1 2.1 collective-permute-done.23
  200.2 11.8 %mixer_middle.2 = (bf16[4096,512]{1,0:T(8,128)(2,1)}, bf16[4096,256]{1,0:T(8,128)(2,1)S(1)}, bf16[4096,256]{1,0:T(8,128)(2,1)S(1)}, bf16[4096,256]{1,0:T(8,128)(...) custom-call(s32[2]{0:T(128)S(1)} %copy-done.24, ...), custom_call_target="tpu_custom_call" | custom-call | tf_op jit(solution)/shard_map/mixer_middle/pallas_call | solution.py:497
  212.0 1.4 copy-done.4
  215.3 1.6 copy-done.5
  216.9 10.8 %mixer_middle.3 = (bf16[4096,512]{1,0:T(8,128)(2,1)}, bf16[4096,256]{1,0:T(8,128)(2,1)S(1)}, bf16[4096,256]{1,0:T(8,128)(2,1)S(1)}, bf16[4096,256]{1,0:T(8,128)(...) custom-call(s32[2]{0:T(128)S(1)} %copy-done.24, ...), custom_call_target="tpu_custom_call", output_to_operand_aliasing={{0}: (9, {}), {1}: (10, {}), {2}: (11, {}), {3}: (12, {}), ... | custom-call | tf_op jit(solution)/shard_map/mixer_middle/pallas_call | solution.py:497
  228.8 4.6 convolution_bitcast_fusion.3
  233.4 3.0 convolution_bitcast_fusion
  237.8 2.9 convolution_bitcast_fusion.2
  242.6 2.5 collective-permute-done.39
  245.2 38.2 %mixer_backward.2 = (bf16[2048,768]{1,0:T(8,128)(2,1)}, bf16[2048,640]{1,0:T(8,128)(2,1)}, bf16[2048,256]{1,0:T(8,128)(2,1)S(1)}, bf16[2048,256]{1,0:T(8,128)(2,...) custom-call(s32[2]{0:T(128)S(1)} %copy-done.24, ...), custom_call_target="tpu_custom_call" | custom-call | tf_op jit(solution)/shard_map/mixer_backward/pallas_call | solution.py:553
  287.4 27.7 %mixer_backward.3 = (bf16[2048,768]{1,0:T(8,128)(2,1)}, bf16[2048,640]{1,0:T(8,128)(2,1)}, bf16[2048,256]{1,0:T(8,128)(2,1)S(1)}, bf16[2048,256]{1,0:T(8,128)(2,...) custom-call(s32[2]{0:T(128)S(1)} %copy-done.24, ...), custom_call_target="tpu_custom_call" | custom-call | tf_op jit(solution)/shard_map/mixer_backward/pallas_call | solution.py:553
  318.5 2.4 add_reduce_fusion
  321.0 6.2 %fusion.4 = f32[1024,640]{1,0:T(8,128)S(1)} fusion(bf16[2048,640]{1,0:T(8,128)(2,1)} %get-tuple-element.134, bf16[4096,1024]{1,0:T(8,128)(2,1)} %get-tuple-element.132), kind=kOutput, calls=%fused_computation.7 | convolution fusion | flops 2684354560 | bytes 9437184 | tf_op jit(solution)/shard_map/dot_general | solution.py:772
  327.3 5.5 %fusion.6 = f32[1024,768]{1,0:T(8,128)S(1)} fusion(bf16[2048,768]{1,0:T(8,128)(2,1)S(1)} %copy-done.49, bf16[4096,1024]{1,0:T(8,128)(2,1)} %get-tuple-element.132), kind=kOutput, calls=%fused_computation.9 | convolution fusion | flops 3221225472 | bytes 10485760 | tf_op jit(solution)/shard_map/dot_general | solution.py:772
  332.8 5.7 %add_select_fusion = f32[1024,640]{1,0:T(8,128)S(1)} fusion(f32[1024,640]{1,0:T(8,128)S(1)} %fusion.4, f32[1024]{0:T(1024)S(1)} %add_reduce_fusion.3, pred[640]{0:T(1024)(128)(4,1)S(1)} %copy-done.51, bf16[2048,640]{1,0:T(8,128)(2,1)S(1)} %copy-done.50, bf16[4096,1024]{1,0:T(8,128)(2,1)} %get-tuple-element.132), kind=kOutput, calls=%fused_computation.11 | convolution fusion | flops 2685665280 | bytes 12063360 | tf_op jit(solution)/shard_map/dot_general | solution.py:772
  339.6 23.1 %collective-permute-start.43 = (bf16[2,128,640]{2,1,0:T(8,128)(2,1)}, bf16[2,128,640]{2,1,0:T(8,128)(2,1)S(1)}, u32[]{:S(2)}, u32[]{:S(2)}) collective-permute-start(bf16[2,128,640]{2,1,0:T(8,128)(2,1)} %get-tuple-element.176), channel_id=1, source_target_pairs={{0,24},{1,9},{2,26},{3,11},{4,28},{5,13},{6,30},{7,15},{8,16},{9,1... | collective-permute-start | bytes 983048 | tf_op jit(solution)/shard_map/ppermute | solution.py:669
  362.8 3.7 fusion.8
  367.1 2.4 collective-permute-start.56
  369.6 1.4 collective-permute-start.57
  372.0 3.0 collective-permute-done.55
  374.9 2.5 collective-permute-start.45
  377.4 10.9 %collective-permute-done.56 = f32[4880]{0:T(1024)S(1)} collective-permute-done((f32[4880]{0:T(1024)S(1)}, f32[4880]{0:T(1024)S(1)}, u32[]{:S(2)}, u32[]{:S(2)}) %collective-permute-start.56) | collective-permute-done | bytes 19552 | tf_op jit(solution)/shard_map/ppermute | solution.py:602
  393.7 1.5 collective-permute-start.62
  395.9 1.9 collective-permute-start.63
  397.9 2.1 collective-permute-start.50
  401.2 3.0 collective-permute-done.61
  404.2 15.2 %collective-permute-done.62 = bf16[2,128,512]{2,1,0:T(8,128)(2,1)} collective-permute-done((bf16[2,128,512]{2,1,0:T(8,128)(2,1)}, bf16[2,128,512]{2,1,0:T(8,128)(2,1)}, u32[]{:S(2)}, u32[]{:S(2)}) %collective-permute-start.62) | collective-permute-done | bytes 262176 | tf_op jit(solution)/shard_map/ppermute | solution.py:669
  419.4 2.0 collective-permute-start.46
  422.9 2.8 collective-permute-done.46
  426.4 1.4 collective-permute-done.64
  430.8 2.1 bitcast_add_fusion
  433.0 1.5 collective-permute-start.51
  434.5 2.9 collective-permute-start.53
  438.3 4.4 collective-permute-done.51
  444.1 6.3 %collective-permute-done.52 = bf16[128,768]{1,0:T(8,128)(2,1)S(1)} collective-permute-done((bf16[128,768]{1,0:T(8,128)(2,1)S(1)}, bf16[128,768]{1,0:T(8,128)(2,1)S(1)}, u32[]{:S(2)}, u32[]{:S(2)}) %collective-permute-start.52) | collective-permute-done | bytes 196640 | tf_op jit(solution)/shard_map/ppermute | solution.py:669
  452.8 1.4 collective-permute-start.36
  455.4 2.2 add_convert_fusion.1
  457.6 1.4 collective-permute-start.30
  459.0 19.9 %collective-permute-done.36 = bf16[2048,256]{1,0:T(8,128)(2,1)S(1)} collective-permute-done((bf16[2048,256]{1,0:T(8,128)(2,1)S(1)}, bf16[2048,256]{1,0:T(8,128)(2,1)S(1)}, u32[]{:S(2)}, u32[]{:S(2)}) %collective-permute-start.36) | collective-permute-done | bytes 1048608 | tf_op jit(solution)/shard_map/ppermute | solution.py:602
  479.4 22.0 %collective-permute-done.42 = bf16[2048,256]{1,0:T(8,128)(2,1)S(1)} collective-permute-done((bf16[2048,256]{1,0:T(8,128)(2,1)S(1)}, bf16[2048,256]{1,0:T(8,128)(2,1)S(1)}, u32[]{:S(2)}, u32[]{:S(2)}) %collective-permute-start.42) | collective-permute-done | bytes 1048608 | tf_op jit(solution)/shard_map/ppermute | solution.py:602
  503.0 4.5 maximum_add_fusion
  507.5 38.3 %collective-permute-done.30 = bf16[4096,256]{1,0:T(8,128)(2,1)S(1)} collective-permute-done((bf16[4096,256]{1,0:T(8,128)(2,1)S(1)}, bf16[4096,256]{1,0:T(8,128)(2,1)S(1)}, u32[]{:S(2)}, u32[]{:S(2)}) %collective-permute-start.30) | collective-permute-done | bytes 2097184 | tf_op jit(solution)/shard_map/ppermute | solution.py:602
  545.8 2.5 add_convert_fusion
  (289 shorter events, 57.6 us)
Async XLA Ops:
  5.2 22.8 %collective-permute-start.11 = (bf16[768,128]{1,0:T(8,128)(2,1)S(1)}, bf16[768,128]{1,0:T(8,128)(2,1)S(1)}, u32[]{:S(2)}, u32[]{:S(2)}) collective-permute-start(bf16[768,128]{1,0:T(8,128)(2,1)S(1)} %get-tuple-element.214), channel_id=1, source_target_pairs={{0,24},{1,9},{2,26},{3,11},{4,28},{5,13},{6,30},{7,15},{8,16},{9,1... | collective-permute-start | bytes 589832 | tf_op jit(solution)/shard_map/ppermute | solution.py:669
  10.3 17.9 %collective-permute-start.12 = (bf16[768,128]{1,0:T(8,128)(2,1)S(1)}, bf16[768,128]{1,0:T(8,128)(2,1)S(1)}, u32[]{:S(2)}, u32[]{:S(2)}) collective-permute-start(bf16[768,128]{1,0:T(8,128)(2,1)S(1)} %get-tuple-element.214), channel_id=1, source_target_pairs={{0,16},{1,25},{2,18},{3,27},{4,20},{5,29},{6,22},{7,31},{8,24},{9,... | collective-permute-start | bytes 589832 | tf_op jit(solution)/shard_map/ppermute | solution.py:669
  10.3 18.3 %collective-permute-start.13 = (bf16[768,128]{1,0:T(8,128)(2,1)S(1)}, bf16[768,128]{1,0:T(8,128)(2,1)S(1)}, u32[]{:S(2)}, u32[]{:S(2)}) collective-permute-start(bf16[768,128]{1,0:T(8,128)(2,1)S(1)} %get-tuple-element.214), channel_id=1, source_target_pairs={{0,8},{1,17},{2,10},{3,19},{4,12},{5,21},{6,14},{7,23},{8,0},{9,25... | collective-permute-start | bytes 589832 | tf_op jit(solution)/shard_map/ppermute | solution.py:669
  11.0 67.8 %collective-permute-start.17 = (bf16[768,128]{1,0:T(8,128)(2,1)S(1)}, bf16[768,128]{1,0:T(8,128)(2,1)S(1)}, u32[]{:S(2)}, u32[]{:S(2)}) collective-permute-start(bf16[768,128]{1,0:T(8,128)(2,1)S(1)} %get-tuple-element.214), channel_id=1, source_target_pairs={{0,4},{4,0},{8,12},{12,8},{16,20},{20,16},{24,28},{28,24},{1,5},{5... | collective-permute-start | bytes 589832 | tf_op jit(solution)/shard_map/ppermute | solution.py:602
  13.3 7.7 %collective-permute-start.3 = (bf16[528,128]{1,0:T(8,128)(2,1)}, bf16[528,128]{1,0:T(8,128)(2,1)}, u32[]{:S(2)}, u32[]{:S(2)}) collective-permute-start(bf16[528,128]{1,0:T(8,128)(2,1)} %get-tuple-element.216), channel_id=1, source_target_pairs={{0,4},{4,0},{8,12},{12,8},{16,20},{20,16},{24,28},{28,24},{1,5},{5... | collective-permute-start | bytes 405512 | tf_op jit(solution)/shard_map/ppermute | solution.py:602
  24.2 11.3 %collective-permute-start.14 = (bf16[2,528,128]{2,1,0:T(8,128)(2,1)S(1)}, bf16[2,528,128]{2,1,0:T(8,128)(2,1)S(1)}, u32[]{:S(2)}, u32[]{:S(2)}) collective-permute-start(bf16[2,528,128]{2,1,0:T(8,128)(2,1)S(1)} %get-tuple-element.218), channel_id=1, source_target_pairs={{0,24},{1,9},{2,26},{3,11},{4,28},{5,13},{6,30},{7,15},{8,16},{9,1... | collective-permute-start | bytes 811016 | tf_op jit(solution)/shard_map/ppermute | solution.py:669
  28.0 32.2 %collective-permute-start.15 = (bf16[2,528,128]{2,1,0:T(8,128)(2,1)S(1)}, bf16[2,528,128]{2,1,0:T(8,128)(2,1)S(1)}, u32[]{:S(2)}, u32[]{:S(2)}) collective-permute-start(bf16[2,528,128]{2,1,0:T(8,128)(2,1)S(1)} %get-tuple-element.218), channel_id=1, source_target_pairs={{0,16},{1,25},{2,18},{3,27},{4,20},{5,29},{6,22},{7,31},{8,24},{9,... | collective-permute-start | bytes 811016 | tf_op jit(solution)/shard_map/ppermute | solution.py:669
  28.3 32.0 %collective-permute-start.16 = (bf16[2,528,128]{2,1,0:T(8,128)(2,1)S(1)}, bf16[2,528,128]{2,1,0:T(8,128)(2,1)S(1)}, u32[]{:S(2)}, u32[]{:S(2)}) collective-permute-start(bf16[2,528,128]{2,1,0:T(8,128)(2,1)S(1)} %get-tuple-element.218), channel_id=1, source_target_pairs={{0,8},{1,17},{2,10},{3,19},{4,12},{5,21},{6,14},{7,23},{8,0},{9,25... | collective-permute-start | bytes 811016 | tf_op jit(solution)/shard_map/ppermute | solution.py:669
  28.7 5.0 collective-permute-start.4
  33.7 57.2 %collective-permute-start.20 = (bf16[2048,256]{1,0:T(8,128)(2,1)S(1)}, bf16[2048,256]{1,0:T(8,128)(2,1)S(1)}, u32[]{:S(2)}, u32[]{:S(2)}) collective-permute-start(bf16[2048,256]{1,0:T(8,128)(2,1)S(1)} %get-tuple-element.182.refs_0_), channel_id=1, source_target_pairs={{0,2},{1,3},{2,0},{3,1},{4,6},{5,7},{6,4},{7,5},{8,10},{9,11},{10,... | collective-permute-start | bytes 3145736 | tf_op jit(solution)/shard_map/ppermute | solution.py:602
  35.5 30.5 %collective-permute-start.6 = (bf16[2,512,128]{2,1,0:T(8,128)(2,1)S(1)}, bf16[2,512,128]{2,1,0:T(8,128)(2,1)S(1)}, u32[]{:S(2)}, u32[]{:S(2)}) collective-permute-start(bf16[2,512,128]{2,1,0:T(8,128)(2,1)S(1)} %get-tuple-element.220), channel_id=1, source_target_pairs={{0,16},{1,25},{2,18},{3,27},{4,20},{5,29},{6,22},{7,31},{8,24},{9,... | collective-permute-start | bytes 786440 | tf_op jit(solution)/shard_map/ppermute | solution.py:669
  60.3 14.9 %collective-permute-start.7 = (bf16[2,512,128]{2,1,0:T(8,128)(2,1)S(1)}, bf16[2,512,128]{2,1,0:T(8,128)(2,1)S(1)}, u32[]{:S(2)}, u32[]{:S(2)}) collective-permute-start(bf16[2,512,128]{2,1,0:T(8,128)(2,1)S(1)} %get-tuple-element.220), channel_id=1, source_target_pairs={{0,8},{1,17},{2,10},{3,19},{4,12},{5,21},{6,14},{7,23},{8,0},{9,25... | collective-permute-start | bytes 786440 | tf_op jit(solution)/shard_map/ppermute | solution.py:669
  60.3 16.5 %collective-permute-start.5 = (bf16[2,512,128]{2,1,0:T(8,128)(2,1)S(1)}, bf16[2,512,128]{2,1,0:T(8,128)(2,1)S(1)}, u32[]{:S(2)}, u32[]{:S(2)}) collective-permute-start(bf16[2,512,128]{2,1,0:T(8,128)(2,1)S(1)} %get-tuple-element.220), channel_id=1, source_target_pairs={{0,24},{1,9},{2,26},{3,11},{4,28},{5,13},{6,30},{7,15},{8,16},{9,1... | collective-permute-start | bytes 786440 | tf_op jit(solution)/shard_map/ppermute | solution.py:669
  66.0 25.5 %collective-permute-start.19 = (bf16[2048,256]{1,0:T(8,128)(2,1)S(1)}, bf16[2048,256]{1,0:T(8,128)(2,1)S(1)}, u32[]{:S(2)}, u32[]{:S(2)}) collective-permute-start(bf16[2048,256]{1,0:T(8,128)(2,1)S(1)} %get-tuple-element.182.refs_0_), channel_id=1, source_target_pairs={{0,1},{1,0},{2,3},{3,2},{4,5},{5,4},{6,7},{7,6},{8,9},{9,8},{10,11... | collective-permute-start | bytes 3145736 | tf_op jit(solution)/shard_map/ppermute | solution.py:602
  75.2 68.0 %collective-permute-start.1 = (bf16[4096,256]{1,0:T(8,128)(2,1)S(1)}, bf16[4096,256]{1,0:T(8,128)(2,1)S(1)}, u32[]{:S(2)}, u32[]{:S(2)}) collective-permute-start(bf16[4096,256]{1,0:T(8,128)(2,1)S(1)} %copy-done.33), channel_id=1, source_target_pairs={{0,2},{1,3},{2,0},{3,1},{4,6},{5,7},{6,4},{7,5},{8,10},{9,11},{10,... | collective-permute-start | bytes 6291464 | tf_op jit(solution)/shard_map/ppermute | solution.py:602
  76.7 13.0 %collective-permute-start.18 = (bf16[3,768,128]{2,1,0:T(8,128)(2,1)S(1)}, bf16[3,768,128]{2,1,0:T(8,128)(2,1)S(1)}, u32[]{:S(2)}, u32[]{:S(2)}) collective-permute-start(bf16[3,768,128]{2,1,0:T(8,128)(2,1)S(1)} %pad_maximum_fusion.4), channel_id=1, source_target_pairs={{0,4},{4,0},{8,12},{12,8},{16,20},{20,16},{24,28},{28,24},{1,5},{5... | collective-permute-start | bytes 1769480 | tf_op jit(solution)/shard_map/ppermute | solution.py:602
  78.8 64.4 %collective-permute-start.9 = (bf16[2048,256]{1,0:T(8,128)(2,1)S(1)}, bf16[2048,256]{1,0:T(8,128)(2,1)S(1)}, u32[]{:S(2)}, u32[]{:S(2)}) collective-permute-start(bf16[2048,256]{1,0:T(8,128)(2,1)S(1)} %get-tuple-element.183.refs_0_), channel_id=1, source_target_pairs={{0,2},{1,3},{2,0},{3,1},{4,6},{5,7},{6,4},{7,5},{8,10},{9,11},{10,... | collective-permute-start | bytes 3145736 | tf_op jit(solution)/shard_map/ppermute | solution.py:602
  89.7 83.4 %collective-permute-start.8 = (bf16[2048,256]{1,0:T(8,128)(2,1)S(1)}, bf16[2048,256]{1,0:T(8,128)(2,1)S(1)}, u32[]{:S(2)}, u32[]{:S(2)}) collective-permute-start(bf16[2048,256]{1,0:T(8,128)(2,1)S(1)} %get-tuple-element.183.refs_0_), channel_id=1, source_target_pairs={{0,1},{1,0},{2,3},{3,2},{4,5},{5,4},{6,7},{7,6},{8,9},{9,8},{10,11... | collective-permute-start | bytes 3145736 | tf_op jit(solution)/shard_map/ppermute | solution.py:602
  90.9 109.3 %collective-permute-start = (bf16[4096,256]{1,0:T(8,128)(2,1)S(1)}, bf16[4096,256]{1,0:T(8,128)(2,1)}, u32[]{:S(2)}, u32[]{:S(2)}) collective-permute-start(bf16[4096,256]{1,0:T(8,128)(2,1)S(1)} %copy-done.33), channel_id=1, source_target_pairs={{0,1},{1,0},{2,3},{3,2},{4,5},{5,4},{6,7},{7,6},{8,9},{9,8},{10,11... | collective-permute-start | bytes 6291464 | tf_op jit(solution)/shard_map/ppermute | solution.py:602
  91.5 52.9 %collective-permute-start.21 = (bf16[2048,256]{1,0:T(8,128)(2,1)S(1)}, bf16[2048,256]{1,0:T(8,128)(2,1)S(1)}, u32[]{:S(2)}, u32[]{:S(2)}) collective-permute-start(bf16[2048,256]{1,0:T(8,128)(2,1)S(1)} %collective-permute-done.20.refs_2_), channel_id=1, source_target_pairs={{0,1},{1,0},{2,3},{3,2},{4,5},{5,4},{6,7},{7,6},{8,9},{9,8},{10,11... | collective-permute-start | bytes 3145736 | tf_op jit(solution)/shard_map/ppermute | solution.py:602
  143.2 31.4 %collective-permute-start.10 = (bf16[2048,256]{1,0:T(8,128)(2,1)S(1)}, bf16[2048,256]{1,0:T(8,128)(2,1)S(1)}, u32[]{:S(2)}, u32[]{:S(2)}) collective-permute-start(bf16[2048,256]{1,0:T(8,128)(2,1)S(1)} %collective-permute-done.9.refs_2_), channel_id=1, source_target_pairs={{0,1},{1,0},{2,3},{3,2},{4,5},{5,4},{6,7},{7,6},{8,9},{9,8},{10,11... | collective-permute-start | bytes 3145736 | tf_op jit(solution)/shard_map/ppermute | solution.py:602
  143.2 57.0 %collective-permute-start.2 = (bf16[4096,256]{1,0:T(8,128)(2,1)S(1)}, bf16[4096,256]{1,0:T(8,128)(2,1)}, u32[]{:S(2)}, u32[]{:S(2)}) collective-permute-start(bf16[4096,256]{1,0:T(8,128)(2,1)S(1)} %collective-permute-done.1.refs_2_), channel_id=1, source_target_pairs={{0,1},{1,0},{2,3},{3,2},{4,5},{5,4},{6,7},{7,6},{8,9},{9,8},{10,11... | collective-permute-start | bytes 6291464 | tf_op jit(solution)/shard_map/ppermute | solution.py:602
  172.9 22.1 %collective-permute-start.25 = (f32[1,2048]{1,0:T(1,128)S(1)}, f32[1,2048]{1,0:T(1,128)S(1)}, u32[]{:S(2)}, u32[]{:S(2)}) collective-permute-start(f32[1,2048]{1,0:T(1,128)S(1)} %get-tuple-element.99), channel_id=1, source_target_pairs={{0,1},{1,0},{2,3},{3,2},{4,5},{5,4},{6,7},{7,6},{8,9},{9,8},{10,11... | collective-permute-start | bytes 24584 | tf_op jit(solution)/shard_map/ppermute | solution.py:602
  173.1 22.4 %collective-permute-start.26 = (f32[1,2048]{1,0:T(1,128)S(1)}, f32[1,2048]{1,0:T(1,128)S(1)}, u32[]{:S(2)}, u32[]{:S(2)}) collective-permute-start(f32[1,2048]{1,0:T(1,128)S(1)} %get-tuple-element.99), channel_id=1, source_target_pairs={{0,2},{1,3},{2,0},{3,1},{4,6},{5,7},{6,4},{7,5},{8,10},{9,11},{10,... | collective-permute-start | bytes 24584 | tf_op jit(solution)/shard_map/ppermute | solution.py:602
  174.6 22.4 %collective-permute-start.27 = (f32[1,2048]{1,0:T(1,128)S(1)}, f32[1,2048]{1,0:T(1,128)S(1)}, u32[]{:S(2)}, u32[]{:S(2)}) collective-permute-start(f32[1,2048]{1,0:T(1,128)S(1)} %get-tuple-element.99), channel_id=1, source_target_pairs={{0,3},{1,2},{2,1},{3,0},{4,7},{5,6},{6,5},{7,4},{8,11},{9,10},{10,... | collective-permute-start | bytes 24584 | tf_op jit(solution)/shard_map/ppermute | solution.py:602
  195.1 2.0 collective-permute-start.22
  195.5 3.7 collective-permute-start.23
  197.0 3.1 collective-permute-start.24
  213.4 28.6 %collective-permute-start.31 = (f32[1,2048]{1,0:T(1,128)S(1)}, f32[1,2048]{1,0:T(1,128)S(1)}, u32[]{:S(2)}, u32[]{:S(2)}) collective-permute-start(f32[1,2048]{1,0:T(1,128)S(1)} %get-tuple-element.120), channel_id=1, source_target_pairs={{0,1},{1,0},{2,3},{3,2},{4,5},{5,4},{6,7},{7,6},{8,9},{9,8},{10,11... | collective-permute-start | bytes 24584 | tf_op jit(solution)/shard_map/ppermute | solution.py:602
  213.5 29.0 %collective-permute-start.32 = (f32[1,2048]{1,0:T(1,128)S(1)}, f32[1,2048]{1,0:T(1,128)S(1)}, u32[]{:S(2)}, u32[]{:S(2)}) collective-permute-start(f32[1,2048]{1,0:T(1,128)S(1)} %get-tuple-element.120), channel_id=1, source_target_pairs={{0,2},{1,3},{2,0},{3,1},{4,6},{5,7},{6,4},{7,5},{8,10},{9,11},{10,... | collective-permute-start | bytes 24584 | tf_op jit(solution)/shard_map/ppermute | solution.py:602
  214.1 28.5 %collective-permute-start.33 = (f32[1,2048]{1,0:T(1,128)S(1)}, f32[1,2048]{1,0:T(1,128)S(1)}, u32[]{:S(2)}, u32[]{:S(2)}) collective-permute-start(f32[1,2048]{1,0:T(1,128)S(1)} %get-tuple-element.120), channel_id=1, source_target_pairs={{0,3},{1,2},{2,1},{3,0},{4,7},{5,6},{6,5},{7,4},{8,11},{9,10},{10,... | collective-permute-start | bytes 24584 | tf_op jit(solution)/shard_map/ppermute | solution.py:602
  227.7 14.9 %collective-permute-start.37 = (f32[1,2048]{1,0:T(1,128)S(1)}, f32[1,2048]{1,0:T(1,128)S(1)}, u32[]{:S(2)}, u32[]{:S(2)}) collective-permute-start(f32[1,2048]{1,0:T(1,128)S(1)} %get-tuple-element.125), channel_id=1, source_target_pairs={{0,1},{1,0},{2,3},{3,2},{4,5},{5,4},{6,7},{7,6},{8,9},{9,8},{10,11... | collective-permute-start | bytes 24584 | tf_op jit(solution)/shard_map/ppermute | solution.py:602
  228.2 14.4 %collective-permute-start.38 = (f32[1,2048]{1,0:T(1,128)S(1)}, f32[1,2048]{1,0:T(1,128)S(1)}, u32[]{:S(2)}, u32[]{:S(2)}) collective-permute-start(f32[1,2048]{1,0:T(1,128)S(1)} %get-tuple-element.125), channel_id=1, source_target_pairs={{0,2},{1,3},{2,0},{3,1},{4,6},{5,7},{6,4},{7,5},{8,10},{9,11},{10,... | collective-permute-start | bytes 24584 | tf_op jit(solution)/shard_map/ppermute | solution.py:602
  242.0 3.1 collective-permute-start.39
  321.0 45.5 %collective-permute-start.54 = (f32[4880]{0:T(1024)S(1)}, f32[4880]{0:T(1024)S(1)}, u32[]{:S(2)}, u32[]{:S(2)}) collective-permute-start(f32[4880]{0:T(1024)S(1)} %concatenate.99), channel_id=1, source_target_pairs={{0,4},{4,0},{8,12},{12,8},{16,20},{20,16},{24,28},{28,24},{1,5},{5... | collective-permute-start | bytes 58568 | tf_op jit(solution)/shard_map/ppermute | solution.py:602
  339.6 56.3 %collective-permute-start.43 = (bf16[2,128,640]{2,1,0:T(8,128)(2,1)}, bf16[2,128,640]{2,1,0:T(8,128)(2,1)S(1)}, u32[]{:S(2)}, u32[]{:S(2)}) collective-permute-start(bf16[2,128,640]{2,1,0:T(8,128)(2,1)} %get-tuple-element.176), channel_id=1, source_target_pairs={{0,24},{1,9},{2,26},{3,11},{4,28},{5,13},{6,30},{7,15},{8,16},{9,1... | collective-permute-start | bytes 983048 | tf_op jit(solution)/shard_map/ppermute | solution.py:669
  362.7 35.1 %collective-permute-start.44 = (bf16[2,128,640]{2,1,0:T(8,128)(2,1)}, bf16[2,128,640]{2,1,0:T(8,128)(2,1)S(1)}, u32[]{:S(2)}, u32[]{:S(2)}) collective-permute-start(bf16[2,128,640]{2,1,0:T(8,128)(2,1)} %get-tuple-element.178), channel_id=1, source_target_pairs={{0,16},{1,25},{2,18},{3,27},{4,20},{5,29},{6,22},{7,31},{8,24},{9,... | collective-permute-start | bytes 983048 | tf_op jit(solution)/shard_map/ppermute | solution.py:669
  366.5 8.4 %collective-permute-start.55 = (f32[4880]{0:T(1024)S(1)}, f32[4880]{0:T(1024)S(1)}, u32[]{:S(2)}, u32[]{:S(2)}) collective-permute-start(f32[4880]{0:T(1024)S(1)} %add.354), channel_id=1, source_target_pairs={{0,8},{4,12},{8,0},{12,4},{16,24},{20,28},{24,16},{28,20},{1,9},{5... | collective-permute-start | bytes 58568 | tf_op jit(solution)/shard_map/ppermute | solution.py:602
  367.1 21.2 %collective-permute-start.56 = (f32[4880]{0:T(1024)S(1)}, f32[4880]{0:T(1024)S(1)}, u32[]{:S(2)}, u32[]{:S(2)}) collective-permute-start(f32[4880]{0:T(1024)S(1)} %add.354), channel_id=1, source_target_pairs={{0,16},{4,20},{8,24},{12,28},{16,0},{20,4},{24,8},{28,12},{1,17},{... | collective-permute-start | bytes 58568 | tf_op jit(solution)/shard_map/ppermute | solution.py:602
  369.6 18.7 %collective-permute-start.57 = (f32[4880]{0:T(1024)S(1)}, f32[4880]{0:T(1024)S(1)}, u32[]{:S(2)}, u32[]{:S(2)}) collective-permute-start(f32[4880]{0:T(1024)S(1)} %add.354), channel_id=1, source_target_pairs={{0,24},{4,28},{8,16},{12,20},{16,8},{20,12},{24,0},{28,4},{1,25},{... | collective-permute-start | bytes 58568 | tf_op jit(solution)/shard_map/ppermute | solution.py:602
  374.9 22.9 %collective-permute-start.45 = (bf16[2,128,640]{2,1,0:T(8,128)(2,1)S(1)}, bf16[2,128,640]{2,1,0:T(8,128)(2,1)S(1)}, u32[]{:S(2)}, u32[]{:S(2)}) collective-permute-start(bf16[2,128,640]{2,1,0:T(8,128)(2,1)S(1)} %get-tuple-element.177), channel_id=1, source_target_pairs={{0,8},{1,17},{2,10},{3,19},{4,12},{5,21},{6,14},{7,23},{8,0},{9,25... | collective-permute-start | bytes 983048 | tf_op jit(solution)/shard_map/ppermute | solution.py:669
  388.4 4.3 collective-permute-start.59
  389.6 4.1 collective-permute-start.60
  392.8 11.4 %collective-permute-start.61 = (bf16[2,128,512]{2,1,0:T(8,128)(2,1)}, bf16[2,128,512]{2,1,0:T(8,128)(2,1)}, u32[]{:S(2)}, u32[]{:S(2)}) collective-permute-start(bf16[2,128,512]{2,1,0:T(8,128)(2,1)} %get-tuple-element.179), channel_id=1, source_target_pairs={{0,24},{1,9},{2,26},{3,11},{4,28},{5,13},{6,30},{7,15},{8,16},{9,1... | collective-permute-start | bytes 786440 | tf_op jit(solution)/shard_map/ppermute | solution.py:669
  393.7 25.7 %collective-permute-start.62 = (bf16[2,128,512]{2,1,0:T(8,128)(2,1)}, bf16[2,128,512]{2,1,0:T(8,128)(2,1)}, u32[]{:S(2)}, u32[]{:S(2)}) collective-permute-start(bf16[2,128,512]{2,1,0:T(8,128)(2,1)} %get-tuple-element.181), channel_id=1, source_target_pairs={{0,16},{1,25},{2,18},{3,27},{4,20},{5,29},{6,22},{7,31},{8,24},{9,... | collective-permute-start | bytes 786440 | tf_op jit(solution)/shard_map/ppermute | solution.py:669
  395.9 25.5 %collective-permute-start.63 = (bf16[2,128,512]{2,1,0:T(8,128)(2,1)}, bf16[2,128,512]{2,1,0:T(8,128)(2,1)S(1)}, u32[]{:S(2)}, u32[]{:S(2)}) collective-permute-start(bf16[2,128,512]{2,1,0:T(8,128)(2,1)} %get-tuple-element.180), channel_id=1, source_target_pairs={{0,8},{1,17},{2,10},{3,19},{4,12},{5,21},{6,14},{7,23},{8,0},{9,25... | collective-permute-start | bytes 786440 | tf_op jit(solution)/shard_map/ppermute | solution.py:669
  397.9 56.8 %collective-permute-start.29 = (bf16[4096,256]{1,0:T(8,128)(2,1)}, bf16[4096,256]{1,0:T(8,128)(2,1)}, u32[]{:S(2)}, u32[]{:S(2)}) collective-permute-start(bf16[4096,256]{1,0:T(8,128)(2,1)} %get-tuple-element.109), channel_id=1, source_target_pairs={{0,1},{1,0},{2,3},{3,2},{4,5},{5,4},{6,7},{7,6},{8,9},{9,8},{10,11... | collective-permute-start | bytes 6291464 | tf_op jit(solution)/shard_map/ppermute | solution.py:602
  397.9 32.9 %collective-permute-start.50 = (bf16[4,128,768]{2,1,0:T(8,128)(2,1)}, bf16[4,128,768]{2,1,0:T(8,128)(2,1)}, u32[]{:S(2)}, u32[]{:S(2)}) collective-permute-start(bf16[4,128,768]{2,1,0:T(8,128)(2,1)} %fusion.11), channel_id=1, source_target_pairs={{0,4},{4,0},{8,12},{12,8},{16,20},{20,16},{24,28},{28,24},{1,5},{5... | collective-permute-start | bytes 2359304 | tf_op jit(solution)/shard_map/ppermute | solution.py:602
  404.2 48.3 %collective-permute-start.35 = (bf16[2048,256]{1,0:T(8,128)(2,1)S(1)}, bf16[2048,256]{1,0:T(8,128)(2,1)S(1)}, u32[]{:S(2)}, u32[]{:S(2)}) collective-permute-start(bf16[2048,256]{1,0:T(8,128)(2,1)S(1)} %copy-done.30), channel_id=1, source_target_pairs={{0,1},{1,0},{2,3},{3,2},{4,5},{5,4},{6,7},{7,6},{8,9},{9,8},{10,11... | collective-permute-start | bytes 3145736 | tf_op jit(solution)/shard_map/ppermute | solution.py:602
  419.4 6.2 %collective-permute-start.46 = (bf16[128,640]{1,0:T(8,128)(2,1)S(1)}, bf16[128,640]{1,0:T(8,128)(2,1)S(1)}, u32[]{:S(2)}, u32[]{:S(2)}) collective-permute-start(bf16[128,640]{1,0:T(8,128)(2,1)S(1)} %fusion.35), channel_id=1, source_target_pairs={{0,4},{4,0},{8,12},{12,8},{16,20},{20,16},{24,28},{28,24},{1,5},{5... | collective-permute-start | bytes 491528 | tf_op jit(solution)/shard_map/ppermute | solution.py:602
  422.8 5.0 collective-permute-start.64
  426.4 2.9 collective-permute-start.48
  428.6 6.0 %collective-permute-start.47 = (f32[32,384]{1,0:T(8,128)}, f32[32,384]{1,0:T(8,128)}, u32[]{:S(2)}, u32[]{:S(2)}) collective-permute-start(f32[32,384]{1,0:T(8,128)} %get-tuple-element.221), channel_id=1, source_target_pairs={{0,1},{1,0},{2,3},{3,2},{4,5},{5,4},{6,7},{7,6},{8,9},{9,8},{10,11... | collective-permute-start | bytes 147464 | tf_op jit(solution)/shard_map/ppermute | solution.py:602
  430.2 4.4 collective-permute-start.49
  433.0 9.7 %collective-permute-start.51 = (bf16[128,768]{1,0:T(8,128)(2,1)S(1)}, bf16[128,768]{1,0:T(8,128)(2,1)S(1)}, u32[]{:S(2)}, u32[]{:S(2)}) collective-permute-start(bf16[128,768]{1,0:T(8,128)(2,1)S(1)} %get-tuple-element.184), channel_id=1, source_target_pairs={{0,24},{1,9},{2,26},{3,11},{4,28},{5,13},{6,30},{7,15},{8,16},{9,1... | collective-permute-start | bytes 589832 | tf_op jit(solution)/shard_map/ppermute | solution.py:669
  434.5 15.8 %collective-permute-start.52 = (bf16[128,768]{1,0:T(8,128)(2,1)S(1)}, bf16[128,768]{1,0:T(8,128)(2,1)S(1)}, u32[]{:S(2)}, u32[]{:S(2)}) collective-permute-start(bf16[128,768]{1,0:T(8,128)(2,1)S(1)} %get-tuple-element.186), channel_id=1, source_target_pairs={{0,16},{1,25},{2,18},{3,27},{4,20},{5,29},{6,22},{7,31},{8,24},{9,... | collective-permute-start | bytes 589832 | tf_op jit(solution)/shard_map/ppermute | solution.py:669
  434.5 15.8 %collective-permute-start.53 = (bf16[128,768]{1,0:T(8,128)(2,1)S(1)}, bf16[128,768]{1,0:T(8,128)(2,1)S(1)}, u32[]{:S(2)}, u32[]{:S(2)}) collective-permute-start(bf16[128,768]{1,0:T(8,128)(2,1)S(1)} %get-tuple-element.185), channel_id=1, source_target_pairs={{0,8},{1,17},{2,10},{3,19},{4,12},{5,21},{6,14},{7,23},{8,0},{9,25... | collective-permute-start | bytes 589832 | tf_op jit(solution)/shard_map/ppermute | solution.py:669
  442.7 10.1 %collective-permute-start.41 = (bf16[2048,256]{1,0:T(8,128)(2,1)S(1)}, bf16[2048,256]{1,0:T(8,128)(2,1)S(1)}, u32[]{:S(2)}, u32[]{:S(2)}) collective-permute-start(bf16[2048,256]{1,0:T(8,128)(2,1)S(1)} %copy-done.32), channel_id=1, source_target_pairs={{0,1},{1,0},{2,3},{3,2},{4,5},{5,4},{6,7},{7,6},{8,9},{9,8},{10,11... | collective-permute-start | bytes 3145736 | tf_op jit(solution)/shard_map/ppermute | solution.py:602
  450.4 57.2 %collective-permute-start.28 = (bf16[4096,256]{1,0:T(8,128)(2,1)S(1)}, bf16[4096,256]{1,0:T(8,128)(2,1)S(1)}, u32[]{:S(2)}, u32[]{:S(2)}) collective-permute-start(bf16[4096,256]{1,0:T(8,128)(2,1)S(1)} %copy-done.17), channel_id=1, source_target_pairs={{0,1},{1,0},{2,3},{3,2},{4,5},{5,4},{6,7},{7,6},{8,9},{9,8},{10,11... | collective-permute-start | bytes 6291464 | tf_op jit(solution)/shard_map/ppermute | solution.py:602
  450.4 7.2 %collective-permute-start.34 = (bf16[2048,256]{1,0:T(8,128)(2,1)S(1)}, bf16[2048,256]{1,0:T(8,128)(2,1)S(1)}, u32[]{:S(2)}, u32[]{:S(2)}) collective-permute-start(bf16[2048,256]{1,0:T(8,128)(2,1)S(1)} %copy-done.26), channel_id=1, source_target_pairs={{0,1},{1,0},{2,3},{3,2},{4,5},{5,4},{6,7},{7,6},{8,9},{9,8},{10,11... | collective-permute-start | bytes 3145736 | tf_op jit(solution)/shard_map/ppermute | solution.py:602
  452.5 26.9 %collective-permute-start.40 = (bf16[2048,256]{1,0:T(8,128)(2,1)S(1)}, bf16[2048,256]{1,0:T(8,128)(2,1)S(1)}, u32[]{:S(2)}, u32[]{:S(2)}) collective-permute-start(bf16[2048,256]{1,0:T(8,128)(2,1)S(1)} %copy-done.28), channel_id=1, source_target_pairs={{0,1},{1,0},{2,3},{3,2},{4,5},{5,4},{6,7},{7,6},{8,9},{9,8},{10,11... | collective-permute-start | bytes 3145736 | tf_op jit(solution)/shard_map/ppermute | solution.py:602
  452.8 26.1 %collective-permute-start.36 = (bf16[2048,256]{1,0:T(8,128)(2,1)S(1)}, bf16[2048,256]{1,0:T(8,128)(2,1)S(1)}, u32[]{:S(2)}, u32[]{:S(2)}) collective-permute-start(bf16[2048,256]{1,0:T(8,128)(2,1)S(1)} %add_convert_fusion.3), channel_id=1, source_target_pairs={{0,2},{1,3},{2,0},{3,1},{4,6},{5,7},{6,4},{7,5},{8,10},{9,11},{10,... | collective-permute-start | bytes 3145736 | tf_op jit(solution)/shard_map/ppermute | solution.py:602
  454.6 46.8 %collective-permute-start.42 = (bf16[2048,256]{1,0:T(8,128)(2,1)S(1)}, bf16[2048,256]{1,0:T(8,128)(2,1)S(1)}, u32[]{:S(2)}, u32[]{:S(2)}) collective-permute-start(bf16[2048,256]{1,0:T(8,128)(2,1)S(1)} %add_convert_fusion.2), channel_id=1, source_target_pairs={{0,2},{1,3},{2,0},{3,1},{4,6},{5,7},{6,4},{7,5},{8,10},{9,11},{10,... | collective-permute-start | bytes 3145736 | tf_op jit(solution)/shard_map/ppermute | solution.py:602
  457.6 88.2 %collective-permute-start.30 = (bf16[4096,256]{1,0:T(8,128)(2,1)S(1)}, bf16[4096,256]{1,0:T(8,128)(2,1)S(1)}, u32[]{:S(2)}, u32[]{:S(2)}) collective-permute-start(bf16[4096,256]{1,0:T(8,128)(2,1)S(1)} %add_convert_fusion.1), channel_id=1, source_target_pairs={{0,2},{1,3},{2,0},{3,1},{4,6},{5,7},{6,4},{7,5},{8,10},{9,11},{10,... | collective-permute-start | bytes 6291464 | tf_op jit(solution)/shard_map/ppermute | solution.py:602
  (55 other events, 1075.0 us)

commit v3 on v2

--- a/solution.py
+++ b/solution.py
@@ -15,6 +15,7 @@
 BF16 = jnp.bfloat16
 epsilon = 1e-05
 NEG = -1e30
+LOG2E = 1.4426950408889634
 
 
 def nn(a, b):
@@ -74,9 +75,9 @@
     early, late = run_row[:, :HALF], run_row[:, HALF:]
     col_early = jnp.broadcast_to(run_col[:HALF], (HALF, HALF))
     col_late = jnp.broadcast_to(run_col[HALF:], (HALF, HALF))
-    first = jnp.exp(jnp.where(upper, early - col_early, NEG))
-    cross = jnp.exp(late - col_early)
-    second = jnp.exp(jnp.where(upper, late - col_late, NEG))
+    first = jnp.exp2(jnp.where(upper, early - col_early, NEG))
+    cross = jnp.exp2(late - col_early)
+    second = jnp.exp2(jnp.where(upper, late - col_late, NEG))
     return first, cross, second
 
 
@@ -170,13 +171,15 @@
         step_raw = proj[base : base + heads, :] + twice(headc_ref[0])
         step_ref[...] = step_raw
         steps = softplus(step_raw)
-        running = times_ones(steps * twice(headc_ref[1]), triangle(lambda s, t: s <= t))
+        running = times_ones(
+            steps * (twice(headc_ref[1]) * LOG2E), triangle(lambda s, t: s <= t)
+        )
         run_ref[...] = running
         run_cols = jnp.transpose(running)
         ends = running[:, Q - 1 :]
-        grow = jnp.exp(running)
-        to_end = jnp.exp(ends - running)
-        whole = jnp.exp(ends)
+        grow = jnp.exp2(running)
+        to_end = jnp.exp2(ends - running)
+        whole = jnp.exp2(ends)
         upper = upper_half()
 
         state_ref[...] = state[...]
@@ -211,7 +214,7 @@
 
 def middle_kernel(len_ref, *refs, seq, inner, inner_all, width, aliased):
     c0, c1, c2, c3, wo_ref, chan_ref, m_ref, sq_ref = refs[:8]
-    nout_ref, b0, b1, b2, b3, gno_ref, stat_ref, gain_acc, nout = refs[8 + aliased :]
+    nout_ref, gno_ref, b0, b1, b2, b3, stat_ref, gain_acc, nout = refs[8 + aliased :]
     block = pl.program_id(0)
     length = len_ref[seq]
     part = width // 4
@@ -250,10 +253,11 @@
             ref[...] = branch[:, k * part : (k + 1) * part].astype(BF16)
 
 
-def backward_kernel(len_ref, *refs, seq, inner, inner_all, heads, width, blocks):
+def backward_kernel(len_ref, *refs, seq, inner, inner_all, heads, width, blocks, aliased):
     x_refs, (wt_ref, chan_ref, bcc_ref, headc_ref) = refs[:4], refs[4:8]
     (gate_ref, val_ref, z_ref, y_ref, gno_ref, bc_ref, bcz_ref) = refs[8:15]
     (step_ref, run_ref, state_ref, sq_ref, stat_ref) = refs[15:20]
+    refs = refs[:20] + refs[20 + aliased :]
     low_refs, g_refs, (chan_acc, bc_acc, head_acc, norm_acc) = refs[20:22], refs[22:26], refs[26:30]
     low, gstate, vhead, bhead, dcb, wdec, gudec, sent = refs[30:]
     step = pl.program_id(0)
@@ -288,7 +292,7 @@
         bcz = bcz_ref[...]
         sig = jax.nn.sigmoid(bcz)
         shared = bcz * sig
-        shared_slope = sig * (1.0 + bcz * (1.0 - sig))
+        shared_slope = sig + shared * (1.0 - sig)
         b_rows, c_rows = shared[:states], shared[states:]
         cb_blocks, _ = intersection(b_rows, c_rows)
         b_low, c_low = b_rows.astype(BF16), c_rows.astype(BF16)
@@ -298,9 +302,9 @@
         running = run_ref[...]
         run_cols = jnp.transpose(running)
         ends = running[:, Q - 1 :]
-        grow = jnp.exp(running)
-        to_end = jnp.exp(ends - running)
-        whole = jnp.exp(ends)
+        grow = jnp.exp2(running)
+        to_end = jnp.exp2(ends - running)
+        whole = jnp.exp2(ends)
         upper = upper_half()
 
         sent[...] = nn(gstate[...].astype(BF16), b_low)
@@ -317,7 +321,7 @@
             u = y + skip * v
             m = u * silu_g
             gm = inv_gate * gain * gno - m * pull
-            low[rows, :] = (gm * u * (sig_g * (1.0 + gate * (1.0 - sig_g)))).astype(BF16)
+            low[rows, :] = (gm * u * (sig_g + silu_g * (1.0 - sig_g))).astype(BF16)
             gu = gm * silu_g
             chan_acc[5, rows, :] += fold(gu * v)
             w = v * steps[h : h + 1]
@@ -346,7 +350,7 @@
             gud = (gu * grow[h : h + 1]).astype(BF16)
             gudec[rows, :] = gud
             wdec[rows, :] = (w * to_end[h : h + 1]).astype(BF16)
-            gz = (skip * gu + gw * steps[h : h + 1]) * (sig_z * (1.0 + z * (1.0 - sig_z)))
+            gz = (skip * gu + gw * steps[h : h + 1]) * (sig_z + v * (1.0 - sig_z))
             taps = [chan_ref[j, rows, :] for j in range(4)]
             gv, shifted = conv_back(gz, vhead[rows, :], taps)
             vhead[rows, :] = gz[:, :HALF]
@@ -417,7 +421,7 @@
 
 def params(count):
     return pltpu.CompilerParams(
-        dimension_semantics=("arbitrary",) * count, vmem_limit_bytes=44 << 20
+        dimension_semantics=("arbitrary",) * count, vmem_limit_bytes=52 << 20
     )
 
 
@@ -505,8 +509,8 @@
         ),
         out_shape=[
             shape((rows, inner), BF16),
-            *[shape((rows, part), BF16)] * 4,
             shape((inner, rows)),
+            *[shape((SEQ_LEN, part), BF16)] * 4,
             shape((1, SEQ_LEN)),
             shape((inner, HALF)),
         ],
@@ -523,8 +527,8 @@
             ],
             out_specs=[
                 pl.BlockSpec((Q, inner), lambda c, lens: (at(c), 0)),
-                *[piece] * 4,
                 col,
+                *[pl.BlockSpec((Q, part), lambda c, lens: (c, 0))] * 4,
                 stat,
                 pl.BlockSpec((inner, HALF), lambda c, lens: (0, 0)),
             ],
@@ -536,7 +540,9 @@
     )(lengths, *cots, wo, chan, m, squares, *before)
 
 
-def run_backward(seq, lengths, xs, wt, chan, bcc, headc, saved, squares, stat, inner_all):
+def run_backward(
+    seq, lengths, xs, wt, chan, bcc, headc, saved, squares, stat, inner_all, before
+):
     part = xs[0].shape[1]
     width = 4 * part
     inner, heads, states2 = chan.shape[1], headc.shape[1], bcc.shape[1]
@@ -559,9 +565,10 @@
             heads=heads,
             width=width,
             blocks=blocks,
+            aliased=len(before),
         ),
         out_shape=[
-            *[shape((SEQ_LEN, count), BF16) for count in sets],
+            *[shape((saved[0].shape[1], count), BF16) for count in sets],
             *[shape((SEQ_LEN, part), BF16)] * 4,
             *[shape(dims) for dims in accs],
         ],
@@ -576,9 +583,10 @@
                 *[col(heads)] * 2,
                 pl.BlockSpec((inner, states2 // 2), lambda c, lens: (at(c), 0)),
                 *[pl.BlockSpec((1, Q), lambda c, lens: (0, back(c)))] * 2,
+                *[pl.BlockSpec(memory_space=pl.ANY)] * len(before),
             ],
             out_specs=[
-                *[pl.BlockSpec((Q, count), lambda c, lens: (back(c), 0)) for count in sets],
+                *[pl.BlockSpec((Q, count), lambda c, lens: (at(c), 0)) for count in sets],
                 *[piece] * 4,
                 *[keep(dims) for dims in accs],
             ],
@@ -593,9 +601,10 @@
                 pltpu.VMEM((inner, Q), F32),
             ],
         ),
+        input_output_aliases={21 + i: i for i in range(len(before))},
         compiler_params=params(1),
         name="mixer_backward",
-    )(lengths, *xs, *consts, *saved, squares, stat)
+    )(lengths, *xs, *consts, *saved, squares, stat, *before)
 
 
 def exchange(a, axis, bit):
@@ -803,7 +812,7 @@
 ):
     tensor_count = lax.axis_size("tensor")
     tensor = lax.axis_index("tensor")
-    rows, _ = tokens.shape
+    rows, part = tokens.shape
     seqs = rows // SEQ_LEN
     inner = w_gate.shape[1]
     inner_all = inner * tensor_count
@@ -836,55 +845,49 @@
         *saved, here = run_forward(q, seqs, lengths, xs[q], wt, chan, bcc, headc, saved)
         squares.append(direct_sum(here, "tensor", (1, 2, 3)))
     normed, gate, val, z, y, m, *shared = saved
-    middle, stats, gain_acc = [], [], None
+    middle, stats, gain_acc, out_rows = [], [], None, []
     for q in range(seqs):
         *middle, stat, here = run_middle(
             q, lengths, cots, wo, chan, m, squares[q], inner_all, middle
         )
+        middle, branch = middle[:2], middle[2:]
         stats.append(direct_sum(stat, "tensor", (1, 2, 3)))
         gain_acc = here if gain_acc is None else gain_acc + here
-    nout, *branch, gno = middle
+        out_rows.append(reduce_pieces(branch))
+    nout, gno = middle
     g_out = jnp.concatenate([over_rows(cot, nout) for cot in cots], 0)
-    branch = reduce_pieces(branch)
-    out_rows = (tokens.astype(F32) + branch).astype(BF16)
     grad_out_rows = rows_line_first(g_out)
-
-    grad_rows, accs, sums = [], None, None
+    out_rows = (tokens.astype(F32) + jnp.concatenate(out_rows, 0)).astype(BF16)
+
+    grad_rows, accs, lows = [], None, []
     kept = (gate, val, z, y, gno, *shared)
     for q in range(seqs):
-        low_a, low_b, *rest = run_backward(
-            q, lengths, xs[q], wt, chan, bcc, headc, kept, squares[q], stats[q], inner_all
+        *lows, g0, g1, g2, g3, a0, a1, a2, a3 = run_backward(
+            q, lengths, xs[q], wt, chan, bcc, headc, kept, squares[q], stats[q], inner_all, lows
         )
-        gin, here = rest[:4], rest[4:]
+        here = (a0, a1, a2, a3)
         accs = here if accs is None else [a + b for a, b in zip(accs, here)]
-        grad_rows.append(reduce_pieces(gin))
-        here = normed[q * SEQ_LEN : (q + 1) * SEQ_LEN]
-        part_b = over_rows(here, low_b)
-        part_a = over_rows(here, low_a)
-        if sums is None:
-            sums = lax.optimization_barrier((part_a, part_b))
-        else:
-            part_b = sums[1] + part_b
-            part_a = sums[0] + part_a
-            sums = (part_a, part_b)
+        grad_rows.append(reduce_pieces((g0, g1, g2, g3)))
+    sum_b = over_rows(normed, lows[1])
+    sum_a = over_rows(normed, lows[0])
+    sums = (sum_a, sum_b)
     valid = (jnp.arange(SEQ_LEN)[None] < lengths[:, None]).reshape(rows)[:, None]
     grad_rows = jnp.concatenate(grad_rows, 0) + jnp.where(valid, grad_out.astype(F32), 0.0)
 
     chan_acc, bc_acc, head_acc, norm_acc = accs
-    cut = sums[0].shape[1]
-    column = jnp.arange(sums[1].shape[1]) == base + heads - cut
-    norm_column = jnp.sum(norm_acc, 0)[:, None]
-    sum_b = jnp.where(column[None], norm_column, sums[1])
-    grads = jnp.concatenate([rows_pair_first(sums[0]), rows_line_first(sum_b)], 1)
+    grads = jnp.concatenate([rows_pair_first(sums[0]), rows_line_first(sums[1])], 1)
     rest = grads[:, 2 * inner :].reshape(tensor_count, -1, states2 + HALF)
     rest = reduce_pieces([take(rest, tensor ^ i, 0) for i in range(4)], F32)
-    sizes = [5 * inner, inner, inner, 2 * heads, 5 * states2]
+    norm = jnp.sum(norm_acc, 0).reshape(tensor_count, part)
+    norm = jnp.concatenate([take(norm, tensor ^ i, 0) for i in range(tensor_count)])
+    sizes = [5 * inner, inner, inner, 2 * heads]
     flat = jnp.concatenate(
         [
             jnp.sum(chan_acc, -1).reshape(-1),
             jnp.sum(gain_acc, -1),
             jnp.sum(head_acc, -1).reshape(-1),
             jnp.sum(bc_acc, -1).reshape(-1),
+            norm,
         ]
     )
     if lax.axis_size("dp") == 8:
@@ -893,12 +896,16 @@
     else:
         flat = exchange_sum(flat, "dp")
     cuts = [sum(sizes[: i + 1]) for i in range(4)]
-    g_conv, g_skip, g_gain, g_head, g_conv_bc = jnp.split(flat, cuts)
-    g_conv_bc = direct_sum(g_conv_bc, "tensor", (1, 2, 3))
+    g_conv, g_skip, g_gain, g_head, everywhere = jnp.split(flat, cuts)
+    everywhere = direct_sum(everywhere, "tensor", (1, 2, 3))
+    g_conv_bc = everywhere[: 5 * states2]
+    share = part // lax.axis_size("dp")
+    first = 5 * states2 + (lax.axis_index("dp") * tensor_count + tensor) * share
+    g_norm = lax.dynamic_slice_in_dim(everywhere, first, share, 0)
     return (
         out_rows,
         grad_rows,
-        rest[:, states2 + heads],
+        g_norm,
         grads[:, :inner],
         grads[:, inner : 2 * inner],
         rest[:, :states2],

time: 554 us -> 552 us (level)
  Pallas kernels: 137 us -> 144 us
  waiting for transfers between devices: 221 us -> 214 us
    ppermute x47 -> x50, waiting for transfers between devices: 169 us -> 162 us  [exchange(): lax.ppermute(a, axis, [(i, i ^ bit) for i in range(lax.axis_size(axis))])]
    unnamed x120 -> x82, local copies, waits for them, and re-layouts: 16.9 us -> 11.1 us
    ppermute x47 -> x50, starting transfers between devices: 33.1 us -> 36.7 us  [exchange(): lax.ppermute(a, axis, [(i, i ^ bit) for i in range(lax.axis_size(axis))])]
    dot_general x8 -> x6, matrix products: 33 us -> 34.3 us  [over_rows(): lax.dot_general(left, right, (((0,), (0,)), ((), ())), preferred_element_...]
  transfers between devices with their start and end apart: 65 -> 68, of which waited for: 22 -> 23; matrix products, arithmetic and copies ran while one was open for 13% -> 12% of each run, Pallas kernels for 11% -> 12%
where the time goes in v3:
time: 552 us; the launch traced here: 546 us
  waiting for transfers between devices  214 us (39%)
  Pallas kernels  144 us (26%)
  starting transfers between devices  96.1 us (17%)
  matrix products  34.3 us (6%)
  other arithmetic  29 us (5%)
  local copies, waits for them, and re-layouts  26.6 us (5%)
    ppermute x50, waiting for transfers between devices, exchange(): lax.ppermute(a, axis, [(i, i ^ bit) for i in range(lax.axis_size(axis))])  162 us
    pallas_call x2, Pallas kernels, run_backward(): pl.pallas_call(functools.partial(backward_kernel, seq=seq, inner=inner, i...  66.1 us
    ppermute x18, starting transfers between devices, exchange_z(): return lax.ppermute(a, ('dp', 'tensor'), pairs)  59.4 us
    pallas_call x2, Pallas kernels, run_forward(): pl.pallas_call(functools.partial(forward_kernel, seq=seq, inner=inner, he...  52.9 us
    ppermute x18, waiting for transfers between devices, exchange_z(): return lax.ppermute(a, ('dp', 'tensor'), pairs)  52.2 us
    ppermute x50, starting transfers between devices, exchange(): lax.ppermute(a, axis, [(i, i ^ bit) for i in range(lax.axis_size(axis))])  36.7 us
    dot_general x6, matrix products, over_rows(): lax.dot_general(left, right, (((0,), (0,)), ((), ())), preferred_element_...  34.3 us
    pallas_call x2, Pallas kernels, run_middle(): pl.pallas_call(functools.partial(middle_kernel, seq=seq, inner=inner, inn...  25.3 us
  transfers between devices with their start and end apart: 68, of which 23 were waited for; matrix products, arithmetic and copies ran while one was open for 12% of the time, Pallas kernels for 12%

profile of v3, /device:TPU:0, one launch (start us, length us, event | category | flops | bytes accessed | tf_op | source)
XLA Modules:
  0.0 546.0 jit_solution(3583533893185841369)
XLA Ops:
  3.7 1.4 concatenate.79
  5.2 5.1 collective-permute-start.11
  11.0 1.6 collective-permute-start.17
  15.6 1.7 fusion.30
  20.5 2.5 broadcast_in_dim.51.refs_5_
  25.0 3.8 collective-permute-start.14
  29.5 1.6 collective-permute-start.4
  31.4 3.1 collective-permute-done.4
  34.4 1.7 collective-permute-start.20
  36.4 15.6 %collective-permute-start.6 = (bf16[2,512,128]{2,1,0:T(8,128)(2,1)S(1)}, bf16[2,512,128]{2,1,0:T(8,128)(2,1)S(1)}, u32[]{:S(2)}, u32[]{:S(2)}) collective-permute-start(bf16[2,512,128]{2,1,0:T(8,128)(2,1)S(1)} %get-tuple-element.216), channel_id=1, source_target_pairs={{0,16},{1,25},{2,18},{3,27},{4,20},{5,29},{6,22},{7,31},{8,24},{9,... | collective-permute-start | bytes 786440 | tf_op jit(solution)/shard_map/ppermute | solution.py:678
  52.0 9.1 %collective-permute-done.15 = bf16[2,528,128]{2,1,0:T(8,128)(2,1)S(1)} collective-permute-done((bf16[2,528,128]{2,1,0:T(8,128)(2,1)S(1)}, bf16[2,528,128]{2,1,0:T(8,128)(2,1)S(1)}, u32[]{:S(2)}, u32[]{:S(2)}) %collective-permute-start.15) | collective-permute-done | bytes 270368 | tf_op jit(solution)/shard_map/ppermute | solution.py:678
  61.1 2.4 collective-permute-start.5
  63.7 3.1 collective-permute-done.6
  66.8 7.0 %collective-permute-done.7 = bf16[2,512,128]{2,1,0:T(8,128)(2,1)S(1)} collective-permute-done((bf16[2,512,128]{2,1,0:T(8,128)(2,1)S(1)}, bf16[2,512,128]{2,1,0:T(8,128)(2,1)S(1)}, u32[]{:S(2)}, u32[]{:S(2)}) %collective-permute-start.7) | collective-permute-done | bytes 262176 | tf_op jit(solution)/shard_map/ppermute | solution.py:678
  73.8 1.5 collective-permute-start.1
  75.3 1.5 collective-permute-start.18
  78.0 10.9 %collective-permute-done.18 = bf16[3,768,128]{2,1,0:T(8,128)(2,1)S(1)} collective-permute-done((bf16[3,768,128]{2,1,0:T(8,128)(2,1)S(1)}, bf16[3,768,128]{2,1,0:T(8,128)(2,1)S(1)}, u32[]{:S(2)}, u32[]{:S(2)}) %collective-permute-start.18) | collective-permute-done | bytes 589856 | tf_op jit(solution)/shard_map/ppermute | solution.py:611
  90.8 51.6 %collective-permute-done.9.refs_2_ = bf16[2048,256]{1,0:T(8,128)(2,1)S(1)} collective-permute-done((bf16[2048,256]{1,0:T(8,128)(2,1)S(1)}, bf16[2048,256]{1,0:T(8,128)(2,1)S(1)}, u32[]{:S(2)}, u32[]{:S(2)}) %collective-permute-start.9) | collective-permute-done | bytes 1048608 | tf_op jit(solution)/shard_map/ppermute | solution.py:611
  143.6 1.6 copy-done.3
  145.2 30.4 %mixer_forward.2 = (bf16[4096,1024]{1,0:T(8,128)(2,1)}, f32[512,4096]{1,0:T(8,128)}, f32[512,4096]{1,0:T(8,128)}, f32[512,4096]{1,0:T(8,128)}, f32[512,4096]{1,0...) custom-call(s32[2]{0:T(128)S(1)} %copy-done.2, ...), custom_call_target="tpu_custom_call" | custom-call | tf_op jit(solution)/shard_map/mixer_forward/pallas_call | solution.py:458
  175.7 1.5 collective-permute-start.23
  177.6 22.5 %mixer_forward.3 = (bf16[4096,1024]{1,0:T(8,128)(2,1)}, f32[512,4096]{1,0:T(8,128)}, f32[512,4096]{1,0:T(8,128)}, f32[512,4096]{1,0:T(8,128)}, f32[512,4096]{1,0...) custom-call(s32[2]{0:T(128)S(1)} %copy-done.2, ...), custom_call_target="tpu_custom_call", output_to_operand_aliasing={{0}: (9, {}), {1}: (10, {}), {2}: (11, {}), {3}: (12, {}), ... | custom-call | tf_op jit(solution)/shard_map/mixer_forward/pallas_call | solution.py:458
  200.5 1.5 collective-permute-start.29
  202.1 2.1 collective-permute-done.29
  205.2 13.1 %mixer_middle.2 = (bf16[4096,512]{1,0:T(8,128)(2,1)}, f32[512,4096]{1,0:T(8,128)}, bf16[2048,256]{1,0:T(8,128)(2,1)S(1)}, bf16[2048,256]{1,0:T(8,128)(2,1)}, bf1...) custom-call(s32[2]{0:T(128)S(1)} %copy-done.2, ...), custom_call_target="tpu_custom_call" | custom-call | tf_op jit(solution)/shard_map/mixer_middle/pallas_call | solution.py:501
  220.2 12.2 %mixer_middle.3 = (bf16[4096,512]{1,0:T(8,128)(2,1)}, f32[512,4096]{1,0:T(8,128)}, bf16[2048,256]{1,0:T(8,128)(2,1)S(1)}, bf16[2048,256]{1,0:T(8,128)(2,1)}, bf1...) custom-call(s32[2]{0:T(128)S(1)} %copy-done.2, ...), custom_call_target="tpu_custom_call", output_to_operand_aliasing={{0}: (9, {}), {1}: (10, {})} | custom-call | tf_op jit(solution)/shard_map/mixer_middle/pallas_call | solution.py:501
  233.4 3.6 convolution_bitcast_fusion.3
  237.1 2.9 convolution_bitcast_fusion
  240.0 2.9 convolution_bitcast_fusion.1
  242.9 2.9 convolution_bitcast_fusion.2
  248.1 2.2 collective-permute-done.42
  250.3 37.5 %mixer_backward.2 = (bf16[4096,768]{1,0:T(8,128)(2,1)}, bf16[4096,640]{1,0:T(8,128)(2,1)}, bf16[2048,256]{1,0:T(8,128)(2,1)}, bf16[2048,256]{1,0:T(8,128)(2,1)},...) custom-call(s32[2]{0:T(128)S(1)} %copy-done.2, ...), custom_call_target="tpu_custom_call" | custom-call | tf_op jit(solution)/shard_map/mixer_backward/pallas_call | solution.py:559
  287.8 28.6 %mixer_backward.3 = (bf16[4096,768]{1,0:T(8,128)(2,1)}, bf16[4096,640]{1,0:T(8,128)(2,1)}, bf16[2048,256]{1,0:T(8,128)(2,1)}, bf16[2048,256]{1,0:T(8,128)(2,1)},...) custom-call(s32[2]{0:T(128)S(1)} %copy-done.2, ...), custom_call_target="tpu_custom_call", output_to_operand_aliasing={{0}: (21, {}), {1}: (22, {})} | custom-call | tf_op jit(solution)/shard_map/mixer_backward/pallas_call | solution.py:559
  316.4 10.7 %fusion.33 = f32[1024,640]{1,0:T(8,128)S(1)} fusion(bf16[4096,1024]{1,0:T(8,128)(2,1)} %get-tuple-element.140, bf16[4096,640]{1,0:T(8,128)(2,1)} %get-tuple-element.142), kind=kOutput, calls=%fused_computation.153 | convolution fusion | flops 5368709120 | bytes 16252928 | tf_op jit(solution)/shard_map/dot_general | solution.py:781
  327.2 1.5 copy-done.21
  329.6 20.8 %collective-permute-start.57 = (bf16[2,128,640]{2,1,0:T(8,128)(2,1)}, bf16[2,128,640]{2,1,0:T(8,128)(2,1)}, u32[]{:S(2)}, u32[]{:S(2)}) collective-permute-start(bf16[2,128,640]{2,1,0:T(8,128)(2,1)} %get-tuple-element.172), channel_id=1, source_target_pairs={{0,24},{1,9},{2,26},{3,11},{4,28},{5,13},{6,30},{7,15},{8,16},{9,1... | collective-permute-start | bytes 983048 | tf_op jit(solution)/shard_map/ppermute | solution.py:678
  350.9 2.4 add_reduce_fusion
  353.4 11.3 %fusion.32 = f32[1024,768]{1,0:T(8,128)S(1)} fusion(bf16[4096,1024]{1,0:T(8,128)(2,1)} %get-tuple-element.140, bf16[4096,768]{1,0:T(8,128)(2,1)} %get-tuple-element.141), kind=kOutput, calls=%fused_computation.152 | convolution fusion | flops 6442450944 | bytes 17825792 | tf_op jit(solution)/shard_map/dot_general | solution.py:781
  365.5 2.4 collective-permute-start.48
  367.9 1.4 collective-permute-start.49
  370.8 3.1 collective-permute-done.49
  374.0 1.6 collective-permute-start.51
  378.3 3.0 collective-permute-start.64
  384.6 1.4 fusion.3
  386.1 3.4 collective-permute-done.64
  389.4 1.6 collective-permute-start.53
  391.1 15.5 %collective-permute-done.65 = bf16[2,128,512]{2,1,0:T(8,128)(2,1)} collective-permute-done((bf16[2,128,512]{2,1,0:T(8,128)(2,1)}, bf16[2,128,512]{2,1,0:T(8,128)(2,1)}, u32[]{:S(2)}, u32[]{:S(2)}) %collective-permute-start.65) | collective-permute-done | bytes 262176 | tf_op jit(solution)/shard_map/ppermute | solution.py:678
  406.6 1.8 collective-permute-start.60
  410.1 3.0 collective-permute-done.60
  417.2 1.5 collective-permute-start.63
  418.7 1.8 bitcast_add_fusion
  420.6 2.2 collective-permute-start.54
  422.9 2.9 collective-permute-start.55
  426.0 1.4 slice_add_fusion
  428.7 1.7 collective-permute-start.25
  430.4 12.5 %collective-permute-done.55 = bf16[128,768]{1,0:T(8,128)(2,1)S(1)} collective-permute-done((bf16[128,768]{1,0:T(8,128)(2,1)S(1)}, bf16[128,768]{1,0:T(8,128)(2,1)S(1)}, u32[]{:S(2)}, u32[]{:S(2)}) %collective-permute-start.55) | collective-permute-done | bytes 196640 | tf_op jit(solution)/shard_map/ppermute | solution.py:678
  444.5 1.6 add_convert_fusion.3
  448.2 1.8 collective-permute-done.44
  451.3 21.8 %collective-permute-done.27 = bf16[2048,256]{1,0:T(8,128)(2,1)S(1)} collective-permute-done((bf16[2048,256]{1,0:T(8,128)(2,1)S(1)}, bf16[2048,256]{1,0:T(8,128)(2,1)S(1)}, u32[]{:S(2)}, u32[]{:S(2)}) %collective-permute-start.27) | collective-permute-done | bytes 1048608 | tf_op jit(solution)/shard_map/ppermute | solution.py:611
  475.7 19.9 %collective-permute-done.33 = bf16[2048,256]{1,0:T(8,128)(2,1)S(1)} collective-permute-done((bf16[2048,256]{1,0:T(8,128)(2,1)S(1)}, bf16[2048,256]{1,0:T(8,128)(2,1)S(1)}, u32[]{:S(2)}, u32[]{:S(2)}) %collective-permute-start.33) | collective-permute-done | bytes 1048608 | tf_op jit(solution)/shard_map/ppermute | solution.py:611
  497.2 2.0 fusion
  499.1 18.9 %collective-permute-done.39 = bf16[2048,256]{1,0:T(8,128)(2,1)S(1)} collective-permute-done((bf16[2048,256]{1,0:T(8,128)(2,1)S(1)}, bf16[2048,256]{1,0:T(8,128)(2,1)S(1)}, u32[]{:S(2)}, u32[]{:S(2)}) %collective-permute-start.39) | collective-permute-done | bytes 1048608 | tf_op jit(solution)/shard_map/ppermute | solution.py:611
  518.4 21.3 %collective-permute-done.45 = bf16[2048,256]{1,0:T(8,128)(2,1)S(1)} collective-permute-done((bf16[2048,256]{1,0:T(8,128)(2,1)S(1)}, bf16[2048,256]{1,0:T(8,128)(2,1)S(1)}, u32[]{:S(2)}, u32[]{:S(2)}) %collective-permute-start.45) | collective-permute-done | bytes 1048608 | tf_op jit(solution)/shard_map/ppermute | solution.py:611
  541.3 4.5 maximum_add_fusion.1
  (258 shorter events, 52.9 us)
Async XLA Ops:
  5.2 23.6 %collective-permute-start.11 = (bf16[768,128]{1,0:T(8,128)(2,1)S(1)}, bf16[768,128]{1,0:T(8,128)(2,1)S(1)}, u32[]{:S(2)}, u32[]{:S(2)}) collective-permute-start(bf16[768,128]{1,0:T(8,128)(2,1)S(1)} %get-tuple-element.210), channel_id=1, source_target_pairs={{0,24},{1,9},{2,26},{3,11},{4,28},{5,13},{6,30},{7,15},{8,16},{9,1... | collective-permute-start | bytes 589832 | tf_op jit(solution)/shard_map/ppermute | solution.py:678
  10.3 18.5 %collective-permute-start.12 = (bf16[768,128]{1,0:T(8,128)(2,1)S(1)}, bf16[768,128]{1,0:T(8,128)(2,1)S(1)}, u32[]{:S(2)}, u32[]{:S(2)}) collective-permute-start(bf16[768,128]{1,0:T(8,128)(2,1)S(1)} %get-tuple-element.210), channel_id=1, source_target_pairs={{0,16},{1,25},{2,18},{3,27},{4,20},{5,29},{6,22},{7,31},{8,24},{9,... | collective-permute-start | bytes 589832 | tf_op jit(solution)/shard_map/ppermute | solution.py:678
  10.3 19.2 %collective-permute-start.13 = (bf16[768,128]{1,0:T(8,128)(2,1)S(1)}, bf16[768,128]{1,0:T(8,128)(2,1)S(1)}, u32[]{:S(2)}, u32[]{:S(2)}) collective-permute-start(bf16[768,128]{1,0:T(8,128)(2,1)S(1)} %get-tuple-element.210), channel_id=1, source_target_pairs={{0,8},{1,17},{2,10},{3,19},{4,12},{5,21},{6,14},{7,23},{8,0},{9,25... | collective-permute-start | bytes 589832 | tf_op jit(solution)/shard_map/ppermute | solution.py:678
  11.0 66.5 %collective-permute-start.17 = (bf16[768,128]{1,0:T(8,128)(2,1)S(1)}, bf16[768,128]{1,0:T(8,128)(2,1)S(1)}, u32[]{:S(2)}, u32[]{:S(2)}) collective-permute-start(bf16[768,128]{1,0:T(8,128)(2,1)S(1)} %get-tuple-element.210), channel_id=1, source_target_pairs={{0,4},{4,0},{8,12},{12,8},{16,20},{20,16},{24,28},{28,24},{1,5},{5... | collective-permute-start | bytes 589832 | tf_op jit(solution)/shard_map/ppermute | solution.py:611
  13.3 7.3 %collective-permute-start.3 = (bf16[528,128]{1,0:T(8,128)(2,1)}, bf16[528,128]{1,0:T(8,128)(2,1)}, u32[]{:S(2)}, u32[]{:S(2)}) collective-permute-start(bf16[528,128]{1,0:T(8,128)(2,1)} %get-tuple-element.212), channel_id=1, source_target_pairs={{0,4},{4,0},{8,12},{12,8},{16,20},{20,16},{24,28},{28,24},{1,5},{5... | collective-permute-start | bytes 405512 | tf_op jit(solution)/shard_map/ppermute | solution.py:611
  25.0 11.4 %collective-permute-start.14 = (bf16[2,528,128]{2,1,0:T(8,128)(2,1)S(1)}, bf16[2,528,128]{2,1,0:T(8,128)(2,1)S(1)}, u32[]{:S(2)}, u32[]{:S(2)}) collective-permute-start(bf16[2,528,128]{2,1,0:T(8,128)(2,1)S(1)} %get-tuple-element.214), channel_id=1, source_target_pairs={{0,24},{1,9},{2,26},{3,11},{4,28},{5,13},{6,30},{7,15},{8,16},{9,1... | collective-permute-start | bytes 811016 | tf_op jit(solution)/shard_map/ppermute | solution.py:678
  28.8 32.2 %collective-permute-start.15 = (bf16[2,528,128]{2,1,0:T(8,128)(2,1)S(1)}, bf16[2,528,128]{2,1,0:T(8,128)(2,1)S(1)}, u32[]{:S(2)}, u32[]{:S(2)}) collective-permute-start(bf16[2,528,128]{2,1,0:T(8,128)(2,1)S(1)} %get-tuple-element.214), channel_id=1, source_target_pairs={{0,16},{1,25},{2,18},{3,27},{4,20},{5,29},{6,22},{7,31},{8,24},{9,... | collective-permute-start | bytes 811016 | tf_op jit(solution)/shard_map/ppermute | solution.py:678
  28.8 32.2 %collective-permute-start.16 = (bf16[2,528,128]{2,1,0:T(8,128)(2,1)S(1)}, bf16[2,528,128]{2,1,0:T(8,128)(2,1)S(1)}, u32[]{:S(2)}, u32[]{:S(2)}) collective-permute-start(bf16[2,528,128]{2,1,0:T(8,128)(2,1)S(1)} %get-tuple-element.214), channel_id=1, source_target_pairs={{0,8},{1,17},{2,10},{3,19},{4,12},{5,21},{6,14},{7,23},{8,0},{9,25... | collective-permute-start | bytes 811016 | tf_op jit(solution)/shard_map/ppermute | solution.py:678
  29.5 5.0 collective-permute-start.4
  34.4 55.6 %collective-permute-start.20 = (bf16[2048,256]{1,0:T(8,128)(2,1)S(1)}, bf16[2048,256]{1,0:T(8,128)(2,1)S(1)}, u32[]{:S(2)}, u32[]{:S(2)}) collective-permute-start(bf16[2048,256]{1,0:T(8,128)(2,1)S(1)} %get-tuple-element.178.refs_0_), channel_id=1, source_target_pairs={{0,2},{1,3},{2,0},{3,1},{4,6},{5,7},{6,4},{7,5},{8,10},{9,11},{10,... | collective-permute-start | bytes 3145736 | tf_op jit(solution)/shard_map/ppermute | solution.py:611
  36.4 30.3 %collective-permute-start.6 = (bf16[2,512,128]{2,1,0:T(8,128)(2,1)S(1)}, bf16[2,512,128]{2,1,0:T(8,128)(2,1)S(1)}, u32[]{:S(2)}, u32[]{:S(2)}) collective-permute-start(bf16[2,512,128]{2,1,0:T(8,128)(2,1)S(1)} %get-tuple-element.216), channel_id=1, source_target_pairs={{0,16},{1,25},{2,18},{3,27},{4,20},{5,29},{6,22},{7,31},{8,24},{9,... | collective-permute-start | bytes 786440 | tf_op jit(solution)/shard_map/ppermute | solution.py:678
  61.0 12.8 %collective-permute-start.7 = (bf16[2,512,128]{2,1,0:T(8,128)(2,1)S(1)}, bf16[2,512,128]{2,1,0:T(8,128)(2,1)S(1)}, u32[]{:S(2)}, u32[]{:S(2)}) collective-permute-start(bf16[2,512,128]{2,1,0:T(8,128)(2,1)S(1)} %get-tuple-element.216), channel_id=1, source_target_pairs={{0,8},{1,17},{2,10},{3,19},{4,12},{5,21},{6,14},{7,23},{8,0},{9,25... | collective-permute-start | bytes 786440 | tf_op jit(solution)/shard_map/ppermute | solution.py:678
  61.1 14.3 %collective-permute-start.5 = (bf16[2,512,128]{2,1,0:T(8,128)(2,1)S(1)}, bf16[2,512,128]{2,1,0:T(8,128)(2,1)S(1)}, u32[]{:S(2)}, u32[]{:S(2)}) collective-permute-start(bf16[2,512,128]{2,1,0:T(8,128)(2,1)S(1)} %get-tuple-element.216), channel_id=1, source_target_pairs={{0,24},{1,9},{2,26},{3,11},{4,28},{5,13},{6,30},{7,15},{8,16},{9,1... | collective-permute-start | bytes 786440 | tf_op jit(solution)/shard_map/ppermute | solution.py:678
  66.8 23.9 %collective-permute-start.19 = (bf16[2048,256]{1,0:T(8,128)(2,1)S(1)}, bf16[2048,256]{1,0:T(8,128)(2,1)S(1)}, u32[]{:S(2)}, u32[]{:S(2)}) collective-permute-start(bf16[2048,256]{1,0:T(8,128)(2,1)S(1)} %get-tuple-element.178.refs_0_), channel_id=1, source_target_pairs={{0,1},{1,0},{2,3},{3,2},{4,5},{5,4},{6,7},{7,6},{8,9},{9,8},{10,11... | collective-permute-start | bytes 3145736 | tf_op jit(solution)/shard_map/ppermute | solution.py:611
  73.8 68.6 %collective-permute-start.1 = (bf16[4096,256]{1,0:T(8,128)(2,1)S(1)}, bf16[4096,256]{1,0:T(8,128)(2,1)}, u32[]{:S(2)}, u32[]{:S(2)}) collective-permute-start(bf16[4096,256]{1,0:T(8,128)(2,1)S(1)} %copy-done.4), channel_id=1, source_target_pairs={{0,2},{1,3},{2,0},{3,1},{4,6},{5,7},{6,4},{7,5},{8,10},{9,11},{10,... | collective-permute-start | bytes 6291464 | tf_op jit(solution)/shard_map/ppermute | solution.py:611
  75.3 13.5 %collective-permute-start.18 = (bf16[3,768,128]{2,1,0:T(8,128)(2,1)S(1)}, bf16[3,768,128]{2,1,0:T(8,128)(2,1)S(1)}, u32[]{:S(2)}, u32[]{:S(2)}) collective-permute-start(bf16[3,768,128]{2,1,0:T(8,128)(2,1)S(1)} %pad_maximum_fusion.4), channel_id=1, source_target_pairs={{0,4},{4,0},{8,12},{12,8},{16,20},{20,16},{24,28},{28,24},{1,5},{5... | collective-permute-start | bytes 1769480 | tf_op jit(solution)/shard_map/ppermute | solution.py:611
  77.4 65.0 %collective-permute-start.9 = (bf16[2048,256]{1,0:T(8,128)(2,1)S(1)}, bf16[2048,256]{1,0:T(8,128)(2,1)S(1)}, u32[]{:S(2)}, u32[]{:S(2)}) collective-permute-start(bf16[2048,256]{1,0:T(8,128)(2,1)S(1)} %get-tuple-element.179.refs_0_), channel_id=1, source_target_pairs={{0,2},{1,3},{2,0},{3,1},{4,6},{5,7},{6,4},{7,5},{8,10},{9,11},{10,... | collective-permute-start | bytes 3145736 | tf_op jit(solution)/shard_map/ppermute | solution.py:611
  88.9 86.9 %collective-permute-start.8 = (bf16[2048,256]{1,0:T(8,128)(2,1)S(1)}, bf16[2048,256]{1,0:T(8,128)(2,1)}, u32[]{:S(2)}, u32[]{:S(2)}) collective-permute-start(bf16[2048,256]{1,0:T(8,128)(2,1)S(1)} %get-tuple-element.179.refs_0_), channel_id=1, source_target_pairs={{0,1},{1,0},{2,3},{3,2},{4,5},{5,4},{6,7},{7,6},{8,9},{9,8},{10,11... | collective-permute-start | bytes 3145736 | tf_op jit(solution)/shard_map/ppermute | solution.py:611
  90.1 115.1 %collective-permute-start = (bf16[4096,256]{1,0:T(8,128)(2,1)S(1)}, bf16[4096,256]{1,0:T(8,128)(2,1)}, u32[]{:S(2)}, u32[]{:S(2)}) collective-permute-start(bf16[4096,256]{1,0:T(8,128)(2,1)S(1)} %copy-done.4), channel_id=1, source_target_pairs={{0,1},{1,0},{2,3},{3,2},{4,5},{5,4},{6,7},{7,6},{8,9},{9,8},{10,11... | collective-permute-start | bytes 6291464 | tf_op jit(solution)/shard_map/ppermute | solution.py:611
  90.7 52.9 %collective-permute-start.21 = (bf16[2048,256]{1,0:T(8,128)(2,1)S(1)}, bf16[2048,256]{1,0:T(8,128)(2,1)}, u32[]{:S(2)}, u32[]{:S(2)}) collective-permute-start(bf16[2048,256]{1,0:T(8,128)(2,1)S(1)} %collective-permute-done.20.refs_2_), channel_id=1, source_target_pairs={{0,1},{1,0},{2,3},{3,2},{4,5},{5,4},{6,7},{7,6},{8,9},{9,8},{10,11... | collective-permute-start | bytes 3145736 | tf_op jit(solution)/shard_map/ppermute | solution.py:611
  142.4 34.9 %collective-permute-start.10 = (bf16[2048,256]{1,0:T(8,128)(2,1)S(1)}, bf16[2048,256]{1,0:T(8,128)(2,1)}, u32[]{:S(2)}, u32[]{:S(2)}) collective-permute-start(bf16[2048,256]{1,0:T(8,128)(2,1)S(1)} %collective-permute-done.9.refs_2_), channel_id=1, source_target_pairs={{0,1},{1,0},{2,3},{3,2},{4,5},{5,4},{6,7},{7,6},{8,9},{9,8},{10,11... | collective-permute-start | bytes 3145736 | tf_op jit(solution)/shard_map/ppermute | solution.py:611
  142.4 62.8 %collective-permute-start.2 = (bf16[4096,256]{1,0:T(8,128)(2,1)}, bf16[4096,256]{1,0:T(8,128)(2,1)}, u32[]{:S(2)}, u32[]{:S(2)}) collective-permute-start(bf16[4096,256]{1,0:T(8,128)(2,1)} %collective-permute-done.1.refs_2_), channel_id=1, source_target_pairs={{0,1},{1,0},{2,3},{3,2},{4,5},{5,4},{6,7},{7,6},{8,9},{9,8},{10,11... | collective-permute-start | bytes 6291464 | tf_op jit(solution)/shard_map/ppermute | solution.py:611
  175.6 24.5 %collective-permute-start.22 = (f32[1,2048]{1,0:T(1,128)S(1)}, f32[1,2048]{1,0:T(1,128)S(1)}, u32[]{:S(2)}, u32[]{:S(2)}) collective-permute-start(f32[1,2048]{1,0:T(1,128)S(1)} %get-tuple-element.96), channel_id=1, source_target_pairs={{0,1},{1,0},{2,3},{3,2},{4,5},{5,4},{6,7},{7,6},{8,9},{9,8},{10,11... | collective-permute-start | bytes 24584 | tf_op jit(solution)/shard_map/ppermute | solution.py:611
  175.7 24.8 %collective-permute-start.23 = (f32[1,2048]{1,0:T(1,128)S(1)}, f32[1,2048]{1,0:T(1,128)S(1)}, u32[]{:S(2)}, u32[]{:S(2)}) collective-permute-start(f32[1,2048]{1,0:T(1,128)S(1)} %get-tuple-element.96), channel_id=1, source_target_pairs={{0,2},{1,3},{2,0},{3,1},{4,6},{5,7},{6,4},{7,5},{8,10},{9,11},{10,... | collective-permute-start | bytes 24584 | tf_op jit(solution)/shard_map/ppermute | solution.py:611
  177.3 24.8 %collective-permute-start.24 = (f32[1,2048]{1,0:T(1,128)S(1)}, f32[1,2048]{1,0:T(1,128)S(1)}, u32[]{:S(2)}, u32[]{:S(2)}) collective-permute-start(f32[1,2048]{1,0:T(1,128)S(1)} %get-tuple-element.96), channel_id=1, source_target_pairs={{0,3},{1,2},{2,1},{3,0},{4,7},{5,6},{6,5},{7,4},{8,11},{9,10},{10,... | collective-permute-start | bytes 24584 | tf_op jit(solution)/shard_map/ppermute | solution.py:611
  200.5 3.7 collective-permute-start.29
  218.3 28.8 %collective-permute-start.34 = (f32[1,2048]{1,0:T(1,128)S(1)}, f32[1,2048]{1,0:T(1,128)S(1)}, u32[]{:S(2)}, u32[]{:S(2)}) collective-permute-start(f32[1,2048]{1,0:T(1,128)S(1)} %get-tuple-element.118), channel_id=1, source_target_pairs={{0,1},{1,0},{2,3},{3,2},{4,5},{5,4},{6,7},{7,6},{8,9},{9,8},{10,11... | collective-permute-start | bytes 24584 | tf_op jit(solution)/shard_map/ppermute | solution.py:611
  218.5 29.6 %collective-permute-start.35 = (f32[1,2048]{1,0:T(1,128)S(1)}, f32[1,2048]{1,0:T(1,128)S(1)}, u32[]{:S(2)}, u32[]{:S(2)}) collective-permute-start(f32[1,2048]{1,0:T(1,128)S(1)} %get-tuple-element.118), channel_id=1, source_target_pairs={{0,2},{1,3},{2,0},{3,1},{4,6},{5,7},{6,4},{7,5},{8,10},{9,11},{10,... | collective-permute-start | bytes 24584 | tf_op jit(solution)/shard_map/ppermute | solution.py:611
  219.0 29.0 %collective-permute-start.36 = (f32[1,2048]{1,0:T(1,128)S(1)}, f32[1,2048]{1,0:T(1,128)S(1)}, u32[]{:S(2)}, u32[]{:S(2)}) collective-permute-start(f32[1,2048]{1,0:T(1,128)S(1)} %get-tuple-element.118), channel_id=1, source_target_pairs={{0,3},{1,2},{2,1},{3,0},{4,7},{5,6},{6,5},{7,4},{8,11},{9,10},{10,... | collective-permute-start | bytes 24584 | tf_op jit(solution)/shard_map/ppermute | solution.py:611
  232.4 15.7 %collective-permute-start.40 = (f32[1,2048]{1,0:T(1,128)S(1)}, f32[1,2048]{1,0:T(1,128)S(1)}, u32[]{:S(2)}, u32[]{:S(2)}) collective-permute-start(f32[1,2048]{1,0:T(1,128)S(1)} %get-tuple-element.123), channel_id=1, source_target_pairs={{0,1},{1,0},{2,3},{3,2},{4,5},{5,4},{6,7},{7,6},{8,9},{9,8},{10,11... | collective-permute-start | bytes 24584 | tf_op jit(solution)/shard_map/ppermute | solution.py:611
  232.9 15.2 %collective-permute-start.41 = (f32[1,2048]{1,0:T(1,128)S(1)}, f32[1,2048]{1,0:T(1,128)S(1)}, u32[]{:S(2)}, u32[]{:S(2)}) collective-permute-start(f32[1,2048]{1,0:T(1,128)S(1)} %get-tuple-element.123), channel_id=1, source_target_pairs={{0,2},{1,3},{2,0},{3,1},{4,6},{5,7},{6,4},{7,5},{8,10},{9,11},{10,... | collective-permute-start | bytes 24584 | tf_op jit(solution)/shard_map/ppermute | solution.py:611
  247.1 3.2 collective-permute-start.42
  329.6 54.3 %collective-permute-start.57 = (bf16[2,128,640]{2,1,0:T(8,128)(2,1)}, bf16[2,128,640]{2,1,0:T(8,128)(2,1)}, u32[]{:S(2)}, u32[]{:S(2)}) collective-permute-start(bf16[2,128,640]{2,1,0:T(8,128)(2,1)} %get-tuple-element.172), channel_id=1, source_target_pairs={{0,24},{1,9},{2,26},{3,11},{4,28},{5,13},{6,30},{7,15},{8,16},{9,1... | collective-permute-start | bytes 983048 | tf_op jit(solution)/shard_map/ppermute | solution.py:678
  350.4 33.7 %collective-permute-start.58 = (bf16[2,128,640]{2,1,0:T(8,128)(2,1)}, bf16[2,128,640]{2,1,0:T(8,128)(2,1)}, u32[]{:S(2)}, u32[]{:S(2)}) collective-permute-start(bf16[2,128,640]{2,1,0:T(8,128)(2,1)} %get-tuple-element.174), channel_id=1, source_target_pairs={{0,16},{1,25},{2,18},{3,27},{4,20},{5,29},{6,22},{7,31},{8,24},{9,... | collective-permute-start | bytes 983048 | tf_op jit(solution)/shard_map/ppermute | solution.py:678
  353.4 11.4 %collective-permute-start.46 = (f32[5904]{0:T(1024)S(1)}, f32[5904]{0:T(1024)S(1)}, u32[]{:S(2)}, u32[]{:S(2)}) collective-permute-start(f32[5904]{0:T(1024)S(1)} %concatenate.102), channel_id=1, source_target_pairs={{0,4},{4,0},{8,12},{12,8},{16,20},{20,16},{24,28},{28,24},{1,5},{5... | collective-permute-start | bytes 70856 | tf_op jit(solution)/shard_map/ppermute | solution.py:611
  364.8 5.4 collective-permute-start.47
  365.5 5.4 collective-permute-start.48
  367.9 6.0 %collective-permute-start.49 = (f32[5904]{0:T(1024)S(1)}, f32[5904]{0:T(1024)S(1)}, u32[]{:S(2)}, u32[]{:S(2)}) collective-permute-start(f32[5904]{0:T(1024)S(1)} %add.354), channel_id=1, source_target_pairs={{0,24},{4,28},{8,16},{12,20},{16,8},{20,12},{24,0},{28,4},{1,25},{... | collective-permute-start | bytes 70856 | tf_op jit(solution)/shard_map/ppermute | solution.py:611
  370.2 14.2 %collective-permute-start.59 = (bf16[2,128,640]{2,1,0:T(8,128)(2,1)S(1)}, bf16[2,128,640]{2,1,0:T(8,128)(2,1)S(1)}, u32[]{:S(2)}, u32[]{:S(2)}) collective-permute-start(bf16[2,128,640]{2,1,0:T(8,128)(2,1)S(1)} %copy-done.23), channel_id=1, source_target_pairs={{0,8},{1,17},{2,10},{3,19},{4,12},{5,21},{6,14},{7,23},{8,0},{9,25... | collective-permute-start | bytes 983048 | tf_op jit(solution)/shard_map/ppermute | solution.py:678
  374.0 4.3 collective-permute-start.51
  376.1 5.2 collective-permute-start.52
  378.3 11.1 %collective-permute-start.64 = (bf16[2,128,512]{2,1,0:T(8,128)(2,1)}, bf16[2,128,512]{2,1,0:T(8,128)(2,1)}, u32[]{:S(2)}, u32[]{:S(2)}) collective-permute-start(bf16[2,128,512]{2,1,0:T(8,128)(2,1)} %get-tuple-element.175), channel_id=1, source_target_pairs={{0,24},{1,9},{2,26},{3,11},{4,28},{5,13},{6,30},{7,15},{8,16},{9,1... | collective-permute-start | bytes 786440 | tf_op jit(solution)/shard_map/ppermute | solution.py:678
  381.3 25.3 %collective-permute-start.65 = (bf16[2,128,512]{2,1,0:T(8,128)(2,1)}, bf16[2,128,512]{2,1,0:T(8,128)(2,1)}, u32[]{:S(2)}, u32[]{:S(2)}) collective-permute-start(bf16[2,128,512]{2,1,0:T(8,128)(2,1)} %get-tuple-element.177), channel_id=1, source_target_pairs={{0,16},{1,25},{2,18},{3,27},{4,20},{5,29},{6,22},{7,31},{8,24},{9,... | collective-permute-start | bytes 786440 | tf_op jit(solution)/shard_map/ppermute | solution.py:678
  384.0 24.4 %collective-permute-start.66 = (bf16[2,128,512]{2,1,0:T(8,128)(2,1)}, bf16[2,128,512]{2,1,0:T(8,128)(2,1)S(1)}, u32[]{:S(2)}, u32[]{:S(2)}) collective-permute-start(bf16[2,128,512]{2,1,0:T(8,128)(2,1)} %get-tuple-element.176), channel_id=1, source_target_pairs={{0,8},{1,17},{2,10},{3,19},{4,12},{5,21},{6,14},{7,23},{8,0},{9,25... | collective-permute-start | bytes 786440 | tf_op jit(solution)/shard_map/ppermute | solution.py:678
  384.1 60.3 %collective-permute-start.26 = (bf16[2048,256]{1,0:T(8,128)(2,1)}, bf16[2048,256]{1,0:T(8,128)(2,1)}, u32[]{:S(2)}, u32[]{:S(2)}) collective-permute-start(bf16[2048,256]{1,0:T(8,128)(2,1)} %get-tuple-element.100), channel_id=1, source_target_pairs={{0,1},{1,0},{2,3},{3,2},{4,5},{5,4},{6,7},{7,6},{8,9},{9,8},{10,11... | collective-permute-start | bytes 3145736 | tf_op jit(solution)/shard_map/ppermute | solution.py:611
  384.5 61.6 %collective-permute-start.32 = (bf16[2048,256]{1,0:T(8,128)(2,1)}, bf16[2048,256]{1,0:T(8,128)(2,1)S(1)}, u32[]{:S(2)}, u32[]{:S(2)}) collective-permute-start(bf16[2048,256]{1,0:T(8,128)(2,1)} %get-tuple-element.107), channel_id=1, source_target_pairs={{0,1},{1,0},{2,3},{3,2},{4,5},{5,4},{6,7},{7,6},{8,9},{9,8},{10,11... | collective-permute-start | bytes 3145736 | tf_op jit(solution)/shard_map/ppermute | solution.py:611
  389.4 29.3 %collective-permute-start.53 = (bf16[4,128,768]{2,1,0:T(8,128)(2,1)}, bf16[4,128,768]{2,1,0:T(8,128)(2,1)}, u32[]{:S(2)}, u32[]{:S(2)}) collective-permute-start(bf16[4,128,768]{2,1,0:T(8,128)(2,1)} %fusion.1), channel_id=1, source_target_pairs={{0,4},{4,0},{8,12},{12,8},{16,20},{20,16},{24,28},{28,24},{1,5},{5... | collective-permute-start | bytes 2359304 | tf_op jit(solution)/shard_map/ppermute | solution.py:611
  406.6 6.4 %collective-permute-start.60 = (bf16[128,640]{1,0:T(8,128)(2,1)S(1)}, bf16[128,640]{1,0:T(8,128)(2,1)S(1)}, u32[]{:S(2)}, u32[]{:S(2)}) collective-permute-start(bf16[128,640]{1,0:T(8,128)(2,1)S(1)} %fusion.25), channel_id=1, source_target_pairs={{0,4},{4,0},{8,12},{12,8},{16,20},{20,16},{24,28},{28,24},{1,5},{5... | collective-permute-start | bytes 491528 | tf_op jit(solution)/shard_map/ppermute | solution.py:611
  409.8 5.0 collective-permute-start.67
  415.6 7.3 %collective-permute-start.61 = (f32[32,384]{1,0:T(8,128)}, f32[32,384]{1,0:T(8,128)}, u32[]{:S(2)}, u32[]{:S(2)}) collective-permute-start(f32[32,384]{1,0:T(8,128)} %get-tuple-element.219), channel_id=1, source_target_pairs={{0,1},{1,0},{2,3},{3,2},{4,5},{5,4},{6,7},{7,6},{8,9},{9,8},{10,11... | collective-permute-start | bytes 147464 | tf_op jit(solution)/shard_map/ppermute | solution.py:611
  417.2 8.6 %collective-permute-start.63 = (f32[32,384]{1,0:T(8,128)S(1)}, f32[32,384]{1,0:T(8,128)S(1)}, u32[]{:S(2)}, u32[]{:S(2)}) collective-permute-start(f32[32,384]{1,0:T(8,128)S(1)} %bitcast_add_fusion.6), channel_id=1, source_target_pairs={{0,2},{1,3},{2,0},{3,1},{4,6},{5,7},{6,4},{7,5},{8,10},{9,11},{10,... | collective-permute-start | bytes 147464 | tf_op jit(solution)/shard_map/ppermute | solution.py:611
  420.6 8.1 %collective-permute-start.54 = (bf16[128,768]{1,0:T(8,128)(2,1)S(1)}, bf16[128,768]{1,0:T(8,128)(2,1)S(1)}, u32[]{:S(2)}, u32[]{:S(2)}) collective-permute-start(bf16[128,768]{1,0:T(8,128)(2,1)S(1)} %get-tuple-element.180), channel_id=1, source_target_pairs={{0,24},{1,9},{2,26},{3,11},{4,28},{5,13},{6,30},{7,15},{8,16},{9,1... | collective-permute-start | bytes 589832 | tf_op jit(solution)/shard_map/ppermute | solution.py:678
  422.9 20.0 %collective-permute-start.55 = (bf16[128,768]{1,0:T(8,128)(2,1)S(1)}, bf16[128,768]{1,0:T(8,128)(2,1)S(1)}, u32[]{:S(2)}, u32[]{:S(2)}) collective-permute-start(bf16[128,768]{1,0:T(8,128)(2,1)S(1)} %get-tuple-element.182), channel_id=1, source_target_pairs={{0,16},{1,25},{2,18},{3,27},{4,20},{5,29},{6,22},{7,31},{8,24},{9,... | collective-permute-start | bytes 589832 | tf_op jit(solution)/shard_map/ppermute | solution.py:678
  425.7 17.2 %collective-permute-start.56 = (bf16[128,768]{1,0:T(8,128)(2,1)S(1)}, bf16[128,768]{1,0:T(8,128)(2,1)S(1)}, u32[]{:S(2)}, u32[]{:S(2)}) collective-permute-start(bf16[128,768]{1,0:T(8,128)(2,1)S(1)} %get-tuple-element.181), channel_id=1, source_target_pairs={{0,8},{1,17},{2,10},{3,19},{4,12},{5,21},{6,14},{7,23},{8,0},{9,25... | collective-permute-start | bytes 589832 | tf_op jit(solution)/shard_map/ppermute | solution.py:678
  428.7 22.5 %collective-permute-start.25 = (bf16[2048,256]{1,0:T(8,128)(2,1)S(1)}, bf16[2048,256]{1,0:T(8,128)(2,1)S(1)}, u32[]{:S(2)}, u32[]{:S(2)}) collective-permute-start(bf16[2048,256]{1,0:T(8,128)(2,1)S(1)} %copy-done.29), channel_id=1, source_target_pairs={{0,1},{1,0},{2,3},{3,2},{4,5},{5,4},{6,7},{7,6},{8,9},{9,8},{10,11... | collective-permute-start | bytes 3145736 | tf_op jit(solution)/shard_map/ppermute | solution.py:611
  442.9 31.5 %collective-permute-start.31 = (bf16[2048,256]{1,0:T(8,128)(2,1)S(1)}, bf16[2048,256]{1,0:T(8,128)(2,1)S(1)}, u32[]{:S(2)}, u32[]{:S(2)}) collective-permute-start(bf16[2048,256]{1,0:T(8,128)(2,1)S(1)} %copy-done.30), channel_id=1, source_target_pairs={{0,1},{1,0},{2,3},{3,2},{4,5},{5,4},{6,7},{7,6},{8,9},{9,8},{10,11... | collective-permute-start | bytes 3145736 | tf_op jit(solution)/shard_map/ppermute | solution.py:611
  442.9 4.1 collective-permute-start.38
  444.4 54.7 %collective-permute-start.37 = (bf16[2048,256]{1,0:T(8,128)(2,1)S(1)}, bf16[2048,256]{1,0:T(8,128)(2,1)S(1)}, u32[]{:S(2)}, u32[]{:S(2)}) collective-permute-start(bf16[2048,256]{1,0:T(8,128)(2,1)S(1)} %copy-done.31), channel_id=1, source_target_pairs={{0,1},{1,0},{2,3},{3,2},{4,5},{5,4},{6,7},{7,6},{8,9},{9,8},{10,11... | collective-permute-start | bytes 3145736 | tf_op jit(solution)/shard_map/ppermute | solution.py:611
  446.1 4.0 collective-permute-start.44
  447.1 26.0 %collective-permute-start.27 = (bf16[2048,256]{1,0:T(8,128)(2,1)S(1)}, bf16[2048,256]{1,0:T(8,128)(2,1)S(1)}, u32[]{:S(2)}, u32[]{:S(2)}) collective-permute-start(bf16[2048,256]{1,0:T(8,128)(2,1)S(1)} %add_convert_fusion.3), channel_id=1, source_target_pairs={{0,2},{1,3},{2,0},{3,1},{4,6},{5,7},{6,4},{7,5},{8,10},{9,11},{10,... | collective-permute-start | bytes 3145736 | tf_op jit(solution)/shard_map/ppermute | solution.py:611
  450.1 45.5 %collective-permute-start.33 = (bf16[2048,256]{1,0:T(8,128)(2,1)S(1)}, bf16[2048,256]{1,0:T(8,128)(2,1)S(1)}, u32[]{:S(2)}, u32[]{:S(2)}) collective-permute-start(bf16[2048,256]{1,0:T(8,128)(2,1)S(1)} %add_convert_fusion.2), channel_id=1, source_target_pairs={{0,2},{1,3},{2,0},{3,1},{4,6},{5,7},{6,4},{7,5},{8,10},{9,11},{10,... | collective-permute-start | bytes 3145736 | tf_op jit(solution)/shard_map/ppermute | solution.py:611
  451.3 67.1 %collective-permute-start.43 = (bf16[2048,256]{1,0:T(8,128)(2,1)S(1)}, bf16[2048,256]{1,0:T(8,128)(2,1)S(1)}, u32[]{:S(2)}, u32[]{:S(2)}) collective-permute-start(bf16[2048,256]{1,0:T(8,128)(2,1)S(1)} %copy-done.32), channel_id=1, source_target_pairs={{0,1},{1,0},{2,3},{3,2},{4,5},{5,4},{6,7},{7,6},{8,9},{9,8},{10,11... | collective-permute-start | bytes 3145736 | tf_op jit(solution)/shard_map/ppermute | solution.py:611
  473.1 44.9 %collective-permute-start.39 = (bf16[2048,256]{1,0:T(8,128)(2,1)S(1)}, bf16[2048,256]{1,0:T(8,128)(2,1)S(1)}, u32[]{:S(2)}, u32[]{:S(2)}) collective-permute-start(bf16[2048,256]{1,0:T(8,128)(2,1)S(1)} %add_convert_fusion.1), channel_id=1, source_target_pairs={{0,2},{1,3},{2,0},{3,1},{4,6},{5,7},{6,4},{7,5},{8,10},{9,11},{10,... | collective-permute-start | bytes 3145736 | tf_op jit(solution)/shard_map/ppermute | solution.py:611
  474.4 65.3 %collective-permute-start.45 = (bf16[2048,256]{1,0:T(8,128)(2,1)S(1)}, bf16[2048,256]{1,0:T(8,128)(2,1)S(1)}, u32[]{:S(2)}, u32[]{:S(2)}) collective-permute-start(bf16[2048,256]{1,0:T(8,128)(2,1)S(1)} %add_convert_fusion), channel_id=1, source_target_pairs={{0,2},{1,3},{2,0},{3,1},{4,6},{5,7},{6,4},{7,5},{8,10},{9,11},{10,... | collective-permute-start | bytes 3145736 | tf_op jit(solution)/shard_map/ppermute | solution.py:611
  (39 other events, 831.0 us)

commit v4 on v3

--- a/solution.py
+++ b/solution.py
@@ -16,6 +16,8 @@
 epsilon = 1e-05
 NEG = -1e30
 LOG2E = 1.4426950408889634
+TENSOR = "tensor"
+DP = "dp"
 
 
 def nn(a, b):
@@ -607,6 +609,36 @@
     )(lengths, *xs, *consts, *saved, squares, stat, *before)
 
 
+def finish_kernel(len_ref, base_ref, own_ref, beside_ref, last_ref, *refs, seq, masked):
+    total = own_ref[...].astype(F32) + beside_ref[...].astype(F32) + last_ref[...].astype(F32)
+    base = base_ref[...].astype(F32)
+    if masked:
+        count = base.shape[0]
+        row = pl.program_id(0) * count + lax.broadcasted_iota(jnp.int32, (count, 1), 0)
+        base = jnp.where(row < len_ref[seq], base, 0.0)
+    refs[-1][...] = (base + total).astype(refs[-1].dtype)
+
+
+def run_finish(seq, lengths, base, parts, kind, before):
+    rows, part = base.shape
+    count = SEQ_LEN // 2
+    joint = pl.BlockSpec((count, part), lambda c, lens: (seq * 2 + c, 0))
+    alone = pl.BlockSpec((count, part), lambda c, lens: (c, 0))
+    return pl.pallas_call(
+        functools.partial(finish_kernel, seq=seq, masked=kind == F32),
+        out_shape=[shape((rows, part), kind)],
+        grid_spec=pltpu.PrefetchScalarGridSpec(
+            num_scalar_prefetch=1,
+            grid=(2,),
+            in_specs=[joint, *[alone] * 3, *[pl.BlockSpec(memory_space=pl.ANY)] * len(before)],
+            out_specs=[joint],
+        ),
+        input_output_aliases={5 + i: i for i in range(len(before))},
+        compiler_params=pltpu.CompilerParams(vmem_limit_bytes=16 << 20),
+        name="finish",
+    )(lengths, base, *parts, *before)
+
+
 def exchange(a, axis, bit):
     return lax.ppermute(a, axis, [(i, i ^ bit) for i in range(lax.axis_size(axis))])
 
@@ -620,22 +652,21 @@
 
 
 def gather_pieces(a):
-    across = exchange(a, "tensor", 2)
-    beside = exchange(a, "tensor", 1)
-    return a, beside, across, exchange(across, "tensor", 1)
+    across = exchange(a, TENSOR, 2)
+    beside = exchange(a, TENSOR, 1)
+    return a, beside, across, exchange(across, TENSOR, 1)
 
 
 def reduce_pieces(pieces, kind=BF16):
     own, beside, across, corner = pieces
-    got_corner = exchange(corner.astype(kind), "tensor", 1)
-    got_beside = exchange(beside.astype(kind), "tensor", 1)
+    got_corner = exchange(corner.astype(kind), TENSOR, 1)
+    got_beside = exchange(beside.astype(kind), TENSOR, 1)
     onward = (across.astype(F32) + got_corner.astype(F32)).astype(kind)
-    last = exchange(onward, "tensor", 2).astype(F32)
-    return own.astype(F32) + got_beside.astype(F32) + last
+    return own, got_beside, exchange(onward, TENSOR, 2)
 
 
 def place():
-    index = lax.axis_index("dp")
+    index = lax.axis_index(DP)
     return index // 2, index % 2
 
 
@@ -659,8 +690,8 @@
 
 
 def gather_other_way(a):
-    tensor = lax.axis_index("tensor")
-    whole = jnp.transpose(lax.all_gather(jnp.transpose(a), "dp", axis=0, tiled=True))
+    tensor = lax.axis_index(TENSOR)
+    whole = jnp.transpose(lax.all_gather(jnp.transpose(a), DP, axis=0, tiled=True))
     blocks = whole.reshape(a.shape[0], 4, -1)
     return jnp.concatenate([take(blocks, tensor ^ m, 1) for m in range(4)], 1)
 
@@ -669,17 +700,17 @@
 
 
 def exchange_z(a, turn):
-    count, tensor_count = lax.axis_size("dp"), lax.axis_size("tensor")
+    count, tensor_count = lax.axis_size(DP), lax.axis_size(TENSOR)
     pairs = [
         (d * tensor_count + t, (d ^ (2 * ROUNDS[t % 2][turn])) * tensor_count + t)
         for d in range(count)
         for t in range(tensor_count)
     ]
-    return lax.ppermute(a, ("dp", "tensor"), pairs)
+    return lax.ppermute(a, (DP, TENSOR), pairs)
 
 
 def even_core():
-    return lax.axis_index("tensor") % 2 == 0
+    return lax.axis_index(TENSOR) % 2 == 0
 
 
 def distance(turn):
@@ -692,22 +723,22 @@
 
 def slot_of(m):
     z, _ = place()
-    j = (lax.axis_index("tensor") ^ m) ^ z
+    j = (lax.axis_index(TENSOR) ^ m) ^ z
     return jnp.where(even_core(), (4 - j) % 4, jnp.where(j >= 2, 5 - j, j))
 
 
 def weight_columns(a, extra, ready):
-    if lax.axis_size("dp") != 8:
+    if lax.axis_size(DP) != 8:
         return jnp.pad(gather_other_way(a), ((0, extra), (0, 0))), ready
     cut = round_to(a.shape[0] * 6 // 10, 16)
     first, second = a[:cut], a[cut:]
-    beside = exchange(second, "dp", 1)
+    beside = exchange(second, DP, 1)
     beside, ready = lax.optimization_barrier((beside, ready))
     mine = z_stack(first)
-    other = exchange(first, "dp", 1)
+    other = exchange(first, DP, 1)
     pair = jnp.stack([second, beside])
     both = z_stack(pair)
-    other = jnp.concatenate([other[None], exchange(mine[1:], "dp", 1)], 0)
+    other = jnp.concatenate([other[None], exchange(mine[1:], DP, 1)], 0)
 
     def pick(m):
         slot = slot_of(m)
@@ -721,9 +752,9 @@
 
 
 def hidden_columns(a):
-    if lax.axis_size("dp") != 8:
+    if lax.axis_size(DP) != 8:
         return gather_other_way(a)
-    both = z_stack(jnp.stack([a, exchange(a, "dp", 1)]))
+    both = z_stack(jnp.stack([a, exchange(a, DP, 1)]))
 
     def pick(m):
         low = take(both, slot_of(m), 0)
@@ -734,7 +765,7 @@
 
 def along_z(pick):
     z, _ = place()
-    total = pick(z)
+    total = pick(z).astype(F32)
     for turn in range(3):
         send = pick(z ^ distance(turn)).astype(BF16)
         total = total + exchange_z(send, turn).astype(F32)
@@ -742,31 +773,31 @@
 
 
 def reduce_other_way(a):
-    tensor = lax.axis_index("tensor")
+    tensor = lax.axis_index(TENSOR)
     blocks = a.reshape(4, -1, a.shape[1])
     ordered = jnp.concatenate([take(blocks, tensor ^ m, 0) for m in range(4)], 0)
-    return lax.psum_scatter(ordered, "dp", scatter_dimension=0, tiled=True)
+    return lax.psum_scatter(ordered.astype(F32), DP, scatter_dimension=0, tiled=True)
 
 
 def rows_pair_first(a):
-    if lax.axis_size("dp") != 8:
+    if lax.axis_size(DP) != 8:
         return reduce_other_way(a)
-    tensor = lax.axis_index("tensor")
+    tensor = lax.axis_index(TENSOR)
     _, x = place()
     blocks = a.reshape(4, 2, a.shape[0] // 8, a.shape[1])
-    got = exchange(take(blocks, 1 - x, 1).astype(BF16), "dp", 1).astype(F32)
-    halves = take(blocks, x, 1) + got
+    got = exchange(take(blocks, 1 - x, 1), DP, 1).astype(F32)
+    halves = take(blocks, x, 1).astype(F32) + got
     return along_z(lambda z: take(halves, z ^ tensor, 0))
 
 
 def rows_line_first(a):
-    if lax.axis_size("dp") != 8:
+    if lax.axis_size(DP) != 8:
         return reduce_other_way(a)
-    tensor = lax.axis_index("tensor")
+    tensor = lax.axis_index(TENSOR)
     _, x = place()
     blocks = a.reshape(4, 2, a.shape[0] // 8, a.shape[1])
     pairs = along_z(lambda z: take(blocks, z ^ tensor, 0))
-    late = exchange(take(pairs, 1 - x, 0).astype(BF16), "dp", 1).astype(F32)
+    late = exchange(take(pairs, 1 - x, 0).astype(BF16), DP, 1).astype(F32)
     return take(pairs, x, 0) + late
 
 
@@ -779,7 +810,7 @@
 
 def over_rows(left, right):
     return lax.dot_general(
-        left, right, (((0,), (0,)), ((), ())), preferred_element_type=F32
+        left, right, (((0,), (0,)), ((), ())), preferred_element_type=BF16
     )
 
 
@@ -810,8 +841,8 @@
     gate_gain,
     w_out,
 ):
-    tensor_count = lax.axis_size("tensor")
-    tensor = lax.axis_index("tensor")
+    tensor_count = lax.axis_size(TENSOR)
+    tensor = lax.axis_index(TENSOR)
     rows, part = tokens.shape
     seqs = rows // SEQ_LEN
     inner = w_gate.shape[1]
@@ -843,21 +874,23 @@
     saved, squares = [], []
     for q in range(seqs):
         *saved, here = run_forward(q, seqs, lengths, xs[q], wt, chan, bcc, headc, saved)
-        squares.append(direct_sum(here, "tensor", (1, 2, 3)))
+        squares.append(direct_sum(here, TENSOR, (1, 2, 3)))
     normed, gate, val, z, y, m, *shared = saved
-    middle, stats, gain_acc, out_rows = [], [], None, []
+    middle, stats, gain_acc, branches = [], [], None, []
     for q in range(seqs):
         *middle, stat, here = run_middle(
             q, lengths, cots, wo, chan, m, squares[q], inner_all, middle
         )
         middle, branch = middle[:2], middle[2:]
-        stats.append(direct_sum(stat, "tensor", (1, 2, 3)))
+        stats.append(direct_sum(stat, TENSOR, (1, 2, 3)))
         gain_acc = here if gain_acc is None else gain_acc + here
-        out_rows.append(reduce_pieces(branch))
+        branches.append(reduce_pieces(branch))
     nout, gno = middle
     g_out = jnp.concatenate([over_rows(cot, nout) for cot in cots], 0)
     grad_out_rows = rows_line_first(g_out)
-    out_rows = (tokens.astype(F32) + jnp.concatenate(out_rows, 0)).astype(BF16)
+    out_rows = []
+    for q in range(seqs):
+        out_rows = run_finish(q, lengths, tokens, branches[q], BF16, out_rows)
 
     grad_rows, accs, lows = [], None, []
     kept = (gate, val, z, y, gno, *shared)
@@ -871,13 +904,14 @@
     sum_b = over_rows(normed, lows[1])
     sum_a = over_rows(normed, lows[0])
     sums = (sum_a, sum_b)
-    valid = (jnp.arange(SEQ_LEN)[None] < lengths[:, None]).reshape(rows)[:, None]
-    grad_rows = jnp.concatenate(grad_rows, 0) + jnp.where(valid, grad_out.astype(F32), 0.0)
+    inputs, grad_rows = grad_rows, []
+    for q in range(seqs):
+        grad_rows = run_finish(q, lengths, grad_out, inputs[q], F32, grad_rows)
 
     chan_acc, bc_acc, head_acc, norm_acc = accs
     grads = jnp.concatenate([rows_pair_first(sums[0]), rows_line_first(sums[1])], 1)
     rest = grads[:, 2 * inner :].reshape(tensor_count, -1, states2 + HALF)
-    rest = reduce_pieces([take(rest, tensor ^ i, 0) for i in range(4)], F32)
+    rest = sum(reduce_pieces([take(rest, tensor ^ i, 0) for i in range(4)], F32))
     norm = jnp.sum(norm_acc, 0).reshape(tensor_count, part)
     norm = jnp.concatenate([take(norm, tensor ^ i, 0) for i in range(tensor_count)])
     sizes = [5 * inner, inner, inner, 2 * heads]
@@ -890,21 +924,21 @@
             norm,
         ]
     )
-    if lax.axis_size("dp") == 8:
-        flat = direct_sum(flat, "dp", (1,))
-        flat = direct_sum(flat, "dp", (2, 4, 6))
+    if lax.axis_size(DP) == 8:
+        flat = direct_sum(flat, DP, (1,))
+        flat = direct_sum(flat, DP, (2, 4, 6))
     else:
-        flat = exchange_sum(flat, "dp")
+        flat = exchange_sum(flat, DP)
     cuts = [sum(sizes[: i + 1]) for i in range(4)]
     g_conv, g_skip, g_gain, g_head, everywhere = jnp.split(flat, cuts)
-    everywhere = direct_sum(everywhere, "tensor", (1, 2, 3))
+    everywhere = direct_sum(everywhere, TENSOR, (1, 2, 3))
     g_conv_bc = everywhere[: 5 * states2]
-    share = part // lax.axis_size("dp")
-    first = 5 * states2 + (lax.axis_index("dp") * tensor_count + tensor) * share
+    share = part // lax.axis_size(DP)
+    first = 5 * states2 + (lax.axis_index(DP) * tensor_count + tensor) * share
     g_norm = lax.dynamic_slice_in_dim(everywhere, first, share, 0)
     return (
-        out_rows,
-        grad_rows,
+        out_rows[0],
+        grad_rows[0],
         g_norm,
         grads[:, :inner],
         grads[:, inner : 2 * inner],
@@ -925,42 +959,42 @@
 
 
 def mapped(mesh):
-    both = ("dp", "tensor")
+    both = (DP, TENSOR)
     return jax.shard_map(
         per_device,
         mesh=mesh,
         in_specs=(
-            P("dp", "tensor"),
-            P("dp"),
-            P("dp", "tensor"),
-            P("dp"),
-            P("dp", "tensor"),
-            P("dp", "tensor"),
-            P("dp", None),
-            P("dp", "tensor"),
-            P(None, "tensor"),
+            P(DP, TENSOR),
+            P(DP),
+            P(DP, TENSOR),
+            P(DP),
+            P(DP, TENSOR),
+            P(DP, TENSOR),
+            P(DP, None),
+            P(DP, TENSOR),
+            P(None, TENSOR),
             P(),
-            P("tensor"),
-            P("tensor"),
-            P("tensor"),
-            P("tensor"),
-            P("dp", "tensor"),
+            P(TENSOR),
+            P(TENSOR),
+            P(TENSOR),
+            P(TENSOR),
+            P(DP, TENSOR),
         ),
         out_specs=(
-            P("dp", "tensor"),
-            P("dp", "tensor"),
+            P(DP, TENSOR),
+            P(DP, TENSOR),
             P(both),
-            P("dp", "tensor"),
-            P("dp", "tensor"),
+            P(DP, TENSOR),
+            P(DP, TENSOR),
             P(both, None),
-            P("dp", "tensor"),
-            P(None, "tensor"),
+            P(DP, TENSOR),
+            P(None, TENSOR),
             P(),
-            P("tensor"),
-            P("tensor"),
-            P("tensor"),
-            P("tensor"),
-            P("dp", "tensor"),
+            P(TENSOR),
+            P(TENSOR),
+            P(TENSOR),
+            P(TENSOR),
+            P(DP, TENSOR),
         ),
         check_vma=False,
     )

time: 552 us -> 549 us (level)
  waiting for transfers between devices: 214 us -> 188 us
  Pallas kernels: 144 us -> 156 us
  local copies, waits for them, and re-layouts: 26.6 us -> 35 us
  starting transfers between devices: 96.1 us -> 102 us
    ppermute x50, waiting for transfers between devices: 162 us -> 138 us  [exchange(): lax.ppermute(a, axis, [(i, i ^ bit) for i in range(lax.axis_size(axis))])]
    pallas_call x0 -> x4, Pallas kernels: none -> 11.7 us  [run_finish(): pl.pallas_call(functools.partial(finish_kernel, seq=seq, masked=kind == F...]
    add x7 -> x2, other arithmetic: 9.32 us -> 1.72 us  [the longest x1 1.56 us: per_device(): sum(reduce_pieces([take(rest, tensor ^ i, 0) for i in range(4)], F32))]
    unnamed x82 -> x108, local copies, waits for them, and re-layouts: 11.1 us -> 17.8 us
  transfers between devices with their start and end apart: 68 -> 68, of which waited for: 23 -> 23; matrix products, arithmetic and copies ran while one was open for 12% -> 14% of each run, Pallas kernels for 12% -> 26%
where the time goes in v4:
time: 549 us; the launch traced here: 543 us
  waiting for transfers between devices  188 us (34%)
  Pallas kernels  156 us (28%)
  starting transfers between devices  102 us (19%)
  local copies, waits for them, and re-layouts  35 us (6%)
  matrix products  34.4 us (6%)
  other arithmetic  26.3 us (5%)
    ppermute x50, waiting for transfers between devices, exchange(): lax.ppermute(a, axis, [(i, i ^ bit) for i in range(lax.axis_size(axis))])  138 us
    pallas_call x2, Pallas kernels, run_backward(): pl.pallas_call(functools.partial(backward_kernel, seq=seq, inner=inner, i...  65.6 us
    ppermute x18, starting transfers between devices, exchange_z(): return lax.ppermute(a, (DP, TENSOR), pairs)  63.6 us
    pallas_call x2, Pallas kernels, run_forward(): pl.pallas_call(functools.partial(forward_kernel, seq=seq, inner=inner, he...  52.9 us
    ppermute x18, waiting for transfers between devices, exchange_z(): return lax.ppermute(a, (DP, TENSOR), pairs)  49.5 us
    ppermute x50, starting transfers between devices, exchange(): lax.ppermute(a, axis, [(i, i ^ bit) for i in range(lax.axis_size(axis))])  38.4 us
    dot_general x6, matrix products, over_rows(): lax.dot_general(left, right, (((0,), (0,)), ((), ())), preferred_element_...  34.4 us
    pallas_call x2, Pallas kernels, run_middle(): pl.pallas_call(functools.partial(middle_kernel, seq=seq, inner=inner, inn...  25.3 us
  transfers between devices with their start and end apart: 68, of which 23 were waited for; matrix products, arithmetic and copies ran while one was open for 14% of the time, Pallas kernels for 26%

profile of v4, /device:TPU:0, one launch (start us, length us, event | category | flops | bytes accessed | tf_op | source)
XLA Modules:
  0.0 542.8 jit_solution(2553657072231148580)
XLA Ops:
  3.9 1.4 concatenate.73
  6.1 5.1 collective-permute-start.11
  11.7 1.7 collective-permute-start.17
  21.0 1.8 broadcast_in_dim.37.refs_5_
  24.8 3.9 collective-permute-start.14
  29.4 1.6 collective-permute-start.4
  33.1 1.6 collective-permute-done.4
  34.7 1.5 collective-permute-start.20
  36.3 14.9 %collective-permute-start.6 = (bf16[2,512,128]{2,1,0:T(8,128)(2,1)S(1)}, bf16[2,512,128]{2,1,0:T(8,128)(2,1)S(1)}, u32[]{:S(2)}, u32[]{:S(2)}) collective-permute-start(bf16[2,512,128]{2,1,0:T(8,128)(2,1)S(1)} %get-tuple-element.216), channel_id=1, source_target_pairs={{0,16},{1,25},{2,18},{3,27},{4,20},{5,29},{6,22},{7,31},{8,24},{9,... | collective-permute-start | bytes 786440 | tf_op jit(solution)/shard_map/ppermute | solution.py:709
  51.2 9.8 %collective-permute-done.15 = bf16[2,528,128]{2,1,0:T(8,128)(2,1)S(1)} collective-permute-done((bf16[2,528,128]{2,1,0:T(8,128)(2,1)S(1)}, bf16[2,528,128]{2,1,0:T(8,128)(2,1)S(1)}, u32[]{:S(2)}, u32[]{:S(2)}) %collective-permute-start.15) | collective-permute-done | bytes 270368 | tf_op jit(solution)/shard_map/ppermute | solution.py:709
  61.0 2.5 collective-permute-start.5
  63.7 3.0 collective-permute-done.6
  66.7 9.5 %collective-permute-done.7 = bf16[2,512,128]{2,1,0:T(8,128)(2,1)S(1)} collective-permute-done((bf16[2,512,128]{2,1,0:T(8,128)(2,1)S(1)}, bf16[2,512,128]{2,1,0:T(8,128)(2,1)S(1)}, u32[]{:S(2)}, u32[]{:S(2)}) %collective-permute-start.7) | collective-permute-done | bytes 262176 | tf_op jit(solution)/shard_map/ppermute | solution.py:709
  76.2 1.5 collective-permute-start.1
  77.8 1.5 collective-permute-start.18
  80.4 10.6 %collective-permute-done.18 = bf16[3,768,128]{2,1,0:T(8,128)(2,1)S(1)} collective-permute-done((bf16[3,768,128]{2,1,0:T(8,128)(2,1)S(1)}, bf16[3,768,128]{2,1,0:T(8,128)(2,1)S(1)}, u32[]{:S(2)}, u32[]{:S(2)}) %collective-permute-start.18) | collective-permute-done | bytes 589856 | tf_op jit(solution)/shard_map/ppermute | solution.py:643
  93.8 50.7 %collective-permute-done.9.refs_2_ = bf16[2048,256]{1,0:T(8,128)(2,1)S(1)} collective-permute-done((bf16[2048,256]{1,0:T(8,128)(2,1)S(1)}, bf16[2048,256]{1,0:T(8,128)(2,1)S(1)}, u32[]{:S(2)}, u32[]{:S(2)}) %collective-permute-start.9) | collective-permute-done | bytes 1048608 | tf_op jit(solution)/shard_map/ppermute | solution.py:643
  145.7 1.5 copy-done.19
  147.3 30.4 %mixer_forward.2 = (bf16[4096,1024]{1,0:T(8,128)(2,1)}, f32[512,4096]{1,0:T(8,128)}, f32[512,4096]{1,0:T(8,128)}, f32[512,4096]{1,0:T(8,128)}, f32[512,4096]{1,0...) custom-call(s32[2]{0:T(128)S(1)} %copy-done.18, ...), custom_call_target="tpu_custom_call" | custom-call | tf_op jit(solution)/shard_map/mixer_forward/pallas_call | solution.py:460
  177.8 1.5 collective-permute-start.26
  179.7 22.5 %mixer_forward.3 = (bf16[4096,1024]{1,0:T(8,128)(2,1)}, f32[512,4096]{1,0:T(8,128)}, f32[512,4096]{1,0:T(8,128)}, f32[512,4096]{1,0:T(8,128)}, f32[512,4096]{1,0...) custom-call(s32[2]{0:T(128)S(1)} %copy-done.18, ...), custom_call_target="tpu_custom_call", output_to_operand_aliasing={{0}: (9, {}), {1}: (10, {}), {2}: (11, {}), {3}: (12, {}), ... | custom-call | tf_op jit(solution)/shard_map/mixer_forward/pallas_call | solution.py:460
  202.6 1.5 collective-permute-start.23
  204.2 2.1 collective-permute-done.23
  207.3 13.1 %mixer_middle.2 = (bf16[4096,512]{1,0:T(8,128)(2,1)}, f32[512,4096]{1,0:T(8,128)}, bf16[2048,256]{1,0:T(8,128)(2,1)S(1)}, bf16[2048,256]{1,0:T(8,128)(2,1)}, bf1...) custom-call(s32[2]{0:T(128)S(1)} %copy-done.18, ...), custom_call_target="tpu_custom_call" | custom-call | tf_op jit(solution)/shard_map/mixer_middle/pallas_call | solution.py:503
  222.3 12.2 %mixer_middle.3 = (bf16[4096,512]{1,0:T(8,128)(2,1)}, f32[512,4096]{1,0:T(8,128)}, bf16[2048,256]{1,0:T(8,128)(2,1)S(1)}, bf16[2048,256]{1,0:T(8,128)(2,1)}, bf1...) custom-call(s32[2]{0:T(128)S(1)} %copy-done.18, ...), custom_call_target="tpu_custom_call", output_to_operand_aliasing={{0}: (9, {}), {1}: (10, {})} | custom-call | tf_op jit(solution)/shard_map/mixer_middle/pallas_call | solution.py:503
  235.5 3.6 convolution_bitcast_fusion.3
  239.2 2.9 convolution_bitcast_fusion
  242.1 2.9 convolution_bitcast_fusion.1
  245.0 2.9 convolution_bitcast_fusion.2
  250.1 11.6 %collective-permute-start.64 = (bf16[2,128,512]{2,1,0:T(8,128)(2,1)}, bf16[2,128,512]{2,1,0:T(8,128)(2,1)}, u32[]{:S(2)}, u32[]{:S(2)}) collective-permute-start(bf16[2,128,512]{2,1,0:T(8,128)(2,1)} %get-tuple-element.188), channel_id=1, source_target_pairs={{0,24},{1,9},{2,26},{3,11},{4,28},{5,13},{6,30},{7,15},{8,16},{9,1... | collective-permute-start | bytes 786440 | tf_op jit(solution)/shard_map/ppermute | solution.py:709
  261.8 37.2 %mixer_backward.2 = (bf16[4096,768]{1,0:T(8,128)(2,1)}, bf16[4096,640]{1,0:T(8,128)(2,1)}, bf16[2048,256]{1,0:T(8,128)(2,1)}, bf16[2048,256]{1,0:T(8,128)(2,1)},...) custom-call(s32[2]{0:T(128)S(1)} %copy-done.18, ...), custom_call_target="tpu_custom_call" | custom-call | tf_op jit(solution)/shard_map/mixer_backward/pallas_call | solution.py:561
  299.8 28.5 %mixer_backward.3 = (bf16[4096,768]{1,0:T(8,128)(2,1)}, bf16[4096,640]{1,0:T(8,128)(2,1)}, bf16[2048,256]{1,0:T(8,128)(2,1)}, bf16[2048,256]{1,0:T(8,128)(2,1)},...) custom-call(s32[2]{0:T(128)S(1)} %copy-done.18, ...), custom_call_target="tpu_custom_call", output_to_operand_aliasing={{0}: (21, {}), {1}: (22, {})} | custom-call | tf_op jit(solution)/shard_map/mixer_backward/pallas_call | solution.py:561
  328.3 11.8 %fusion.25 = bf16[1024,640]{1,0:T(8,128)(2,1)} fusion(bf16[4096,1024]{1,0:T(8,128)(2,1)} %get-tuple-element.140, bf16[4096,640]{1,0:T(8,128)(2,1)} %get-tuple-element.142), kind=kOutput, calls=%fused_computation.138 | convolution fusion | flops 5368709120 | bytes 14942208 | tf_op jit(solution)/shard_map/dot_general | solution.py:812
  340.1 10.3 %fusion.24 = bf16[1024,768]{1,0:T(8,128)(2,1)} fusion(bf16[4096,1024]{1,0:T(8,128)(2,1)} %get-tuple-element.140, bf16[4096,768]{1,0:T(8,128)(2,1)S(1)} %copy-done.20), kind=kOutput, calls=%fused_computation.137 | convolution fusion | flops 6442450944 | bytes 16252928 | tf_op jit(solution)/shard_map/dot_general | solution.py:812
  350.5 1.5 add_reduce_fusion.1
  352.2 2.4 add_reduce_fusion
  354.7 2.1 dynamic-slice_bitcast_fusion.3
  356.8 1.7 collective-permute-done.46
  358.5 11.6 %collective-permute-start.48 = (f32[5904]{0:T(1024)S(1)}, f32[5904]{0:T(1024)S(1)}, u32[]{:S(2)}, u32[]{:S(2)}) collective-permute-start(f32[5904]{0:T(1024)S(1)} %add.314), channel_id=1, source_target_pairs={{0,16},{4,20},{8,24},{12,28},{16,0},{20,4},{24,8},{28,12},{1,17},{... | collective-permute-start | bytes 70856 | tf_op jit(solution)/shard_map/ppermute | solution.py:643
  370.2 2.1 dynamic-slice_bitcast_fusion
  372.2 3.8 collective-permute-start.57
  379.3 5.8 %collective-permute-done.57 = bf16[2,128,640]{2,1,0:T(8,128)(2,1)} collective-permute-done((bf16[2,128,640]{2,1,0:T(8,128)(2,1)}, bf16[2,128,640]{2,1,0:T(8,128)(2,1)}, u32[]{:S(2)}, u32[]{:S(2)}) %collective-permute-start.57) | collective-permute-done | bytes 327712 | tf_op jit(solution)/shard_map/ppermute | solution.py:709
  385.0 15.5 %collective-permute-start.66 = (bf16[2,128,512]{2,1,0:T(8,128)(2,1)}, bf16[2,128,512]{2,1,0:T(8,128)(2,1)S(1)}, u32[]{:S(2)}, u32[]{:S(2)}) collective-permute-start(bf16[2,128,512]{2,1,0:T(8,128)(2,1)} %get-tuple-element.189), channel_id=1, source_target_pairs={{0,8},{1,17},{2,10},{3,19},{4,12},{5,21},{6,14},{7,23},{8,0},{9,25... | collective-permute-start | bytes 786440 | tf_op jit(solution)/shard_map/ppermute | solution.py:709
  400.6 6.6 %collective-permute-done.58 = bf16[2,128,640]{2,1,0:T(8,128)(2,1)} collective-permute-done((bf16[2,128,640]{2,1,0:T(8,128)(2,1)}, bf16[2,128,640]{2,1,0:T(8,128)(2,1)}, u32[]{:S(2)}, u32[]{:S(2)}) %collective-permute-start.58) | collective-permute-done | bytes 327712 | tf_op jit(solution)/shard_map/ppermute | solution.py:709
  407.7 1.4 fusion.1
  409.5 2.9 collective-permute-done.66
  414.1 18.4 %collective-permute-done.60 = bf16[128,640]{1,0:T(8,128)(2,1)S(1)} collective-permute-done((bf16[128,640]{1,0:T(8,128)(2,1)S(1)}, bf16[128,640]{1,0:T(8,128)(2,1)S(1)}, u32[]{:S(2)}, u32[]{:S(2)}) %collective-permute-start.60) | collective-permute-done | bytes 163872 | tf_op jit(solution)/shard_map/ppermute | solution.py:643
  434.7 1.6 collective-permute-start.51
  439.1 1.7 collective-permute-done.52
  442.7 1.9 collective-permute-done.67
  446.0 2.5 collective-permute-start.54
  450.8 3.2 collective-permute-done.54
  454.0 2.5 collective-permute-start.56
  457.8 8.2 %collective-permute-done.55 = bf16[128,768]{1,0:T(8,128)(2,1)S(1)} collective-permute-done((bf16[128,768]{1,0:T(8,128)(2,1)S(1)}, bf16[128,768]{1,0:T(8,128)(2,1)S(1)}, u32[]{:S(2)}, u32[]{:S(2)}) %collective-permute-start.55) | collective-permute-done | bytes 196640 | tf_op jit(solution)/shard_map/ppermute | solution.py:709
  470.5 2.3 collective-permute-done.33.last_ref
  476.1 1.8 bitcast_add_fusion.2
  478.5 1.6 slice_add_fusion
  486.0 1.9 finish.4.refs_0_
  487.9 7.5 %collective-permute-done.30.last_ref = bf16[2048,256]{1,0:T(8,128)(2,1)} collective-permute-done((bf16[2048,256]{1,0:T(8,128)(2,1)}, bf16[2048,256]{1,0:T(8,128)(2,1)}, u32[]{:S(2)}, u32[]{:S(2)}) %collective-permute-start.30) | collective-permute-done | bytes 1048608 | tf_op jit(solution)/shard_map/ppermute | solution.py:643
  495.4 2.9 finish.5
  498.3 19.5 %collective-permute-done.45.last_ref = bf16[2048,256]{1,0:T(8,128)(2,1)} collective-permute-done((bf16[2048,256]{1,0:T(8,128)(2,1)}, bf16[2048,256]{1,0:T(8,128)(2,1)}, u32[]{:S(2)}, u32[]{:S(2)}) %collective-permute-start.45) | collective-permute-done | bytes 1048608 | tf_op jit(solution)/shard_map/ppermute | solution.py:643
  517.9 3.4 finish.6.refs_0_
  521.3 17.9 %collective-permute-done.42.last_ref = bf16[2048,256]{1,0:T(8,128)(2,1)} collective-permute-done((bf16[2048,256]{1,0:T(8,128)(2,1)}, bf16[2048,256]{1,0:T(8,128)(2,1)}, u32[]{:S(2)}, u32[]{:S(2)}) %collective-permute-start.42) | collective-permute-done | bytes 1048608 | tf_op jit(solution)/shard_map/ppermute | solution.py:643
  539.1 3.4 finish.7
  (280 shorter events, 62.2 us)
Async XLA Ops:
  6.1 22.7 %collective-permute-start.11 = (bf16[768,128]{1,0:T(8,128)(2,1)}, bf16[768,128]{1,0:T(8,128)(2,1)S(1)}, u32[]{:S(2)}, u32[]{:S(2)}) collective-permute-start(bf16[768,128]{1,0:T(8,128)(2,1)} %get-tuple-element.210), channel_id=1, source_target_pairs={{0,24},{1,9},{2,26},{3,11},{4,28},{5,13},{6,30},{7,15},{8,16},{9,1... | collective-permute-start | bytes 589832 | tf_op jit(solution)/shard_map/ppermute | solution.py:709
  11.1 18.1 %collective-permute-start.12 = (bf16[768,128]{1,0:T(8,128)(2,1)}, bf16[768,128]{1,0:T(8,128)(2,1)S(1)}, u32[]{:S(2)}, u32[]{:S(2)}) collective-permute-start(bf16[768,128]{1,0:T(8,128)(2,1)} %get-tuple-element.210), channel_id=1, source_target_pairs={{0,16},{1,25},{2,18},{3,27},{4,20},{5,29},{6,22},{7,31},{8,24},{9,... | collective-permute-start | bytes 589832 | tf_op jit(solution)/shard_map/ppermute | solution.py:709
  11.1 18.2 %collective-permute-start.13 = (bf16[768,128]{1,0:T(8,128)(2,1)}, bf16[768,128]{1,0:T(8,128)(2,1)}, u32[]{:S(2)}, u32[]{:S(2)}) collective-permute-start(bf16[768,128]{1,0:T(8,128)(2,1)} %get-tuple-element.210), channel_id=1, source_target_pairs={{0,8},{1,17},{2,10},{3,19},{4,12},{5,21},{6,14},{7,23},{8,0},{9,25... | collective-permute-start | bytes 589832 | tf_op jit(solution)/shard_map/ppermute | solution.py:709
  11.7 68.1 %collective-permute-start.17 = (bf16[768,128]{1,0:T(8,128)(2,1)}, bf16[768,128]{1,0:T(8,128)(2,1)}, u32[]{:S(2)}, u32[]{:S(2)}) collective-permute-start(bf16[768,128]{1,0:T(8,128)(2,1)} %get-tuple-element.210), channel_id=1, source_target_pairs={{0,4},{4,0},{8,12},{12,8},{16,20},{20,16},{24,28},{28,24},{1,5},{5... | collective-permute-start | bytes 589832 | tf_op jit(solution)/shard_map/ppermute | solution.py:643
  14.1 6.9 %collective-permute-start.3 = (bf16[528,128]{1,0:T(8,128)(2,1)}, bf16[528,128]{1,0:T(8,128)(2,1)}, u32[]{:S(2)}, u32[]{:S(2)}) collective-permute-start(bf16[528,128]{1,0:T(8,128)(2,1)} %get-tuple-element.212), channel_id=1, source_target_pairs={{0,4},{4,0},{8,12},{12,8},{16,20},{20,16},{24,28},{28,24},{1,5},{5... | collective-permute-start | bytes 405512 | tf_op jit(solution)/shard_map/ppermute | solution.py:643
  24.8 11.4 %collective-permute-start.14 = (bf16[2,528,128]{2,1,0:T(8,128)(2,1)S(1)}, bf16[2,528,128]{2,1,0:T(8,128)(2,1)S(1)}, u32[]{:S(2)}, u32[]{:S(2)}) collective-permute-start(bf16[2,528,128]{2,1,0:T(8,128)(2,1)S(1)} %get-tuple-element.214), channel_id=1, source_target_pairs={{0,24},{1,9},{2,26},{3,11},{4,28},{5,13},{6,30},{7,15},{8,16},{9,1... | collective-permute-start | bytes 811016 | tf_op jit(solution)/shard_map/ppermute | solution.py:709
  28.7 32.3 %collective-permute-start.15 = (bf16[2,528,128]{2,1,0:T(8,128)(2,1)S(1)}, bf16[2,528,128]{2,1,0:T(8,128)(2,1)S(1)}, u32[]{:S(2)}, u32[]{:S(2)}) collective-permute-start(bf16[2,528,128]{2,1,0:T(8,128)(2,1)S(1)} %get-tuple-element.214), channel_id=1, source_target_pairs={{0,16},{1,25},{2,18},{3,27},{4,20},{5,29},{6,22},{7,31},{8,24},{9,... | collective-permute-start | bytes 811016 | tf_op jit(solution)/shard_map/ppermute | solution.py:709
  29.3 31.7 %collective-permute-start.16 = (bf16[2,528,128]{2,1,0:T(8,128)(2,1)S(1)}, bf16[2,528,128]{2,1,0:T(8,128)(2,1)S(1)}, u32[]{:S(2)}, u32[]{:S(2)}) collective-permute-start(bf16[2,528,128]{2,1,0:T(8,128)(2,1)S(1)} %get-tuple-element.214), channel_id=1, source_target_pairs={{0,8},{1,17},{2,10},{3,19},{4,12},{5,21},{6,14},{7,23},{8,0},{9,25... | collective-permute-start | bytes 811016 | tf_op jit(solution)/shard_map/ppermute | solution.py:709
  29.4 5.3 collective-permute-start.4
  34.7 58.4 %collective-permute-start.20 = (bf16[2048,256]{1,0:T(8,128)(2,1)S(1)}, bf16[2048,256]{1,0:T(8,128)(2,1)S(1)}, u32[]{:S(2)}, u32[]{:S(2)}) collective-permute-start(bf16[2048,256]{1,0:T(8,128)(2,1)S(1)} %copy-done.5), channel_id=1, source_target_pairs={{0,2},{1,3},{2,0},{3,1},{4,6},{5,7},{6,4},{7,5},{8,10},{9,11},{10,... | collective-permute-start | bytes 3145736 | tf_op jit(solution)/shard_map/ppermute | solution.py:643
  36.3 30.4 %collective-permute-start.6 = (bf16[2,512,128]{2,1,0:T(8,128)(2,1)S(1)}, bf16[2,512,128]{2,1,0:T(8,128)(2,1)S(1)}, u32[]{:S(2)}, u32[]{:S(2)}) collective-permute-start(bf16[2,512,128]{2,1,0:T(8,128)(2,1)S(1)} %get-tuple-element.216), channel_id=1, source_target_pairs={{0,16},{1,25},{2,18},{3,27},{4,20},{5,29},{6,22},{7,31},{8,24},{9,... | collective-permute-start | bytes 786440 | tf_op jit(solution)/shard_map/ppermute | solution.py:709
  61.0 15.2 %collective-permute-start.7 = (bf16[2,512,128]{2,1,0:T(8,128)(2,1)S(1)}, bf16[2,512,128]{2,1,0:T(8,128)(2,1)S(1)}, u32[]{:S(2)}, u32[]{:S(2)}) collective-permute-start(bf16[2,512,128]{2,1,0:T(8,128)(2,1)S(1)} %get-tuple-element.216), channel_id=1, source_target_pairs={{0,8},{1,17},{2,10},{3,19},{4,12},{5,21},{6,14},{7,23},{8,0},{9,25... | collective-permute-start | bytes 786440 | tf_op jit(solution)/shard_map/ppermute | solution.py:709
  61.0 16.7 %collective-permute-start.5 = (bf16[2,512,128]{2,1,0:T(8,128)(2,1)S(1)}, bf16[2,512,128]{2,1,0:T(8,128)(2,1)S(1)}, u32[]{:S(2)}, u32[]{:S(2)}) collective-permute-start(bf16[2,512,128]{2,1,0:T(8,128)(2,1)S(1)} %get-tuple-element.216), channel_id=1, source_target_pairs={{0,24},{1,9},{2,26},{3,11},{4,28},{5,13},{6,30},{7,15},{8,16},{9,1... | collective-permute-start | bytes 786440 | tf_op jit(solution)/shard_map/ppermute | solution.py:709
  66.7 27.0 %collective-permute-start.19 = (bf16[2048,256]{1,0:T(8,128)(2,1)S(1)}, bf16[2048,256]{1,0:T(8,128)(2,1)S(1)}, u32[]{:S(2)}, u32[]{:S(2)}) collective-permute-start(bf16[2048,256]{1,0:T(8,128)(2,1)S(1)} %copy-done.5), channel_id=1, source_target_pairs={{0,1},{1,0},{2,3},{3,2},{4,5},{5,4},{6,7},{7,6},{8,9},{9,8},{10,11... | collective-permute-start | bytes 3145736 | tf_op jit(solution)/shard_map/ppermute | solution.py:643
  76.2 68.3 %collective-permute-start.1 = (bf16[4096,256]{1,0:T(8,128)(2,1)S(1)}, bf16[4096,256]{1,0:T(8,128)(2,1)}, u32[]{:S(2)}, u32[]{:S(2)}) collective-permute-start(bf16[4096,256]{1,0:T(8,128)(2,1)S(1)} %copy-done), channel_id=1, source_target_pairs={{0,2},{1,3},{2,0},{3,1},{4,6},{5,7},{6,4},{7,5},{8,10},{9,11},{10,... | collective-permute-start | bytes 6291464 | tf_op jit(solution)/shard_map/ppermute | solution.py:643
  77.8 13.2 %collective-permute-start.18 = (bf16[3,768,128]{2,1,0:T(8,128)(2,1)S(1)}, bf16[3,768,128]{2,1,0:T(8,128)(2,1)S(1)}, u32[]{:S(2)}, u32[]{:S(2)}) collective-permute-start(bf16[3,768,128]{2,1,0:T(8,128)(2,1)S(1)} %pad_maximum_fusion.4), channel_id=1, source_target_pairs={{0,4},{4,0},{8,12},{12,8},{16,20},{20,16},{24,28},{28,24},{1,5},{5... | collective-permute-start | bytes 1769480 | tf_op jit(solution)/shard_map/ppermute | solution.py:643
  79.8 64.7 %collective-permute-start.9 = (bf16[2048,256]{1,0:T(8,128)(2,1)S(1)}, bf16[2048,256]{1,0:T(8,128)(2,1)S(1)}, u32[]{:S(2)}, u32[]{:S(2)}) collective-permute-start(bf16[2048,256]{1,0:T(8,128)(2,1)S(1)} %get-tuple-element.173.refs_0_), channel_id=1, source_target_pairs={{0,2},{1,3},{2,0},{3,1},{4,6},{5,7},{6,4},{7,5},{8,10},{9,11},{10,... | collective-permute-start | bytes 3145736 | tf_op jit(solution)/shard_map/ppermute | solution.py:643
  91.0 86.8 %collective-permute-start.8 = (bf16[2048,256]{1,0:T(8,128)(2,1)S(1)}, bf16[2048,256]{1,0:T(8,128)(2,1)}, u32[]{:S(2)}, u32[]{:S(2)}) collective-permute-start(bf16[2048,256]{1,0:T(8,128)(2,1)S(1)} %get-tuple-element.173.refs_0_), channel_id=1, source_target_pairs={{0,1},{1,0},{2,3},{3,2},{4,5},{5,4},{6,7},{7,6},{8,9},{9,8},{10,11... | collective-permute-start | bytes 3145736 | tf_op jit(solution)/shard_map/ppermute | solution.py:643
  93.2 114.1 %collective-permute-start = (bf16[4096,256]{1,0:T(8,128)(2,1)S(1)}, bf16[4096,256]{1,0:T(8,128)(2,1)}, u32[]{:S(2)}, u32[]{:S(2)}) collective-permute-start(bf16[4096,256]{1,0:T(8,128)(2,1)S(1)} %copy-done), channel_id=1, source_target_pairs={{0,1},{1,0},{2,3},{3,2},{4,5},{5,4},{6,7},{7,6},{8,9},{9,8},{10,11... | collective-permute-start | bytes 6291464 | tf_op jit(solution)/shard_map/ppermute | solution.py:643
  93.7 52.0 %collective-permute-start.21 = (bf16[2048,256]{1,0:T(8,128)(2,1)S(1)}, bf16[2048,256]{1,0:T(8,128)(2,1)}, u32[]{:S(2)}, u32[]{:S(2)}) collective-permute-start(bf16[2048,256]{1,0:T(8,128)(2,1)S(1)} %collective-permute-done.20.refs_2_), channel_id=1, source_target_pairs={{0,1},{1,0},{2,3},{3,2},{4,5},{5,4},{6,7},{7,6},{8,9},{9,8},{10,11... | collective-permute-start | bytes 3145736 | tf_op jit(solution)/shard_map/ppermute | solution.py:643
  144.5 34.8 %collective-permute-start.10 = (bf16[2048,256]{1,0:T(8,128)(2,1)S(1)}, bf16[2048,256]{1,0:T(8,128)(2,1)}, u32[]{:S(2)}, u32[]{:S(2)}) collective-permute-start(bf16[2048,256]{1,0:T(8,128)(2,1)S(1)} %collective-permute-done.9.refs_2_), channel_id=1, source_target_pairs={{0,1},{1,0},{2,3},{3,2},{4,5},{5,4},{6,7},{7,6},{8,9},{9,8},{10,11... | collective-permute-start | bytes 3145736 | tf_op jit(solution)/shard_map/ppermute | solution.py:643
  144.5 62.8 %collective-permute-start.2 = (bf16[4096,256]{1,0:T(8,128)(2,1)}, bf16[4096,256]{1,0:T(8,128)(2,1)}, u32[]{:S(2)}, u32[]{:S(2)}) collective-permute-start(bf16[4096,256]{1,0:T(8,128)(2,1)} %collective-permute-done.1.refs_2_), channel_id=1, source_target_pairs={{0,1},{1,0},{2,3},{3,2},{4,5},{5,4},{6,7},{7,6},{8,9},{9,8},{10,11... | collective-permute-start | bytes 6291464 | tf_op jit(solution)/shard_map/ppermute | solution.py:643
  177.7 24.5 %collective-permute-start.25 = (f32[1,2048]{1,0:T(1,128)S(1)}, f32[1,2048]{1,0:T(1,128)S(1)}, u32[]{:S(2)}, u32[]{:S(2)}) collective-permute-start(f32[1,2048]{1,0:T(1,128)S(1)} %get-tuple-element.97), channel_id=1, source_target_pairs={{0,1},{1,0},{2,3},{3,2},{4,5},{5,4},{6,7},{7,6},{8,9},{9,8},{10,11... | collective-permute-start | bytes 24584 | tf_op jit(solution)/shard_map/ppermute | solution.py:643
  177.8 24.8 %collective-permute-start.26 = (f32[1,2048]{1,0:T(1,128)S(1)}, f32[1,2048]{1,0:T(1,128)S(1)}, u32[]{:S(2)}, u32[]{:S(2)}) collective-permute-start(f32[1,2048]{1,0:T(1,128)S(1)} %get-tuple-element.97), channel_id=1, source_target_pairs={{0,2},{1,3},{2,0},{3,1},{4,6},{5,7},{6,4},{7,5},{8,10},{9,11},{10,... | collective-permute-start | bytes 24584 | tf_op jit(solution)/shard_map/ppermute | solution.py:643
  179.4 24.8 %collective-permute-start.27 = (f32[1,2048]{1,0:T(1,128)S(1)}, f32[1,2048]{1,0:T(1,128)S(1)}, u32[]{:S(2)}, u32[]{:S(2)}) collective-permute-start(f32[1,2048]{1,0:T(1,128)S(1)} %get-tuple-element.97), channel_id=1, source_target_pairs={{0,3},{1,2},{2,1},{3,0},{4,7},{5,6},{6,5},{7,4},{8,11},{9,10},{10,... | collective-permute-start | bytes 24584 | tf_op jit(solution)/shard_map/ppermute | solution.py:643
  202.6 3.7 collective-permute-start.23
  220.4 28.6 %collective-permute-start.37 = (f32[1,2048]{1,0:T(1,128)S(1)}, f32[1,2048]{1,0:T(1,128)S(1)}, u32[]{:S(2)}, u32[]{:S(2)}) collective-permute-start(f32[1,2048]{1,0:T(1,128)S(1)} %get-tuple-element.119), channel_id=1, source_target_pairs={{0,1},{1,0},{2,3},{3,2},{4,5},{5,4},{6,7},{7,6},{8,9},{9,8},{10,11... | collective-permute-start | bytes 24584 | tf_op jit(solution)/shard_map/ppermute | solution.py:643
  220.6 29.5 %collective-permute-start.38 = (f32[1,2048]{1,0:T(1,128)S(1)}, f32[1,2048]{1,0:T(1,128)S(1)}, u32[]{:S(2)}, u32[]{:S(2)}) collective-permute-start(f32[1,2048]{1,0:T(1,128)S(1)} %get-tuple-element.119), channel_id=1, source_target_pairs={{0,2},{1,3},{2,0},{3,1},{4,6},{5,7},{6,4},{7,5},{8,10},{9,11},{10,... | collective-permute-start | bytes 24584 | tf_op jit(solution)/shard_map/ppermute | solution.py:643
  221.1 40.6 %collective-permute-start.39 = (f32[1,2048]{1,0:T(1,128)S(1)}, f32[1,2048]{1,0:T(1,128)S(1)}, u32[]{:S(2)}, u32[]{:S(2)}) collective-permute-start(f32[1,2048]{1,0:T(1,128)S(1)} %get-tuple-element.119), channel_id=1, source_target_pairs={{0,3},{1,2},{2,1},{3,0},{4,7},{5,6},{6,5},{7,4},{8,11},{9,10},{10,... | collective-permute-start | bytes 24584 | tf_op jit(solution)/shard_map/ppermute | solution.py:643
  234.6 27.2 %collective-permute-start.34 = (f32[1,2048]{1,0:T(1,128)S(1)}, f32[1,2048]{1,0:T(1,128)S(1)}, u32[]{:S(2)}, u32[]{:S(2)}) collective-permute-start(f32[1,2048]{1,0:T(1,128)S(1)} %get-tuple-element.118), channel_id=1, source_target_pairs={{0,1},{1,0},{2,3},{3,2},{4,5},{5,4},{6,7},{7,6},{8,9},{9,8},{10,11... | collective-permute-start | bytes 24584 | tf_op jit(solution)/shard_map/ppermute | solution.py:643
  235.0 26.8 %collective-permute-start.35 = (f32[1,2048]{1,0:T(1,128)S(1)}, f32[1,2048]{1,0:T(1,128)S(1)}, u32[]{:S(2)}, u32[]{:S(2)}) collective-permute-start(f32[1,2048]{1,0:T(1,128)S(1)} %get-tuple-element.118), channel_id=1, source_target_pairs={{0,2},{1,3},{2,0},{3,1},{4,6},{5,7},{6,4},{7,5},{8,10},{9,11},{10,... | collective-permute-start | bytes 24584 | tf_op jit(solution)/shard_map/ppermute | solution.py:643
  249.1 12.7 %collective-permute-start.36 = (f32[1,2048]{1,0:T(1,128)S(1)}, f32[1,2048]{1,0:T(1,128)S(1)}, u32[]{:S(2)}, u32[]{:S(2)}) collective-permute-start(f32[1,2048]{1,0:T(1,128)S(1)} %get-tuple-element.118), channel_id=1, source_target_pairs={{0,3},{1,2},{2,1},{3,0},{4,7},{5,6},{6,5},{7,4},{8,11},{9,10},{10,... | collective-permute-start | bytes 24584 | tf_op jit(solution)/shard_map/ppermute | solution.py:643
  250.1 159.0 %collective-permute-start.64 = (bf16[2,128,512]{2,1,0:T(8,128)(2,1)}, bf16[2,128,512]{2,1,0:T(8,128)(2,1)}, u32[]{:S(2)}, u32[]{:S(2)}) collective-permute-start(bf16[2,128,512]{2,1,0:T(8,128)(2,1)} %get-tuple-element.188), channel_id=1, source_target_pairs={{0,24},{1,9},{2,26},{3,11},{4,28},{5,13},{6,30},{7,15},{8,16},{9,1... | collective-permute-start | bytes 786440 | tf_op jit(solution)/shard_map/ppermute | solution.py:709
  261.7 147.5 %collective-permute-start.65 = (bf16[2,128,512]{2,1,0:T(8,128)(2,1)}, bf16[2,128,512]{2,1,0:T(8,128)(2,1)}, u32[]{:S(2)}, u32[]{:S(2)}) collective-permute-start(bf16[2,128,512]{2,1,0:T(8,128)(2,1)} %get-tuple-element.190), channel_id=1, source_target_pairs={{0,16},{1,25},{2,18},{3,27},{4,20},{5,29},{6,22},{7,31},{8,24},{9,... | collective-permute-start | bytes 786440 | tf_op jit(solution)/shard_map/ppermute | solution.py:709
  354.7 3.9 collective-permute-start.46
  358.5 13.7 %collective-permute-start.47 = (f32[5904]{0:T(1024)S(1)}, f32[5904]{0:T(1024)S(1)}, u32[]{:S(2)}, u32[]{:S(2)}) collective-permute-start(f32[5904]{0:T(1024)S(1)} %add.314), channel_id=1, source_target_pairs={{0,8},{4,12},{8,0},{12,4},{16,24},{20,28},{24,16},{28,20},{1,9},{5... | collective-permute-start | bytes 70856 | tf_op jit(solution)/shard_map/ppermute | solution.py:643
  358.5 17.5 %collective-permute-start.48 = (f32[5904]{0:T(1024)S(1)}, f32[5904]{0:T(1024)S(1)}, u32[]{:S(2)}, u32[]{:S(2)}) collective-permute-start(f32[5904]{0:T(1024)S(1)} %add.314), channel_id=1, source_target_pairs={{0,16},{4,20},{8,24},{12,28},{16,0},{20,4},{24,8},{28,12},{1,17},{... | collective-permute-start | bytes 70856 | tf_op jit(solution)/shard_map/ppermute | solution.py:643
  370.2 5.9 %collective-permute-start.49 = (f32[5904]{0:T(1024)S(1)}, f32[5904]{0:T(1024)S(1)}, u32[]{:S(2)}, u32[]{:S(2)}) collective-permute-start(f32[5904]{0:T(1024)S(1)} %add.314), channel_id=1, source_target_pairs={{0,24},{4,28},{8,16},{12,20},{16,8},{20,12},{24,0},{28,4},{1,25},{... | collective-permute-start | bytes 70856 | tf_op jit(solution)/shard_map/ppermute | solution.py:643
  372.2 12.8 %collective-permute-start.57 = (bf16[2,128,640]{2,1,0:T(8,128)(2,1)}, bf16[2,128,640]{2,1,0:T(8,128)(2,1)}, u32[]{:S(2)}, u32[]{:S(2)}) collective-permute-start(bf16[2,128,640]{2,1,0:T(8,128)(2,1)} %get-tuple-element.177), channel_id=1, source_target_pairs={{0,24},{1,9},{2,26},{3,11},{4,28},{5,13},{6,30},{7,15},{8,16},{9,1... | collective-permute-start | bytes 983048 | tf_op jit(solution)/shard_map/ppermute | solution.py:709
  376.1 31.1 %collective-permute-start.58 = (bf16[2,128,640]{2,1,0:T(8,128)(2,1)}, bf16[2,128,640]{2,1,0:T(8,128)(2,1)}, u32[]{:S(2)}, u32[]{:S(2)}) collective-permute-start(bf16[2,128,640]{2,1,0:T(8,128)(2,1)} %get-tuple-element.179), channel_id=1, source_target_pairs={{0,16},{1,25},{2,18},{3,27},{4,20},{5,29},{6,22},{7,31},{8,24},{9,... | collective-permute-start | bytes 983048 | tf_op jit(solution)/shard_map/ppermute | solution.py:709
  376.1 31.1 %collective-permute-start.59 = (bf16[2,128,640]{2,1,0:T(8,128)(2,1)S(1)}, bf16[2,128,640]{2,1,0:T(8,128)(2,1)}, u32[]{:S(2)}, u32[]{:S(2)}) collective-permute-start(bf16[2,128,640]{2,1,0:T(8,128)(2,1)S(1)} %get-tuple-element.178), channel_id=1, source_target_pairs={{0,8},{1,17},{2,10},{3,19},{4,12},{5,21},{6,14},{7,23},{8,0},{9,25... | collective-permute-start | bytes 983048 | tf_op jit(solution)/shard_map/ppermute | solution.py:709
  385.0 27.3 %collective-permute-start.66 = (bf16[2,128,512]{2,1,0:T(8,128)(2,1)}, bf16[2,128,512]{2,1,0:T(8,128)(2,1)S(1)}, u32[]{:S(2)}, u32[]{:S(2)}) collective-permute-start(bf16[2,128,512]{2,1,0:T(8,128)(2,1)} %get-tuple-element.189), channel_id=1, source_target_pairs={{0,8},{1,17},{2,10},{3,19},{4,12},{5,21},{6,14},{7,23},{8,0},{9,25... | collective-permute-start | bytes 786440 | tf_op jit(solution)/shard_map/ppermute | solution.py:709
  407.1 30.5 %collective-permute-start.32 = (bf16[2048,256]{1,0:T(8,128)(2,1)}, bf16[2048,256]{1,0:T(8,128)(2,1)S(1)}, u32[]{:S(2)}, u32[]{:S(2)}) collective-permute-start(bf16[2048,256]{1,0:T(8,128)(2,1)} %get-tuple-element.107), channel_id=1, source_target_pairs={{0,1},{1,0},{2,3},{3,2},{4,5},{5,4},{6,7},{7,6},{8,9},{9,8},{10,11... | collective-permute-start | bytes 3145736 | tf_op jit(solution)/shard_map/ppermute | solution.py:643
  407.1 33.8 %collective-permute-start.29 = (bf16[2048,256]{1,0:T(8,128)(2,1)}, bf16[2048,256]{1,0:T(8,128)(2,1)S(1)}, u32[]{:S(2)}, u32[]{:S(2)}) collective-permute-start(bf16[2048,256]{1,0:T(8,128)(2,1)} %get-tuple-element.103), channel_id=1, source_target_pairs={{0,1},{1,0},{2,3},{3,2},{4,5},{5,4},{6,7},{7,6},{8,9},{9,8},{10,11... | collective-permute-start | bytes 3145736 | tf_op jit(solution)/shard_map/ppermute | solution.py:643
  409.1 25.5 %collective-permute-start.53 = (bf16[4,128,768]{2,1,0:T(8,128)(2,1)}, bf16[4,128,768]{2,1,0:T(8,128)(2,1)S(1)}, u32[]{:S(2)}, u32[]{:S(2)}) collective-permute-start(bf16[4,128,768]{2,1,0:T(8,128)(2,1)} %dynamic-slice_bitcast_fusion), channel_id=1, source_target_pairs={{0,4},{4,0},{8,12},{12,8},{16,20},{20,16},{24,28},{28,24},{1,5},{5... | collective-permute-start | bytes 2359304 | tf_op jit(solution)/shard_map/ppermute | solution.py:643
  409.2 39.2 %collective-permute-start.44 = (bf16[2048,256]{1,0:T(8,128)(2,1)}, bf16[2048,256]{1,0:T(8,128)(2,1)S(1)}, u32[]{:S(2)}, u32[]{:S(2)}) collective-permute-start(bf16[2048,256]{1,0:T(8,128)(2,1)} %get-tuple-element.129), channel_id=1, source_target_pairs={{0,1},{1,0},{2,3},{3,2},{4,5},{5,4},{6,7},{7,6},{8,9},{9,8},{10,11... | collective-permute-start | bytes 3145736 | tf_op jit(solution)/shard_map/ppermute | solution.py:643
  412.3 20.2 %collective-permute-start.60 = (bf16[128,640]{1,0:T(8,128)(2,1)S(1)}, bf16[128,640]{1,0:T(8,128)(2,1)S(1)}, u32[]{:S(2)}, u32[]{:S(2)}) collective-permute-start(bf16[128,640]{1,0:T(8,128)(2,1)S(1)} %fusion.17), channel_id=1, source_target_pairs={{0,4},{4,0},{8,12},{12,8},{16,20},{20,16},{24,28},{28,24},{1,5},{5... | collective-permute-start | bytes 491528 | tf_op jit(solution)/shard_map/ppermute | solution.py:643
  434.5 3.7 collective-permute-start.50
  434.7 4.2 collective-permute-start.51
  438.8 15.2 %collective-permute-start.41 = (bf16[2048,256]{1,0:T(8,128)(2,1)S(1)}, bf16[2048,256]{1,0:T(8,128)(2,1)S(1)}, u32[]{:S(2)}, u32[]{:S(2)}) collective-permute-start(bf16[2048,256]{1,0:T(8,128)(2,1)S(1)} %copy-done.47), channel_id=1, source_target_pairs={{0,1},{1,0},{2,3},{3,2},{4,5},{5,4},{6,7},{7,6},{8,9},{9,8},{10,11... | collective-permute-start | bytes 3145736 | tf_op jit(solution)/shard_map/ppermute | solution.py:643
  438.8 5.8 %collective-permute-start.67 = (bf16[128,512]{1,0:T(8,128)(2,1)S(1)}, bf16[128,512]{1,0:T(8,128)(2,1)S(1)}, u32[]{:S(2)}, u32[]{:S(2)}) collective-permute-start(bf16[128,512]{1,0:T(8,128)(2,1)S(1)} %fusion.18), channel_id=1, source_target_pairs={{0,4},{4,0},{8,12},{12,8},{16,20},{20,16},{24,28},{28,24},{1,5},{5... | collective-permute-start | bytes 393224 | tf_op jit(solution)/shard_map/ppermute | solution.py:643
  440.8 3.9 collective-permute-start.61
  440.9 5.0 collective-permute-start.63
  444.7 21.9 %collective-permute-start.31 = (bf16[2048,256]{1,0:T(8,128)(2,1)S(1)}, bf16[2048,256]{1,0:T(8,128)(2,1)S(1)}, u32[]{:S(2)}, u32[]{:S(2)}) collective-permute-start(bf16[2048,256]{1,0:T(8,128)(2,1)S(1)} %copy-done.45), channel_id=1, source_target_pairs={{0,1},{1,0},{2,3},{3,2},{4,5},{5,4},{6,7},{7,6},{8,9},{9,8},{10,11... | collective-permute-start | bytes 3145736 | tf_op jit(solution)/shard_map/ppermute | solution.py:643
  446.0 22.6 %collective-permute-start.28 = (bf16[2048,256]{1,0:T(8,128)(2,1)S(1)}, bf16[2048,256]{1,0:T(8,128)(2,1)S(1)}, u32[]{:S(2)}, u32[]{:S(2)}) collective-permute-start(bf16[2048,256]{1,0:T(8,128)(2,1)S(1)} %copy-done.46), channel_id=1, source_target_pairs={{0,1},{1,0},{2,3},{3,2},{4,5},{5,4},{6,7},{7,6},{8,9},{9,8},{10,11... | collective-permute-start | bytes 3145736 | tf_op jit(solution)/shard_map/ppermute | solution.py:643
  446.0 8.0 %collective-permute-start.54 = (bf16[128,768]{1,0:T(8,128)(2,1)S(1)}, bf16[128,768]{1,0:T(8,128)(2,1)S(1)}, u32[]{:S(2)}, u32[]{:S(2)}) collective-permute-start(bf16[128,768]{1,0:T(8,128)(2,1)S(1)} %get-tuple-element.174), channel_id=1, source_target_pairs={{0,24},{1,9},{2,26},{3,11},{4,28},{5,13},{6,30},{7,15},{8,16},{9,1... | collective-permute-start | bytes 589832 | tf_op jit(solution)/shard_map/ppermute | solution.py:709
  448.5 24.4 %collective-permute-start.33 = (bf16[2048,256]{1,0:T(8,128)(2,1)S(1)}, bf16[2048,256]{1,0:T(8,128)(2,1)S(1)}, u32[]{:S(2)}, u32[]{:S(2)}) collective-permute-start(bf16[2048,256]{1,0:T(8,128)(2,1)S(1)} %add_convert_fusion.2), channel_id=1, source_target_pairs={{0,2},{1,3},{2,0},{3,1},{4,6},{5,7},{6,4},{7,5},{8,10},{9,11},{10,... | collective-permute-start | bytes 3145736 | tf_op jit(solution)/shard_map/ppermute | solution.py:643
  454.0 12.1 %collective-permute-start.55 = (bf16[128,768]{1,0:T(8,128)(2,1)S(1)}, bf16[128,768]{1,0:T(8,128)(2,1)S(1)}, u32[]{:S(2)}, u32[]{:S(2)}) collective-permute-start(bf16[128,768]{1,0:T(8,128)(2,1)S(1)} %get-tuple-element.176), channel_id=1, source_target_pairs={{0,16},{1,25},{2,18},{3,27},{4,20},{5,29},{6,22},{7,31},{8,24},{9,... | collective-permute-start | bytes 589832 | tf_op jit(solution)/shard_map/ppermute | solution.py:709
  454.0 12.1 %collective-permute-start.56 = (bf16[128,768]{1,0:T(8,128)(2,1)S(1)}, bf16[128,768]{1,0:T(8,128)(2,1)S(1)}, u32[]{:S(2)}, u32[]{:S(2)}) collective-permute-start(bf16[128,768]{1,0:T(8,128)(2,1)S(1)} %get-tuple-element.175), channel_id=1, source_target_pairs={{0,8},{1,17},{2,10},{3,19},{4,12},{5,21},{6,14},{7,23},{8,0},{9,25... | collective-permute-start | bytes 589832 | tf_op jit(solution)/shard_map/ppermute | solution.py:709
  466.0 32.3 %collective-permute-start.43 = (bf16[2048,256]{1,0:T(8,128)(2,1)}, bf16[2048,256]{1,0:T(8,128)(2,1)}, u32[]{:S(2)}, u32[]{:S(2)}) collective-permute-start(bf16[2048,256]{1,0:T(8,128)(2,1)} %get-tuple-element.127), channel_id=1, source_target_pairs={{0,1},{1,0},{2,3},{3,2},{4,5},{5,4},{6,7},{7,6},{8,9},{9,8},{10,11... | collective-permute-start | bytes 3145736 | tf_op jit(solution)/shard_map/ppermute | solution.py:643
  466.0 55.2 %collective-permute-start.40 = (bf16[2048,256]{1,0:T(8,128)(2,1)}, bf16[2048,256]{1,0:T(8,128)(2,1)}, u32[]{:S(2)}, u32[]{:S(2)}) collective-permute-start(bf16[2048,256]{1,0:T(8,128)(2,1)} %get-tuple-element.123), channel_id=1, source_target_pairs={{0,1},{1,0},{2,3},{3,2},{4,5},{5,4},{6,7},{7,6},{8,9},{9,8},{10,11... | collective-permute-start | bytes 3145736 | tf_op jit(solution)/shard_map/ppermute | solution.py:643
  467.5 27.8 %collective-permute-start.30 = (bf16[2048,256]{1,0:T(8,128)(2,1)}, bf16[2048,256]{1,0:T(8,128)(2,1)}, u32[]{:S(2)}, u32[]{:S(2)}) collective-permute-start(bf16[2048,256]{1,0:T(8,128)(2,1)} %add_convert_fusion.3), channel_id=1, source_target_pairs={{0,2},{1,3},{2,0},{3,1},{4,6},{5,7},{6,4},{7,5},{8,10},{9,11},{10,... | collective-permute-start | bytes 3145736 | tf_op jit(solution)/shard_map/ppermute | solution.py:643
  469.5 48.3 %collective-permute-start.45 = (bf16[2048,256]{1,0:T(8,128)(2,1)}, bf16[2048,256]{1,0:T(8,128)(2,1)}, u32[]{:S(2)}, u32[]{:S(2)}) collective-permute-start(bf16[2048,256]{1,0:T(8,128)(2,1)} %add_convert_fusion), channel_id=1, source_target_pairs={{0,2},{1,3},{2,0},{3,1},{4,6},{5,7},{6,4},{7,5},{8,10},{9,11},{10,... | collective-permute-start | bytes 3145736 | tf_op jit(solution)/shard_map/ppermute | solution.py:643
  473.8 65.3 %collective-permute-start.42 = (bf16[2048,256]{1,0:T(8,128)(2,1)}, bf16[2048,256]{1,0:T(8,128)(2,1)}, u32[]{:S(2)}, u32[]{:S(2)}) collective-permute-start(bf16[2048,256]{1,0:T(8,128)(2,1)} %add_convert_fusion.1), channel_id=1, source_target_pairs={{0,2},{1,3},{2,0},{3,1},{4,6},{5,7},{6,4},{7,5},{8,10},{9,11},{10,... | collective-permute-start | bytes 3145736 | tf_op jit(solution)/shard_map/ppermute | solution.py:643
  (52 other events, 842.7 us)

commit v5 on v4

--- a/solution.py
+++ b/solution.py
@@ -158,7 +158,9 @@
         for k in range(4):
             cols = slice(k * part, (k + 1) * part)
             norm_ref[:, cols] = (xs[k] * inv * gain[:, cols]).astype(BF16)
-        proj[...] = nt(wt_ref[: base + 16, :], norm_ref[...])
+        half = inner // 2
+        for lo, hi in ((2 * inner, base + 16), (inner, inner + half), (0, half)):
+            proj[lo:hi, :] = nt(wt_ref[lo:hi, :], norm_ref[...])
 
         raw = proj[2 * inner : base, :]
         bc_ref[...] = raw
@@ -188,6 +190,9 @@
         carried[...] = nn(state[...].astype(BF16), c_low)
         squares = jnp.zeros((1, Q), F32)
         for h in range(heads):
+            if h == 0:
+                for lo in (half, inner + half):
+                    proj[lo : lo + half, :] = nt(wt_ref[lo : lo + half, :], norm_ref[...])
             rows = slice(h * per, (h + 1) * per)
             raw_v = proj[inner + h * per : inner + (h + 1) * per, :]
             gate = proj[rows, :]
@@ -205,7 +210,7 @@
             wdec[rows, :] = (w * to_end[h : h + 1]).astype(BF16)
             u = y + twice(chan_ref[6, rows, :]) * v
             m = u * gate * jax.nn.sigmoid(gate)
-            m_ref[rows, :] = m
+            m_ref[rows, :] = m.astype(BF16)
             squares = squares + jnp.sum(m * m, 0, keepdims=True)
         stat_ref[...] = squares
         fresh = nn(wdec[...], b_time)
@@ -237,13 +242,13 @@
         valid = valid_row(block, length)
         scale = lax.rsqrt(sq_ref[...] / inner_all + epsilon) * valid
         cot = jnp.concatenate([ref[...] for ref in (c0, c1, c2, c3)], 1)
-        gno_ref[...] = nt(wo_ref[...], cot) * valid
+        gno_ref[...] = (nt(wo_ref[...], cot) * valid).astype(BF16)
         inners = jnp.zeros((1, Q), F32)
         for lo in range(0, inner, 64):
             rows = slice(lo, lo + 64)
             gain = twice(chan_ref[5, rows, :])
-            m = m_ref[rows, :]
-            gno = gno_ref[rows, :]
+            m = m_ref[rows, :].astype(F32)
+            gno = gno_ref[rows, :].astype(F32)
             nout[rows, :] = (m * scale * gain).astype(BF16)
             inners = inners + jnp.sum(gno * gain * m, 0, keepdims=True)
             gain_acc[rows, :] += fold(gno * m * scale)
@@ -313,7 +318,8 @@
         direct, both, after, through = [], [], [], []
         for h in range(heads):
             rows = slice(h * per, (h + 1) * per)
-            gate, z, y, gno = gate_ref[rows, :], z_ref[rows, :], y_ref[rows, :], gno_ref[rows, :]
+            gate, z, y = gate_ref[rows, :], z_ref[rows, :], y_ref[rows, :]
+            gno = gno_ref[rows, :].astype(F32)
             gain = twice(chan_ref[5, rows, :])
             skip = twice(chan_ref[6, rows, :])
             sig_g = jax.nn.sigmoid(gate)
@@ -442,7 +448,8 @@
     col = lambda n: pl.BlockSpec((n, Q), lambda c, lens: (0, at(c)))
     out_shape = [
         shape((rows, width), BF16),
-        *[shape((inner, rows))] * 5,
+        *[shape((inner, rows))] * 4,
+        shape((inner, rows), BF16),
         *[shape((states2, rows))] * 2,
         *[shape((heads, rows))] * 2,
         shape((seqs * blocks * inner, states2 // 2)),
@@ -511,7 +518,7 @@
         ),
         out_shape=[
             shape((rows, inner), BF16),
-            shape((inner, rows)),
+            shape((inner, rows), BF16),
             *[shape((SEQ_LEN, part), BF16)] * 4,
             shape((1, SEQ_LEN)),
             shape((inner, HALF)),

time: 549 us -> 534 us (0.973)
  Pallas kernels: 156 us -> 144 us
    pallas_call x2, Pallas kernels: 52.9 us -> 42.7 us  [run_forward(): pl.pallas_call(functools.partial(forward_kernel, seq=seq, inner=inner, he...]
  transfers between devices with their start and end apart: 68 -> 68, of which waited for: 23 -> 23; matrix products, arithmetic and copies ran while one was open for 14% -> 15% of each run, Pallas kernels for 26% -> 24%
where the time goes in v5:
time: 534 us; the launch traced here: 528 us
  waiting for transfers between devices  187 us (35%)
  Pallas kernels  144 us (27%)
  starting transfers between devices  99.5 us (19%)
  local copies, waits for them, and re-layouts  35.2 us (7%)
  matrix products  34.3 us (6%)
  other arithmetic  26.3 us (5%)
    ppermute x50, waiting for transfers between devices, exchange(): lax.ppermute(a, axis, [(i, i ^ bit) for i in range(lax.axis_size(axis))])  138 us
    pallas_call x2, Pallas kernels, run_backward(): pl.pallas_call(functools.partial(backward_kernel, seq=seq, inner=inner, i...  65.4 us
    ppermute x18, starting transfers between devices, exchange_z(): return lax.ppermute(a, (DP, TENSOR), pairs)  60.9 us
    ppermute x18, waiting for transfers between devices, exchange_z(): return lax.ppermute(a, (DP, TENSOR), pairs)  49.5 us
    pallas_call x2, Pallas kernels, run_forward(): pl.pallas_call(functools.partial(forward_kernel, seq=seq, inner=inner, he...  42.7 us
    ppermute x50, starting transfers between devices, exchange(): lax.ppermute(a, axis, [(i, i ^ bit) for i in range(lax.axis_size(axis))])  38.6 us
    dot_general x6, matrix products, over_rows(): lax.dot_general(left, right, (((0,), (0,)), ((), ())), preferred_element_...  34.3 us
    pallas_call x2, Pallas kernels, run_middle(): pl.pallas_call(functools.partial(middle_kernel, seq=seq, inner=inner, inn...  24 us
  transfers between devices with their start and end apart: 68, of which 23 were waited for; matrix products, arithmetic and copies ran while one was open for 15% of the time, Pallas kernels for 24%

profile of v5, /device:TPU:0, one launch (start us, length us, event | category | flops | bytes accessed | tf_op | source)
XLA Modules:
  0.0 528.5 jit_solution(11167136459793321195)
XLA Ops:
  3.9 1.4 concatenate.73
  6.1 5.1 collective-permute-start.11
  11.7 1.7 collective-permute-start.17
  21.1 1.8 broadcast_in_dim.37.refs_5_
  24.9 3.9 collective-permute-start.14
  29.5 1.6 collective-permute-start.4
  33.2 1.5 collective-permute-done.4
  34.7 1.5 collective-permute-start.20
  36.3 14.9 %collective-permute-start.6 = (bf16[2,512,128]{2,1,0:T(8,128)(2,1)S(1)}, bf16[2,512,128]{2,1,0:T(8,128)(2,1)S(1)}, u32[]{:S(2)}, u32[]{:S(2)}) collective-permute-start(bf16[2,512,128]{2,1,0:T(8,128)(2,1)S(1)} %get-tuple-element.216), channel_id=1, source_target_pairs={{0,16},{1,25},{2,18},{3,27},{4,20},{5,29},{6,22},{7,31},{8,24},{9,... | collective-permute-start | bytes 786440 | tf_op jit(solution)/shard_map/ppermute | solution.py:716
  51.2 9.9 %collective-permute-done.15 = bf16[2,528,128]{2,1,0:T(8,128)(2,1)S(1)} collective-permute-done((bf16[2,528,128]{2,1,0:T(8,128)(2,1)S(1)}, bf16[2,528,128]{2,1,0:T(8,128)(2,1)S(1)}, u32[]{:S(2)}, u32[]{:S(2)}) %collective-permute-start.15) | collective-permute-done | bytes 270368 | tf_op jit(solution)/shard_map/ppermute | solution.py:716
  61.1 2.4 collective-permute-start.5
  63.7 3.0 collective-permute-done.6
  66.8 9.4 %collective-permute-done.7 = bf16[2,512,128]{2,1,0:T(8,128)(2,1)S(1)} collective-permute-done((bf16[2,512,128]{2,1,0:T(8,128)(2,1)S(1)}, bf16[2,512,128]{2,1,0:T(8,128)(2,1)S(1)}, u32[]{:S(2)}, u32[]{:S(2)}) %collective-permute-start.7) | collective-permute-done | bytes 262176 | tf_op jit(solution)/shard_map/ppermute | solution.py:716
  76.2 1.5 collective-permute-start.1
  77.8 1.5 collective-permute-start.18
  80.4 10.5 %collective-permute-done.18 = bf16[3,768,128]{2,1,0:T(8,128)(2,1)S(1)} collective-permute-done((bf16[3,768,128]{2,1,0:T(8,128)(2,1)S(1)}, bf16[3,768,128]{2,1,0:T(8,128)(2,1)S(1)}, u32[]{:S(2)}, u32[]{:S(2)}) %collective-permute-start.18) | collective-permute-done | bytes 589856 | tf_op jit(solution)/shard_map/ppermute | solution.py:650
  93.8 50.7 %collective-permute-done.9.refs_2_ = bf16[2048,256]{1,0:T(8,128)(2,1)S(1)} collective-permute-done((bf16[2048,256]{1,0:T(8,128)(2,1)S(1)}, bf16[2048,256]{1,0:T(8,128)(2,1)S(1)}, u32[]{:S(2)}, u32[]{:S(2)}) %collective-permute-start.9) | collective-permute-done | bytes 1048608 | tf_op jit(solution)/shard_map/ppermute | solution.py:650
  145.7 1.6 copy-done.19
  147.2 23.8 %mixer_forward.2 = (bf16[4096,1024]{1,0:T(8,128)(2,1)}, f32[512,4096]{1,0:T(8,128)}, f32[512,4096]{1,0:T(8,128)}, f32[512,4096]{1,0:T(8,128)}, f32[512,4096]{1,0...) custom-call(s32[2]{0:T(128)S(1)} %copy-done.18, ...), custom_call_target="tpu_custom_call" | custom-call | tf_op jit(solution)/shard_map/mixer_forward/pallas_call | solution.py:467
  171.2 1.5 collective-permute-start.26
  173.1 18.8 %mixer_forward.3 = (bf16[4096,1024]{1,0:T(8,128)(2,1)}, f32[512,4096]{1,0:T(8,128)}, f32[512,4096]{1,0:T(8,128)}, f32[512,4096]{1,0:T(8,128)}, f32[512,4096]{1,0...) custom-call(s32[2]{0:T(128)S(1)} %copy-done.18, ...), custom_call_target="tpu_custom_call", output_to_operand_aliasing={{0}: (9, {}), {1}: (10, {}), {2}: (11, {}), {3}: (12, {}), ... | custom-call | tf_op jit(solution)/shard_map/mixer_forward/pallas_call | solution.py:467
  192.3 1.5 collective-permute-start.23
  193.9 2.1 collective-permute-done.23
  197.0 12.5 %mixer_middle.2 = (bf16[4096,512]{1,0:T(8,128)(2,1)}, bf16[512,4096]{1,0:T(8,128)(2,1)}, bf16[2048,256]{1,0:T(8,128)(2,1)S(1)}, bf16[2048,256]{1,0:T(8,128)(2,1)...) custom-call(s32[2]{0:T(128)S(1)} %copy-done.18, ...), custom_call_target="tpu_custom_call" | custom-call | tf_op jit(solution)/shard_map/mixer_middle/pallas_call | solution.py:510
  211.4 11.6 %mixer_middle.3 = (bf16[4096,512]{1,0:T(8,128)(2,1)}, bf16[512,4096]{1,0:T(8,128)(2,1)}, bf16[2048,256]{1,0:T(8,128)(2,1)S(1)}, bf16[2048,256]{1,0:T(8,128)(2,1)...) custom-call(s32[2]{0:T(128)S(1)} %copy-done.18, ...), custom_call_target="tpu_custom_call", output_to_operand_aliasing={{0}: (9, {}), {1}: (10, {})} | custom-call | tf_op jit(solution)/shard_map/mixer_middle/pallas_call | solution.py:510
  224.0 3.6 convolution_bitcast_fusion.3
  227.7 2.9 convolution_bitcast_fusion
  230.6 2.9 convolution_bitcast_fusion.1
  233.5 2.9 convolution_bitcast_fusion.2
  238.6 8.9 %collective-permute-start.64 = (bf16[2,128,512]{2,1,0:T(8,128)(2,1)}, bf16[2,128,512]{2,1,0:T(8,128)(2,1)}, u32[]{:S(2)}, u32[]{:S(2)}) collective-permute-start(bf16[2,128,512]{2,1,0:T(8,128)(2,1)} %get-tuple-element.188), channel_id=1, source_target_pairs={{0,24},{1,9},{2,26},{3,11},{4,28},{5,13},{6,30},{7,15},{8,16},{9,1... | collective-permute-start | bytes 786440 | tf_op jit(solution)/shard_map/ppermute | solution.py:716
  247.5 37.1 %mixer_backward.2 = (bf16[4096,768]{1,0:T(8,128)(2,1)}, bf16[4096,640]{1,0:T(8,128)(2,1)}, bf16[2048,256]{1,0:T(8,128)(2,1)}, bf16[2048,256]{1,0:T(8,128)(2,1)},...) custom-call(s32[2]{0:T(128)S(1)} %copy-done.18, ...), custom_call_target="tpu_custom_call" | custom-call | tf_op jit(solution)/shard_map/mixer_backward/pallas_call | solution.py:568
  285.5 28.3 %mixer_backward.3 = (bf16[4096,768]{1,0:T(8,128)(2,1)}, bf16[4096,640]{1,0:T(8,128)(2,1)}, bf16[2048,256]{1,0:T(8,128)(2,1)}, bf16[2048,256]{1,0:T(8,128)(2,1)},...) custom-call(s32[2]{0:T(128)S(1)} %copy-done.18, ...), custom_call_target="tpu_custom_call", output_to_operand_aliasing={{0}: (21, {}), {1}: (22, {})} | custom-call | tf_op jit(solution)/shard_map/mixer_backward/pallas_call | solution.py:568
  313.8 11.8 %fusion.25 = bf16[1024,640]{1,0:T(8,128)(2,1)} fusion(bf16[4096,1024]{1,0:T(8,128)(2,1)} %get-tuple-element.140, bf16[4096,640]{1,0:T(8,128)(2,1)} %get-tuple-element.142), kind=kOutput, calls=%fused_computation.138 | convolution fusion | flops 5368709120 | bytes 14942208 | tf_op jit(solution)/shard_map/dot_general | solution.py:819
  325.6 10.3 %fusion.24 = bf16[1024,768]{1,0:T(8,128)(2,1)} fusion(bf16[4096,1024]{1,0:T(8,128)(2,1)} %get-tuple-element.140, bf16[4096,768]{1,0:T(8,128)(2,1)S(1)} %copy-done.20), kind=kOutput, calls=%fused_computation.137 | convolution fusion | flops 6442450944 | bytes 16252928 | tf_op jit(solution)/shard_map/dot_general | solution.py:819
  335.9 1.5 add_reduce_fusion.1
  337.6 2.4 add_reduce_fusion
  340.1 2.1 dynamic-slice_bitcast_fusion.3
  342.3 1.7 collective-permute-done.46
  344.0 11.9 %collective-permute-start.48 = (f32[5904]{0:T(1024)S(1)}, f32[5904]{0:T(1024)S(1)}, u32[]{:S(2)}, u32[]{:S(2)}) collective-permute-start(f32[5904]{0:T(1024)S(1)} %add.314), channel_id=1, source_target_pairs={{0,16},{4,20},{8,24},{12,28},{16,0},{20,4},{24,8},{28,12},{1,17},{... | collective-permute-start | bytes 70856 | tf_op jit(solution)/shard_map/ppermute | solution.py:650
  355.8 2.1 dynamic-slice_bitcast_fusion
  357.9 3.8 collective-permute-start.57
  364.9 5.8 %collective-permute-done.57 = bf16[2,128,640]{2,1,0:T(8,128)(2,1)} collective-permute-done((bf16[2,128,640]{2,1,0:T(8,128)(2,1)}, bf16[2,128,640]{2,1,0:T(8,128)(2,1)}, u32[]{:S(2)}, u32[]{:S(2)}) %collective-permute-start.57) | collective-permute-done | bytes 327712 | tf_op jit(solution)/shard_map/ppermute | solution.py:716
  370.7 15.5 %collective-permute-start.66 = (bf16[2,128,512]{2,1,0:T(8,128)(2,1)}, bf16[2,128,512]{2,1,0:T(8,128)(2,1)S(1)}, u32[]{:S(2)}, u32[]{:S(2)}) collective-permute-start(bf16[2,128,512]{2,1,0:T(8,128)(2,1)} %get-tuple-element.189), channel_id=1, source_target_pairs={{0,8},{1,17},{2,10},{3,19},{4,12},{5,21},{6,14},{7,23},{8,0},{9,25... | collective-permute-start | bytes 786440 | tf_op jit(solution)/shard_map/ppermute | solution.py:716
  386.2 6.6 %collective-permute-done.58 = bf16[2,128,640]{2,1,0:T(8,128)(2,1)} collective-permute-done((bf16[2,128,640]{2,1,0:T(8,128)(2,1)}, bf16[2,128,640]{2,1,0:T(8,128)(2,1)}, u32[]{:S(2)}, u32[]{:S(2)}) %collective-permute-start.58) | collective-permute-done | bytes 327712 | tf_op jit(solution)/shard_map/ppermute | solution.py:716
  393.3 1.4 fusion.1
  395.1 2.9 collective-permute-done.66
  399.8 18.4 %collective-permute-done.60 = bf16[128,640]{1,0:T(8,128)(2,1)S(1)} collective-permute-done((bf16[128,640]{1,0:T(8,128)(2,1)S(1)}, bf16[128,640]{1,0:T(8,128)(2,1)S(1)}, u32[]{:S(2)}, u32[]{:S(2)}) %collective-permute-start.60) | collective-permute-done | bytes 163872 | tf_op jit(solution)/shard_map/ppermute | solution.py:650
  420.3 1.6 collective-permute-start.51
  424.8 1.7 collective-permute-done.52
  428.4 1.9 collective-permute-done.67
  431.6 2.5 collective-permute-start.54
  436.4 3.2 collective-permute-done.54
  439.6 2.5 collective-permute-start.56
  443.5 8.2 %collective-permute-done.55 = bf16[128,768]{1,0:T(8,128)(2,1)S(1)} collective-permute-done((bf16[128,768]{1,0:T(8,128)(2,1)S(1)}, bf16[128,768]{1,0:T(8,128)(2,1)S(1)}, u32[]{:S(2)}, u32[]{:S(2)}) %collective-permute-start.55) | collective-permute-done | bytes 196640 | tf_op jit(solution)/shard_map/ppermute | solution.py:716
  456.2 2.3 collective-permute-done.33.last_ref
  461.8 1.8 bitcast_add_fusion.2
  464.2 1.6 slice_add_fusion
  471.7 1.9 finish.4.refs_0_
  473.6 7.5 %collective-permute-done.30.last_ref = bf16[2048,256]{1,0:T(8,128)(2,1)} collective-permute-done((bf16[2048,256]{1,0:T(8,128)(2,1)}, bf16[2048,256]{1,0:T(8,128)(2,1)}, u32[]{:S(2)}, u32[]{:S(2)}) %collective-permute-start.30) | collective-permute-done | bytes 1048608 | tf_op jit(solution)/shard_map/ppermute | solution.py:650
  481.1 2.9 finish.5
  484.0 19.5 %collective-permute-done.45.last_ref = bf16[2048,256]{1,0:T(8,128)(2,1)} collective-permute-done((bf16[2048,256]{1,0:T(8,128)(2,1)}, bf16[2048,256]{1,0:T(8,128)(2,1)}, u32[]{:S(2)}, u32[]{:S(2)}) %collective-permute-start.45) | collective-permute-done | bytes 1048608 | tf_op jit(solution)/shard_map/ppermute | solution.py:650
  503.5 3.4 finish.6.refs_0_
  507.0 17.8 %collective-permute-done.42.last_ref = bf16[2048,256]{1,0:T(8,128)(2,1)} collective-permute-done((bf16[2048,256]{1,0:T(8,128)(2,1)}, bf16[2048,256]{1,0:T(8,128)(2,1)}, u32[]{:S(2)}, u32[]{:S(2)}) %collective-permute-start.42) | collective-permute-done | bytes 1048608 | tf_op jit(solution)/shard_map/ppermute | solution.py:650
  524.8 3.4 finish.7
  (280 shorter events, 62.4 us)
Async XLA Ops:
  6.1 22.8 %collective-permute-start.11 = (bf16[768,128]{1,0:T(8,128)(2,1)}, bf16[768,128]{1,0:T(8,128)(2,1)S(1)}, u32[]{:S(2)}, u32[]{:S(2)}) collective-permute-start(bf16[768,128]{1,0:T(8,128)(2,1)} %get-tuple-element.210), channel_id=1, source_target_pairs={{0,24},{1,9},{2,26},{3,11},{4,28},{5,13},{6,30},{7,15},{8,16},{9,1... | collective-permute-start | bytes 589832 | tf_op jit(solution)/shard_map/ppermute | solution.py:716
  11.1 18.1 %collective-permute-start.12 = (bf16[768,128]{1,0:T(8,128)(2,1)}, bf16[768,128]{1,0:T(8,128)(2,1)S(1)}, u32[]{:S(2)}, u32[]{:S(2)}) collective-permute-start(bf16[768,128]{1,0:T(8,128)(2,1)} %get-tuple-element.210), channel_id=1, source_target_pairs={{0,16},{1,25},{2,18},{3,27},{4,20},{5,29},{6,22},{7,31},{8,24},{9,... | collective-permute-start | bytes 589832 | tf_op jit(solution)/shard_map/ppermute | solution.py:716
  11.1 18.3 %collective-permute-start.13 = (bf16[768,128]{1,0:T(8,128)(2,1)}, bf16[768,128]{1,0:T(8,128)(2,1)}, u32[]{:S(2)}, u32[]{:S(2)}) collective-permute-start(bf16[768,128]{1,0:T(8,128)(2,1)} %get-tuple-element.210), channel_id=1, source_target_pairs={{0,8},{1,17},{2,10},{3,19},{4,12},{5,21},{6,14},{7,23},{8,0},{9,25... | collective-permute-start | bytes 589832 | tf_op jit(solution)/shard_map/ppermute | solution.py:716
  11.7 68.1 %collective-permute-start.17 = (bf16[768,128]{1,0:T(8,128)(2,1)}, bf16[768,128]{1,0:T(8,128)(2,1)}, u32[]{:S(2)}, u32[]{:S(2)}) collective-permute-start(bf16[768,128]{1,0:T(8,128)(2,1)} %get-tuple-element.210), channel_id=1, source_target_pairs={{0,4},{4,0},{8,12},{12,8},{16,20},{20,16},{24,28},{28,24},{1,5},{5... | collective-permute-start | bytes 589832 | tf_op jit(solution)/shard_map/ppermute | solution.py:650
  14.1 7.0 %collective-permute-start.3 = (bf16[528,128]{1,0:T(8,128)(2,1)}, bf16[528,128]{1,0:T(8,128)(2,1)}, u32[]{:S(2)}, u32[]{:S(2)}) collective-permute-start(bf16[528,128]{1,0:T(8,128)(2,1)} %get-tuple-element.212), channel_id=1, source_target_pairs={{0,4},{4,0},{8,12},{12,8},{16,20},{20,16},{24,28},{28,24},{1,5},{5... | collective-permute-start | bytes 405512 | tf_op jit(solution)/shard_map/ppermute | solution.py:650
  24.9 11.3 %collective-permute-start.14 = (bf16[2,528,128]{2,1,0:T(8,128)(2,1)S(1)}, bf16[2,528,128]{2,1,0:T(8,128)(2,1)S(1)}, u32[]{:S(2)}, u32[]{:S(2)}) collective-permute-start(bf16[2,528,128]{2,1,0:T(8,128)(2,1)S(1)} %get-tuple-element.214), channel_id=1, source_target_pairs={{0,24},{1,9},{2,26},{3,11},{4,28},{5,13},{6,30},{7,15},{8,16},{9,1... | collective-permute-start | bytes 811016 | tf_op jit(solution)/shard_map/ppermute | solution.py:716
  28.8 32.2 %collective-permute-start.15 = (bf16[2,528,128]{2,1,0:T(8,128)(2,1)S(1)}, bf16[2,528,128]{2,1,0:T(8,128)(2,1)S(1)}, u32[]{:S(2)}, u32[]{:S(2)}) collective-permute-start(bf16[2,528,128]{2,1,0:T(8,128)(2,1)S(1)} %get-tuple-element.214), channel_id=1, source_target_pairs={{0,16},{1,25},{2,18},{3,27},{4,20},{5,29},{6,22},{7,31},{8,24},{9,... | collective-permute-start | bytes 811016 | tf_op jit(solution)/shard_map/ppermute | solution.py:716
  29.3 31.8 %collective-permute-start.16 = (bf16[2,528,128]{2,1,0:T(8,128)(2,1)S(1)}, bf16[2,528,128]{2,1,0:T(8,128)(2,1)S(1)}, u32[]{:S(2)}, u32[]{:S(2)}) collective-permute-start(bf16[2,528,128]{2,1,0:T(8,128)(2,1)S(1)} %get-tuple-element.214), channel_id=1, source_target_pairs={{0,8},{1,17},{2,10},{3,19},{4,12},{5,21},{6,14},{7,23},{8,0},{9,25... | collective-permute-start | bytes 811016 | tf_op jit(solution)/shard_map/ppermute | solution.py:716
  29.5 5.2 collective-permute-start.4
  34.7 58.3 %collective-permute-start.20 = (bf16[2048,256]{1,0:T(8,128)(2,1)S(1)}, bf16[2048,256]{1,0:T(8,128)(2,1)S(1)}, u32[]{:S(2)}, u32[]{:S(2)}) collective-permute-start(bf16[2048,256]{1,0:T(8,128)(2,1)S(1)} %copy-done.5), channel_id=1, source_target_pairs={{0,2},{1,3},{2,0},{3,1},{4,6},{5,7},{6,4},{7,5},{8,10},{9,11},{10,... | collective-permute-start | bytes 3145736 | tf_op jit(solution)/shard_map/ppermute | solution.py:650
  36.3 30.5 %collective-permute-start.6 = (bf16[2,512,128]{2,1,0:T(8,128)(2,1)S(1)}, bf16[2,512,128]{2,1,0:T(8,128)(2,1)S(1)}, u32[]{:S(2)}, u32[]{:S(2)}) collective-permute-start(bf16[2,512,128]{2,1,0:T(8,128)(2,1)S(1)} %get-tuple-element.216), channel_id=1, source_target_pairs={{0,16},{1,25},{2,18},{3,27},{4,20},{5,29},{6,22},{7,31},{8,24},{9,... | collective-permute-start | bytes 786440 | tf_op jit(solution)/shard_map/ppermute | solution.py:716
  61.1 15.2 %collective-permute-start.7 = (bf16[2,512,128]{2,1,0:T(8,128)(2,1)S(1)}, bf16[2,512,128]{2,1,0:T(8,128)(2,1)S(1)}, u32[]{:S(2)}, u32[]{:S(2)}) collective-permute-start(bf16[2,512,128]{2,1,0:T(8,128)(2,1)S(1)} %get-tuple-element.216), channel_id=1, source_target_pairs={{0,8},{1,17},{2,10},{3,19},{4,12},{5,21},{6,14},{7,23},{8,0},{9,25... | collective-permute-start | bytes 786440 | tf_op jit(solution)/shard_map/ppermute | solution.py:716
  61.1 16.7 %collective-permute-start.5 = (bf16[2,512,128]{2,1,0:T(8,128)(2,1)S(1)}, bf16[2,512,128]{2,1,0:T(8,128)(2,1)S(1)}, u32[]{:S(2)}, u32[]{:S(2)}) collective-permute-start(bf16[2,512,128]{2,1,0:T(8,128)(2,1)S(1)} %get-tuple-element.216), channel_id=1, source_target_pairs={{0,24},{1,9},{2,26},{3,11},{4,28},{5,13},{6,30},{7,15},{8,16},{9,1... | collective-permute-start | bytes 786440 | tf_op jit(solution)/shard_map/ppermute | solution.py:716
  66.8 26.9 %collective-permute-start.19 = (bf16[2048,256]{1,0:T(8,128)(2,1)S(1)}, bf16[2048,256]{1,0:T(8,128)(2,1)S(1)}, u32[]{:S(2)}, u32[]{:S(2)}) collective-permute-start(bf16[2048,256]{1,0:T(8,128)(2,1)S(1)} %copy-done.5), channel_id=1, source_target_pairs={{0,1},{1,0},{2,3},{3,2},{4,5},{5,4},{6,7},{7,6},{8,9},{9,8},{10,11... | collective-permute-start | bytes 3145736 | tf_op jit(solution)/shard_map/ppermute | solution.py:650
  76.2 68.2 %collective-permute-start.1 = (bf16[4096,256]{1,0:T(8,128)(2,1)S(1)}, bf16[4096,256]{1,0:T(8,128)(2,1)}, u32[]{:S(2)}, u32[]{:S(2)}) collective-permute-start(bf16[4096,256]{1,0:T(8,128)(2,1)S(1)} %copy-done), channel_id=1, source_target_pairs={{0,2},{1,3},{2,0},{3,1},{4,6},{5,7},{6,4},{7,5},{8,10},{9,11},{10,... | collective-permute-start | bytes 6291464 | tf_op jit(solution)/shard_map/ppermute | solution.py:650
  77.8 13.2 %collective-permute-start.18 = (bf16[3,768,128]{2,1,0:T(8,128)(2,1)S(1)}, bf16[3,768,128]{2,1,0:T(8,128)(2,1)S(1)}, u32[]{:S(2)}, u32[]{:S(2)}) collective-permute-start(bf16[3,768,128]{2,1,0:T(8,128)(2,1)S(1)} %pad_maximum_fusion.4), channel_id=1, source_target_pairs={{0,4},{4,0},{8,12},{12,8},{16,20},{20,16},{24,28},{28,24},{1,5},{5... | collective-permute-start | bytes 1769480 | tf_op jit(solution)/shard_map/ppermute | solution.py:650
  79.8 64.6 %collective-permute-start.9 = (bf16[2048,256]{1,0:T(8,128)(2,1)S(1)}, bf16[2048,256]{1,0:T(8,128)(2,1)S(1)}, u32[]{:S(2)}, u32[]{:S(2)}) collective-permute-start(bf16[2048,256]{1,0:T(8,128)(2,1)S(1)} %get-tuple-element.173.refs_0_), channel_id=1, source_target_pairs={{0,2},{1,3},{2,0},{3,1},{4,6},{5,7},{6,4},{7,5},{8,10},{9,11},{10,... | collective-permute-start | bytes 3145736 | tf_op jit(solution)/shard_map/ppermute | solution.py:650
  90.9 80.3 %collective-permute-start.8 = (bf16[2048,256]{1,0:T(8,128)(2,1)S(1)}, bf16[2048,256]{1,0:T(8,128)(2,1)}, u32[]{:S(2)}, u32[]{:S(2)}) collective-permute-start(bf16[2048,256]{1,0:T(8,128)(2,1)S(1)} %get-tuple-element.173.refs_0_), channel_id=1, source_target_pairs={{0,1},{1,0},{2,3},{3,2},{4,5},{5,4},{6,7},{7,6},{8,9},{9,8},{10,11... | collective-permute-start | bytes 3145736 | tf_op jit(solution)/shard_map/ppermute | solution.py:650
  93.1 103.9 %collective-permute-start = (bf16[4096,256]{1,0:T(8,128)(2,1)S(1)}, bf16[4096,256]{1,0:T(8,128)(2,1)}, u32[]{:S(2)}, u32[]{:S(2)}) collective-permute-start(bf16[4096,256]{1,0:T(8,128)(2,1)S(1)} %copy-done), channel_id=1, source_target_pairs={{0,1},{1,0},{2,3},{3,2},{4,5},{5,4},{6,7},{7,6},{8,9},{9,8},{10,11... | collective-permute-start | bytes 6291464 | tf_op jit(solution)/shard_map/ppermute | solution.py:650
  93.7 52.0 %collective-permute-start.21 = (bf16[2048,256]{1,0:T(8,128)(2,1)S(1)}, bf16[2048,256]{1,0:T(8,128)(2,1)}, u32[]{:S(2)}, u32[]{:S(2)}) collective-permute-start(bf16[2048,256]{1,0:T(8,128)(2,1)S(1)} %collective-permute-done.20.refs_2_), channel_id=1, source_target_pairs={{0,1},{1,0},{2,3},{3,2},{4,5},{5,4},{6,7},{7,6},{8,9},{9,8},{10,11... | collective-permute-start | bytes 3145736 | tf_op jit(solution)/shard_map/ppermute | solution.py:650
  144.5 28.3 %collective-permute-start.10 = (bf16[2048,256]{1,0:T(8,128)(2,1)S(1)}, bf16[2048,256]{1,0:T(8,128)(2,1)}, u32[]{:S(2)}, u32[]{:S(2)}) collective-permute-start(bf16[2048,256]{1,0:T(8,128)(2,1)S(1)} %collective-permute-done.9.refs_2_), channel_id=1, source_target_pairs={{0,1},{1,0},{2,3},{3,2},{4,5},{5,4},{6,7},{7,6},{8,9},{9,8},{10,11... | collective-permute-start | bytes 3145736 | tf_op jit(solution)/shard_map/ppermute | solution.py:650
  144.5 52.5 %collective-permute-start.2 = (bf16[4096,256]{1,0:T(8,128)(2,1)}, bf16[4096,256]{1,0:T(8,128)(2,1)}, u32[]{:S(2)}, u32[]{:S(2)}) collective-permute-start(bf16[4096,256]{1,0:T(8,128)(2,1)} %collective-permute-done.1.refs_2_), channel_id=1, source_target_pairs={{0,1},{1,0},{2,3},{3,2},{4,5},{5,4},{6,7},{7,6},{8,9},{9,8},{10,11... | collective-permute-start | bytes 6291464 | tf_op jit(solution)/shard_map/ppermute | solution.py:650
  171.1 20.8 %collective-permute-start.25 = (f32[1,2048]{1,0:T(1,128)S(1)}, f32[1,2048]{1,0:T(1,128)S(1)}, u32[]{:S(2)}, u32[]{:S(2)}) collective-permute-start(f32[1,2048]{1,0:T(1,128)S(1)} %get-tuple-element.97), channel_id=1, source_target_pairs={{0,1},{1,0},{2,3},{3,2},{4,5},{5,4},{6,7},{7,6},{8,9},{9,8},{10,11... | collective-permute-start | bytes 24584 | tf_op jit(solution)/shard_map/ppermute | solution.py:650
  171.2 21.1 %collective-permute-start.26 = (f32[1,2048]{1,0:T(1,128)S(1)}, f32[1,2048]{1,0:T(1,128)S(1)}, u32[]{:S(2)}, u32[]{:S(2)}) collective-permute-start(f32[1,2048]{1,0:T(1,128)S(1)} %get-tuple-element.97), channel_id=1, source_target_pairs={{0,2},{1,3},{2,0},{3,1},{4,6},{5,7},{6,4},{7,5},{8,10},{9,11},{10,... | collective-permute-start | bytes 24584 | tf_op jit(solution)/shard_map/ppermute | solution.py:650
  172.7 21.1 %collective-permute-start.27 = (f32[1,2048]{1,0:T(1,128)S(1)}, f32[1,2048]{1,0:T(1,128)S(1)}, u32[]{:S(2)}, u32[]{:S(2)}) collective-permute-start(f32[1,2048]{1,0:T(1,128)S(1)} %get-tuple-element.97), channel_id=1, source_target_pairs={{0,3},{1,2},{2,1},{3,0},{4,7},{5,6},{6,5},{7,4},{8,11},{9,10},{10,... | collective-permute-start | bytes 24584 | tf_op jit(solution)/shard_map/ppermute | solution.py:650
  192.3 3.7 collective-permute-start.23
  209.5 28.1 %collective-permute-start.37 = (f32[1,2048]{1,0:T(1,128)S(1)}, f32[1,2048]{1,0:T(1,128)S(1)}, u32[]{:S(2)}, u32[]{:S(2)}) collective-permute-start(f32[1,2048]{1,0:T(1,128)S(1)} %get-tuple-element.119), channel_id=1, source_target_pairs={{0,1},{1,0},{2,3},{3,2},{4,5},{5,4},{6,7},{7,6},{8,9},{9,8},{10,11... | collective-permute-start | bytes 24584 | tf_op jit(solution)/shard_map/ppermute | solution.py:650
  209.7 28.9 %collective-permute-start.38 = (f32[1,2048]{1,0:T(1,128)S(1)}, f32[1,2048]{1,0:T(1,128)S(1)}, u32[]{:S(2)}, u32[]{:S(2)}) collective-permute-start(f32[1,2048]{1,0:T(1,128)S(1)} %get-tuple-element.119), channel_id=1, source_target_pairs={{0,2},{1,3},{2,0},{3,1},{4,6},{5,7},{6,4},{7,5},{8,10},{9,11},{10,... | collective-permute-start | bytes 24584 | tf_op jit(solution)/shard_map/ppermute | solution.py:650
  210.2 37.2 %collective-permute-start.39 = (f32[1,2048]{1,0:T(1,128)S(1)}, f32[1,2048]{1,0:T(1,128)S(1)}, u32[]{:S(2)}, u32[]{:S(2)}) collective-permute-start(f32[1,2048]{1,0:T(1,128)S(1)} %get-tuple-element.119), channel_id=1, source_target_pairs={{0,3},{1,2},{2,1},{3,0},{4,7},{5,6},{6,5},{7,4},{8,11},{9,10},{10,... | collective-permute-start | bytes 24584 | tf_op jit(solution)/shard_map/ppermute | solution.py:650
  223.0 24.5 %collective-permute-start.34 = (f32[1,2048]{1,0:T(1,128)S(1)}, f32[1,2048]{1,0:T(1,128)S(1)}, u32[]{:S(2)}, u32[]{:S(2)}) collective-permute-start(f32[1,2048]{1,0:T(1,128)S(1)} %get-tuple-element.118), channel_id=1, source_target_pairs={{0,1},{1,0},{2,3},{3,2},{4,5},{5,4},{6,7},{7,6},{8,9},{9,8},{10,11... | collective-permute-start | bytes 24584 | tf_op jit(solution)/shard_map/ppermute | solution.py:650
  223.5 24.0 %collective-permute-start.35 = (f32[1,2048]{1,0:T(1,128)S(1)}, f32[1,2048]{1,0:T(1,128)S(1)}, u32[]{:S(2)}, u32[]{:S(2)}) collective-permute-start(f32[1,2048]{1,0:T(1,128)S(1)} %get-tuple-element.118), channel_id=1, source_target_pairs={{0,2},{1,3},{2,0},{3,1},{4,6},{5,7},{6,4},{7,5},{8,10},{9,11},{10,... | collective-permute-start | bytes 24584 | tf_op jit(solution)/shard_map/ppermute | solution.py:650
  237.6 9.9 %collective-permute-start.36 = (f32[1,2048]{1,0:T(1,128)S(1)}, f32[1,2048]{1,0:T(1,128)S(1)}, u32[]{:S(2)}, u32[]{:S(2)}) collective-permute-start(f32[1,2048]{1,0:T(1,128)S(1)} %get-tuple-element.118), channel_id=1, source_target_pairs={{0,3},{1,2},{2,1},{3,0},{4,7},{5,6},{6,5},{7,4},{8,11},{9,10},{10,... | collective-permute-start | bytes 24584 | tf_op jit(solution)/shard_map/ppermute | solution.py:650
  238.6 156.2 %collective-permute-start.64 = (bf16[2,128,512]{2,1,0:T(8,128)(2,1)}, bf16[2,128,512]{2,1,0:T(8,128)(2,1)}, u32[]{:S(2)}, u32[]{:S(2)}) collective-permute-start(bf16[2,128,512]{2,1,0:T(8,128)(2,1)} %get-tuple-element.188), channel_id=1, source_target_pairs={{0,24},{1,9},{2,26},{3,11},{4,28},{5,13},{6,30},{7,15},{8,16},{9,1... | collective-permute-start | bytes 786440 | tf_op jit(solution)/shard_map/ppermute | solution.py:716
  247.5 147.4 %collective-permute-start.65 = (bf16[2,128,512]{2,1,0:T(8,128)(2,1)}, bf16[2,128,512]{2,1,0:T(8,128)(2,1)}, u32[]{:S(2)}, u32[]{:S(2)}) collective-permute-start(bf16[2,128,512]{2,1,0:T(8,128)(2,1)} %get-tuple-element.190), channel_id=1, source_target_pairs={{0,16},{1,25},{2,18},{3,27},{4,20},{5,29},{6,22},{7,31},{8,24},{9,... | collective-permute-start | bytes 786440 | tf_op jit(solution)/shard_map/ppermute | solution.py:716
  340.1 3.9 collective-permute-start.46
  344.0 13.9 %collective-permute-start.47 = (f32[5904]{0:T(1024)S(1)}, f32[5904]{0:T(1024)S(1)}, u32[]{:S(2)}, u32[]{:S(2)}) collective-permute-start(f32[5904]{0:T(1024)S(1)} %add.314), channel_id=1, source_target_pairs={{0,8},{4,12},{8,0},{12,4},{16,24},{20,28},{24,16},{28,20},{1,9},{5... | collective-permute-start | bytes 70856 | tf_op jit(solution)/shard_map/ppermute | solution.py:650
  344.0 17.8 %collective-permute-start.48 = (f32[5904]{0:T(1024)S(1)}, f32[5904]{0:T(1024)S(1)}, u32[]{:S(2)}, u32[]{:S(2)}) collective-permute-start(f32[5904]{0:T(1024)S(1)} %add.314), channel_id=1, source_target_pairs={{0,16},{4,20},{8,24},{12,28},{16,0},{20,4},{24,8},{28,12},{1,17},{... | collective-permute-start | bytes 70856 | tf_op jit(solution)/shard_map/ppermute | solution.py:650
  355.8 5.9 %collective-permute-start.49 = (f32[5904]{0:T(1024)S(1)}, f32[5904]{0:T(1024)S(1)}, u32[]{:S(2)}, u32[]{:S(2)}) collective-permute-start(f32[5904]{0:T(1024)S(1)} %add.314), channel_id=1, source_target_pairs={{0,24},{4,28},{8,16},{12,20},{16,8},{20,12},{24,0},{28,4},{1,25},{... | collective-permute-start | bytes 70856 | tf_op jit(solution)/shard_map/ppermute | solution.py:650
  357.9 12.8 %collective-permute-start.57 = (bf16[2,128,640]{2,1,0:T(8,128)(2,1)}, bf16[2,128,640]{2,1,0:T(8,128)(2,1)}, u32[]{:S(2)}, u32[]{:S(2)}) collective-permute-start(bf16[2,128,640]{2,1,0:T(8,128)(2,1)} %get-tuple-element.177), channel_id=1, source_target_pairs={{0,24},{1,9},{2,26},{3,11},{4,28},{5,13},{6,30},{7,15},{8,16},{9,1... | collective-permute-start | bytes 983048 | tf_op jit(solution)/shard_map/ppermute | solution.py:716
  361.7 31.1 %collective-permute-start.58 = (bf16[2,128,640]{2,1,0:T(8,128)(2,1)}, bf16[2,128,640]{2,1,0:T(8,128)(2,1)}, u32[]{:S(2)}, u32[]{:S(2)}) collective-permute-start(bf16[2,128,640]{2,1,0:T(8,128)(2,1)} %get-tuple-element.179), channel_id=1, source_target_pairs={{0,16},{1,25},{2,18},{3,27},{4,20},{5,29},{6,22},{7,31},{8,24},{9,... | collective-permute-start | bytes 983048 | tf_op jit(solution)/shard_map/ppermute | solution.py:716
  361.7 31.1 %collective-permute-start.59 = (bf16[2,128,640]{2,1,0:T(8,128)(2,1)S(1)}, bf16[2,128,640]{2,1,0:T(8,128)(2,1)}, u32[]{:S(2)}, u32[]{:S(2)}) collective-permute-start(bf16[2,128,640]{2,1,0:T(8,128)(2,1)S(1)} %get-tuple-element.178), channel_id=1, source_target_pairs={{0,8},{1,17},{2,10},{3,19},{4,12},{5,21},{6,14},{7,23},{8,0},{9,25... | collective-permute-start | bytes 983048 | tf_op jit(solution)/shard_map/ppermute | solution.py:716
  370.7 27.3 %collective-permute-start.66 = (bf16[2,128,512]{2,1,0:T(8,128)(2,1)}, bf16[2,128,512]{2,1,0:T(8,128)(2,1)S(1)}, u32[]{:S(2)}, u32[]{:S(2)}) collective-permute-start(bf16[2,128,512]{2,1,0:T(8,128)(2,1)} %get-tuple-element.189), channel_id=1, source_target_pairs={{0,8},{1,17},{2,10},{3,19},{4,12},{5,21},{6,14},{7,23},{8,0},{9,25... | collective-permute-start | bytes 786440 | tf_op jit(solution)/shard_map/ppermute | solution.py:716
  392.8 30.5 %collective-permute-start.32 = (bf16[2048,256]{1,0:T(8,128)(2,1)}, bf16[2048,256]{1,0:T(8,128)(2,1)S(1)}, u32[]{:S(2)}, u32[]{:S(2)}) collective-permute-start(bf16[2048,256]{1,0:T(8,128)(2,1)} %get-tuple-element.107), channel_id=1, source_target_pairs={{0,1},{1,0},{2,3},{3,2},{4,5},{5,4},{6,7},{7,6},{8,9},{9,8},{10,11... | collective-permute-start | bytes 3145736 | tf_op jit(solution)/shard_map/ppermute | solution.py:650
  392.8 33.8 %collective-permute-start.29 = (bf16[2048,256]{1,0:T(8,128)(2,1)}, bf16[2048,256]{1,0:T(8,128)(2,1)S(1)}, u32[]{:S(2)}, u32[]{:S(2)}) collective-permute-start(bf16[2048,256]{1,0:T(8,128)(2,1)} %get-tuple-element.103), channel_id=1, source_target_pairs={{0,1},{1,0},{2,3},{3,2},{4,5},{5,4},{6,7},{7,6},{8,9},{9,8},{10,11... | collective-permute-start | bytes 3145736 | tf_op jit(solution)/shard_map/ppermute | solution.py:650
  394.8 25.5 %collective-permute-start.53 = (bf16[4,128,768]{2,1,0:T(8,128)(2,1)}, bf16[4,128,768]{2,1,0:T(8,128)(2,1)S(1)}, u32[]{:S(2)}, u32[]{:S(2)}) collective-permute-start(bf16[4,128,768]{2,1,0:T(8,128)(2,1)} %dynamic-slice_bitcast_fusion), channel_id=1, source_target_pairs={{0,4},{4,0},{8,12},{12,8},{16,20},{20,16},{24,28},{28,24},{1,5},{5... | collective-permute-start | bytes 2359304 | tf_op jit(solution)/shard_map/ppermute | solution.py:650
  394.9 39.2 %collective-permute-start.44 = (bf16[2048,256]{1,0:T(8,128)(2,1)}, bf16[2048,256]{1,0:T(8,128)(2,1)S(1)}, u32[]{:S(2)}, u32[]{:S(2)}) collective-permute-start(bf16[2048,256]{1,0:T(8,128)(2,1)} %get-tuple-element.129), channel_id=1, source_target_pairs={{0,1},{1,0},{2,3},{3,2},{4,5},{5,4},{6,7},{7,6},{8,9},{9,8},{10,11... | collective-permute-start | bytes 3145736 | tf_op jit(solution)/shard_map/ppermute | solution.py:650
  398.0 20.2 %collective-permute-start.60 = (bf16[128,640]{1,0:T(8,128)(2,1)S(1)}, bf16[128,640]{1,0:T(8,128)(2,1)S(1)}, u32[]{:S(2)}, u32[]{:S(2)}) collective-permute-start(bf16[128,640]{1,0:T(8,128)(2,1)S(1)} %fusion.17), channel_id=1, source_target_pairs={{0,4},{4,0},{8,12},{12,8},{16,20},{20,16},{24,28},{28,24},{1,5},{5... | collective-permute-start | bytes 491528 | tf_op jit(solution)/shard_map/ppermute | solution.py:650
  420.1 3.7 collective-permute-start.50
  420.3 4.2 collective-permute-start.51
  424.4 15.2 %collective-permute-start.41 = (bf16[2048,256]{1,0:T(8,128)(2,1)S(1)}, bf16[2048,256]{1,0:T(8,128)(2,1)S(1)}, u32[]{:S(2)}, u32[]{:S(2)}) collective-permute-start(bf16[2048,256]{1,0:T(8,128)(2,1)S(1)} %copy-done.47), channel_id=1, source_target_pairs={{0,1},{1,0},{2,3},{3,2},{4,5},{5,4},{6,7},{7,6},{8,9},{9,8},{10,11... | collective-permute-start | bytes 3145736 | tf_op jit(solution)/shard_map/ppermute | solution.py:650
  424.5 5.8 %collective-permute-start.67 = (bf16[128,512]{1,0:T(8,128)(2,1)S(1)}, bf16[128,512]{1,0:T(8,128)(2,1)S(1)}, u32[]{:S(2)}, u32[]{:S(2)}) collective-permute-start(bf16[128,512]{1,0:T(8,128)(2,1)S(1)} %fusion.18), channel_id=1, source_target_pairs={{0,4},{4,0},{8,12},{12,8},{16,20},{20,16},{24,28},{28,24},{1,5},{5... | collective-permute-start | bytes 393224 | tf_op jit(solution)/shard_map/ppermute | solution.py:650
  426.5 3.9 collective-permute-start.61
  426.6 5.1 collective-permute-start.63
  430.3 21.9 %collective-permute-start.31 = (bf16[2048,256]{1,0:T(8,128)(2,1)S(1)}, bf16[2048,256]{1,0:T(8,128)(2,1)S(1)}, u32[]{:S(2)}, u32[]{:S(2)}) collective-permute-start(bf16[2048,256]{1,0:T(8,128)(2,1)S(1)} %copy-done.45), channel_id=1, source_target_pairs={{0,1},{1,0},{2,3},{3,2},{4,5},{5,4},{6,7},{7,6},{8,9},{9,8},{10,11... | collective-permute-start | bytes 3145736 | tf_op jit(solution)/shard_map/ppermute | solution.py:650
  431.6 22.6 %collective-permute-start.28 = (bf16[2048,256]{1,0:T(8,128)(2,1)S(1)}, bf16[2048,256]{1,0:T(8,128)(2,1)S(1)}, u32[]{:S(2)}, u32[]{:S(2)}) collective-permute-start(bf16[2048,256]{1,0:T(8,128)(2,1)S(1)} %copy-done.46), channel_id=1, source_target_pairs={{0,1},{1,0},{2,3},{3,2},{4,5},{5,4},{6,7},{7,6},{8,9},{9,8},{10,11... | collective-permute-start | bytes 3145736 | tf_op jit(solution)/shard_map/ppermute | solution.py:650
  431.6 8.0 %collective-permute-start.54 = (bf16[128,768]{1,0:T(8,128)(2,1)S(1)}, bf16[128,768]{1,0:T(8,128)(2,1)S(1)}, u32[]{:S(2)}, u32[]{:S(2)}) collective-permute-start(bf16[128,768]{1,0:T(8,128)(2,1)S(1)} %get-tuple-element.174), channel_id=1, source_target_pairs={{0,24},{1,9},{2,26},{3,11},{4,28},{5,13},{6,30},{7,15},{8,16},{9,1... | collective-permute-start | bytes 589832 | tf_op jit(solution)/shard_map/ppermute | solution.py:716
  434.1 24.4 %collective-permute-start.33 = (bf16[2048,256]{1,0:T(8,128)(2,1)S(1)}, bf16[2048,256]{1,0:T(8,128)(2,1)S(1)}, u32[]{:S(2)}, u32[]{:S(2)}) collective-permute-start(bf16[2048,256]{1,0:T(8,128)(2,1)S(1)} %add_convert_fusion.2), channel_id=1, source_target_pairs={{0,2},{1,3},{2,0},{3,1},{4,6},{5,7},{6,4},{7,5},{8,10},{9,11},{10,... | collective-permute-start | bytes 3145736 | tf_op jit(solution)/shard_map/ppermute | solution.py:650
  439.6 12.1 %collective-permute-start.55 = (bf16[128,768]{1,0:T(8,128)(2,1)S(1)}, bf16[128,768]{1,0:T(8,128)(2,1)S(1)}, u32[]{:S(2)}, u32[]{:S(2)}) collective-permute-start(bf16[128,768]{1,0:T(8,128)(2,1)S(1)} %get-tuple-element.176), channel_id=1, source_target_pairs={{0,16},{1,25},{2,18},{3,27},{4,20},{5,29},{6,22},{7,31},{8,24},{9,... | collective-permute-start | bytes 589832 | tf_op jit(solution)/shard_map/ppermute | solution.py:716
  439.6 12.1 %collective-permute-start.56 = (bf16[128,768]{1,0:T(8,128)(2,1)S(1)}, bf16[128,768]{1,0:T(8,128)(2,1)S(1)}, u32[]{:S(2)}, u32[]{:S(2)}) collective-permute-start(bf16[128,768]{1,0:T(8,128)(2,1)S(1)} %get-tuple-element.175), channel_id=1, source_target_pairs={{0,8},{1,17},{2,10},{3,19},{4,12},{5,21},{6,14},{7,23},{8,0},{9,25... | collective-permute-start | bytes 589832 | tf_op jit(solution)/shard_map/ppermute | solution.py:716
  451.7 32.3 %collective-permute-start.43 = (bf16[2048,256]{1,0:T(8,128)(2,1)}, bf16[2048,256]{1,0:T(8,128)(2,1)}, u32[]{:S(2)}, u32[]{:S(2)}) collective-permute-start(bf16[2048,256]{1,0:T(8,128)(2,1)} %get-tuple-element.127), channel_id=1, source_target_pairs={{0,1},{1,0},{2,3},{3,2},{4,5},{5,4},{6,7},{7,6},{8,9},{9,8},{10,11... | collective-permute-start | bytes 3145736 | tf_op jit(solution)/shard_map/ppermute | solution.py:650
  451.7 55.2 %collective-permute-start.40 = (bf16[2048,256]{1,0:T(8,128)(2,1)}, bf16[2048,256]{1,0:T(8,128)(2,1)}, u32[]{:S(2)}, u32[]{:S(2)}) collective-permute-start(bf16[2048,256]{1,0:T(8,128)(2,1)} %get-tuple-element.123), channel_id=1, source_target_pairs={{0,1},{1,0},{2,3},{3,2},{4,5},{5,4},{6,7},{7,6},{8,9},{9,8},{10,11... | collective-permute-start | bytes 3145736 | tf_op jit(solution)/shard_map/ppermute | solution.py:650
  453.2 27.9 %collective-permute-start.30 = (bf16[2048,256]{1,0:T(8,128)(2,1)}, bf16[2048,256]{1,0:T(8,128)(2,1)}, u32[]{:S(2)}, u32[]{:S(2)}) collective-permute-start(bf16[2048,256]{1,0:T(8,128)(2,1)} %add_convert_fusion.3), channel_id=1, source_target_pairs={{0,2},{1,3},{2,0},{3,1},{4,6},{5,7},{6,4},{7,5},{8,10},{9,11},{10,... | collective-permute-start | bytes 3145736 | tf_op jit(solution)/shard_map/ppermute | solution.py:650
  455.2 48.3 %collective-permute-start.45 = (bf16[2048,256]{1,0:T(8,128)(2,1)}, bf16[2048,256]{1,0:T(8,128)(2,1)}, u32[]{:S(2)}, u32[]{:S(2)}) collective-permute-start(bf16[2048,256]{1,0:T(8,128)(2,1)} %add_convert_fusion), channel_id=1, source_target_pairs={{0,2},{1,3},{2,0},{3,1},{4,6},{5,7},{6,4},{7,5},{8,10},{9,11},{10,... | collective-permute-start | bytes 3145736 | tf_op jit(solution)/shard_map/ppermute | solution.py:650
  459.5 65.3 %collective-permute-start.42 = (bf16[2048,256]{1,0:T(8,128)(2,1)}, bf16[2048,256]{1,0:T(8,128)(2,1)}, u32[]{:S(2)}, u32[]{:S(2)}) collective-permute-start(bf16[2048,256]{1,0:T(8,128)(2,1)} %add_convert_fusion.1), channel_id=1, source_target_pairs={{0,2},{1,3},{2,0},{3,1},{4,6},{5,7},{6,4},{7,5},{8,10},{9,11},{10,... | collective-permute-start | bytes 3145736 | tf_op jit(solution)/shard_map/ppermute | solution.py:650
  (52 other events, 822.1 us)
